TPU v7x, 32 devices: a whole 2x2x4 slice. The times are simulated.
32 devices in a mesh: iblk: 4 (over x, core), jblk: 8 (over z, y).
Axes of the slice: x: 2, y: 2, z: 4, core: 2. Of those that a mesh axis runs over, the one named last changes fastest.
Arguments:
- pno_basis: bfloat16 [4, 8, 4, 512, 128], P('iblk', 'jblk'), may hold values from -0.5 to 0.5
- amplitudes: bfloat16 [4, 8, 4, 128, 128], P('iblk', 'jblk'), may hold values from -6 to 6
- pno_energy: float32 [4, 8, 4, 128], P('iblk', 'jblk'), may hold values from 0.5 to 2
- fock_values: float32 [256], replicated, may hold values from -0.4 to 0.4
- couplings: int32 [4, 8, 4, 3, 12], P('iblk', 'jblk'), may hold values from 0 to 255, as said below
- counts: int32 [4, 8, 4], P('iblk', 'jblk'), may hold values from 3 to 12, as said below
Outputs:
- residual: float32 [4, 8, 4, 128, 128], P('iblk', 'jblk')
Inputs may be any that keep to these rules, and one draw needn't show every extreme that they name: `couplings`: rows 0 and 1 hold pair numbers below 4, row 2 holds Fock table entries below 256; within one block of pairs and block step, each combination of local pair and visiting pair stands in at most one slot, live or not; slots at or after the live count are unused. `counts`: some block of pairs fills all 12 slots in some block step in every draw.
All inputs are finite; a program needn't handle non-finite values.
Results may differ from a plain program's by a relative error of at most 0.003.
Values may be sent and summed in bfloat16 or wider, within the bound.
No kernel may reach another device: no remote copies, remote signals or barrier semaphores. Data moves between devices by JAX's collectives and lax.ppermute only.
A program may use at most 64 MiB of HBM per device.

v0:
```python
import jax
import jax.numpy as jnp
from jax import lax
from jax.sharding import PartitionSpec as P

REACH = 2


def passed_along(block, axis, distance):
    devices = range(lax.axis_size(axis))
    route = [((i - distance) % len(devices), i) for i in devices]
    return lax.ppermute(block, axis, route)


def lookup_weights(fock_index, live_count, fock_values):
    table_ids = lax.iota(jnp.int32, fock_values.shape[0])
    slot_ids = lax.iota(jnp.int32, fock_index.shape[0])
    picked = jnp.sum(
        jnp.where(
            fock_index[:, None] == table_ids[None, :], fock_values[None, :], jnp.float32(0.0)
        ),
        axis=1,
    )
    return jnp.where(slot_ids < live_count, picked, jnp.float32(0.0))


def coupling_terms(
    couple_plan, live_count, own_basis, own_amps, visit_basis, visit_amps, fock_values
):
    highest = lax.Precision.HIGHEST
    local_index = couple_plan[0]
    visit_index = couple_plan[1]
    weight = lookup_weights(couple_plan[2], live_count, fock_values)
    every_intersection = jnp.einsum(
        "amp,bmq->abpq", own_basis, visit_basis, preferred_element_type=jnp.float32
    )
    intersection = every_intersection[local_index, visit_index]
    intersection = intersection.astype(jnp.bfloat16)
    left_half = jnp.einsum(
        "cpq,cqr->cpr", intersection, visit_amps[visit_index], preferred_element_type=jnp.float32
    ).astype(jnp.bfloat16)
    local_terms = jnp.einsum(
        "cpr,csr->cps", left_half, intersection, preferred_element_type=jnp.float32
    )
    right_half = jnp.einsum(
        "cpq,cpr->cqr", intersection, own_amps[local_index], preferred_element_type=jnp.float32
    ).astype(jnp.bfloat16)
    visit_terms = jnp.einsum(
        "cqr,crs->cqs", right_half, intersection, preferred_element_type=jnp.float32
    )
    pair_ids = lax.iota(jnp.int32, own_basis.shape[0])
    to_local = jnp.where(
        local_index[None, :] == pair_ids[:, None], weight[None, :], jnp.float32(0.0)
    )
    to_visit = jnp.where(
        visit_index[None, :] == pair_ids[:, None], weight[None, :], jnp.float32(0.0)
    )
    width = intersection.shape[1]
    slot_total = local_index.shape[0]
    local_add = jnp.dot(to_local, local_terms.reshape(slot_total, -1), precision=highest).reshape(
        pair_ids.shape[0], width, width
    )
    visit_add = jnp.dot(to_visit, visit_terms.reshape(slot_total, -1), precision=highest).reshape(
        pair_ids.shape[0], width, width
    )
    return (local_add, visit_add)


def on_device(pno_basis, amplitudes, pno_energy, fock_values, couplings, counts):
    own_basis = pno_basis[0, 0]
    own_amps = amplitudes[0, 0]
    own_energy = pno_energy[0, 0]
    couple_plan = couplings[0, 0]
    live_counts = counts[0, 0]
    residual = (own_energy[:, :, None] + own_energy[:, None, :]) * own_amps.astype(jnp.float32)
    for offset in range(REACH):
        visit_basis, visit_amps = passed_along((own_basis, own_amps), "iblk", offset + 1)
        local_add, visit_add = coupling_terms(
            couple_plan[offset],
            live_counts[offset],
            own_basis,
            own_amps,
            visit_basis,
            visit_amps,
            fock_values,
        )
        residual = residual + local_add
        residual = residual + passed_along(
            visit_add.astype(jnp.bfloat16), "iblk", -(offset + 1)
        ).astype(visit_add.dtype)
    for offset in range(REACH):
        visit_basis, visit_amps = passed_along((own_basis, own_amps), "jblk", offset + 1)
        local_add, visit_add = coupling_terms(
            couple_plan[REACH + offset],
            live_counts[REACH + offset],
            own_basis,
            own_amps,
            visit_basis,
            visit_amps,
            fock_values,
        )
        residual = residual + local_add
        residual = residual + passed_along(
            visit_add.astype(jnp.bfloat16), "jblk", -(offset + 1)
        ).astype(visit_add.dtype)
    return residual[None, None]


def solution(mesh):
    placed = (
        P("iblk", "jblk", None, None, None),
        P("iblk", "jblk", None, None, None),
        P("iblk", "jblk", None, None),
        P(),
        P("iblk", "jblk", None, None, None),
        P("iblk", "jblk", None),
    )
    return jax.shard_map(
        on_device,
        mesh=mesh,
        in_specs=placed,
        out_specs=P("iblk", "jblk", None, None, None),
        check_vma=False,
    )
```

profile of v0, /device:TPU:0, one launch (start us, length us, event | category | flops | bytes accessed | tf_op | source)
XLA Modules:
  0.0 76.7 jit_solution(2940545463763893952)
XLA Ops:
  0.0 1.0 %copy.152 = bf16[1,1,4,128,128]{4,2,3,1,0:T(4,128)(2,1)S(1)} copy(bf16[1,1,4,128,128]{4,3,2,1,0:T(8,128)(2,1)} %param.7) | data formatting | bytes 262144 | tf_op args[1]
  1.0 3.1 %collective-permute-start.10 = (bf16[4,128,128]{2,0,1:T(4,128)(2,1)S(1)}, bf16[4,128,128]{2,0,1:T(4,128)(2,1)S(1)}, u32[]{:S(2)}, u32[]{:S(2)}) collective-permute-start(bf16[4,128,128]{2,0,1:T(4,128)(2,1)S(1)} %bitcast.298), channel_id=1, source_target_pairs={{6,0},{7,1},{0,2},{1,3},{2,4},{3,5},{4,6},{5,7},{14,8},{15,9},{8,1... | collective-permute-start | bytes 393224 | tf_op jit(solution)/shard_map/ppermute | solution.py:12
  4.1 1.5 %collective-permute-start.7 = (bf16[4,128,128]{2,0,1:T(4,128)(2,1)S(1)}, bf16[4,128,128]{2,0,1:T(4,128)(2,1)S(1)}, u32[]{:S(2)}, u32[]{:S(2)}) collective-permute-start(bf16[4,128,128]{2,0,1:T(4,128)(2,1)S(1)} %bitcast.299), channel_id=1, source_target_pairs={{7,0},{0,1},{1,2},{2,3},{3,4},{4,5},{5,6},{6,7},{15,8},{8,9},{9,10... | collective-permute-start | bytes 393224 | tf_op jit(solution)/shard_map/ppermute | solution.py:12
  5.6 1.5 %collective-permute-start.4 = (bf16[4,128,128]{2,0,1:T(4,128)(2,1)S(1)}, bf16[4,128,128]{2,0,1:T(4,128)(2,1)S(1)}, u32[]{:S(2)}, u32[]{:S(2)}) collective-permute-start(bf16[4,128,128]{2,0,1:T(4,128)(2,1)S(1)} %bitcast.300), channel_id=1, source_target_pairs={{16,0},{24,8},{0,16},{8,24},{17,1},{25,9},{1,17},{9,25},{18,2},{26... | collective-permute-start | bytes 393224 | tf_op jit(solution)/shard_map/ppermute | solution.py:12
  7.1 2.1 %copy.57 = bf16[1,1,4,512,128]{3,4,2,1,0:T(8,128)(2,1)} copy(bf16[1,1,4,512,128]{4,3,2,1,0:T(8,128)(2,1)} %param.6) | data formatting | bytes 1048576 | tf_op args[0]
  9.2 1.6 %collective-permute-start.9 = (bf16[4,512,128]{1,2,0:T(8,128)(2,1)}, bf16[4,512,128]{1,2,0:T(8,128)(2,1)S(1)}, u32[]{:S(2)}, u32[]{:S(2)}) collective-permute-start(bf16[4,512,128]{1,2,0:T(8,128)(2,1)} %bitcast.6), channel_id=1, source_target_pairs={{6,0},{7,1},{0,2},{1,3},{2,4},{3,5},{4,6},{5,7},{14,8},{15,9},{8,1... | collective-permute-start | bytes 1572872 | tf_op jit(solution)/shard_map/ppermute | solution.py:12
  10.8 0.6 slice_bitcast_fusion.19
  11.5 0.7 fusion.101
  12.2 0.7 copy-done.19
  13.1 1.2 %compare_select_fusion.8 = f32[12]{0:T(128)} fusion(f32[12]{0:T(128)S(1)} %get-tuple-element.8, s32[]{:T(128)} %bitcast.58), kind=kLoop, calls=%fused_computation.122 | loop fusion | flops 24 | bytes 100 | tf_op jit(solution)/shard_map/jit(_where)/select_n | solution.py:24
  14.2 1.3 %compare_select_fusion.9 = f32[12]{0:T(128)} fusion(f32[12]{0:T(128)S(1)} %get-tuple-element.7, s32[]{:T(128)} %bitcast.40), kind=kLoop, calls=%fused_computation.123 | loop fusion | flops 24 | bytes 100 | tf_op jit(solution)/shard_map/jit(_where)/select_n | solution.py:24
  15.5 0.6 compare_select_fusion.10
  16.1 1.1 %compare_select_fusion.11 = f32[12]{0:T(128)} fusion(f32[12]{0:T(128)S(1)} %get-tuple-element.5, s32[]{:T(128)} %bitcast.3), kind=kLoop, calls=%fused_computation.125 | loop fusion | flops 24 | bytes 100 | tf_op jit(solution)/shard_map/jit(_where)/select_n | solution.py:24
  17.2 0.6 gather_fusion.11
  17.8 1.4 %gather_fusion.8 = bf16[12,128,128]{2,1,0:T(8,128)(2,1)} fusion(bf16[4,128,128]{2,1,0:T(8,128)(2,1)S(1)} %copy.63, s32[1024]{0:T(1024)S(1)} %pad_clamp_fusion.2), kind=kCustom, calls=%fused_computation.8 | custom fusion | bytes 786480 | tf_op jit(solution)/shard_map/gather | solution.py:46
  19.2 1.4 %gather_fusion.5 = bf16[12,128,128]{2,1,0:T(8,128)(2,1)} fusion(bf16[4,128,128]{2,1,0:T(8,128)(2,1)S(1)} %copy.63, s32[1024]{0:T(1024)S(1)} %pad_clamp_fusion.4), kind=kCustom, calls=%fused_computation.5 | custom fusion | bytes 786480 | tf_op jit(solution)/shard_map/gather | solution.py:46
  20.6 1.4 %gather_fusion.2 = bf16[12,128,128]{2,1,0:T(8,128)(2,1)} fusion(bf16[4,128,128]{2,1,0:T(8,128)(2,1)S(1)} %copy.63, s32[1024]{0:T(1024)S(1)} %pad_clamp_fusion.6), kind=kCustom, calls=%fused_computation.2 | custom fusion | bytes 786480 | tf_op jit(solution)/shard_map/gather | solution.py:46
  21.9 0.7 copy.55
  22.7 1.6 %collective-permute-start.6 = (bf16[4,512,128]{1,2,0:T(8,128)(2,1)}, bf16[4,512,128]{1,2,0:T(8,128)(2,1)S(1)}, u32[]{:S(2)}, u32[]{:S(2)}) collective-permute-start(bf16[4,512,128]{1,2,0:T(8,128)(2,1)} %bitcast.6), channel_id=1, source_target_pairs={{7,0},{0,1},{1,2},{2,3},{3,4},{4,5},{5,6},{6,7},{15,8},{8,9},{9,10... | collective-permute-start | bytes 1572872 | tf_op jit(solution)/shard_map/ppermute | solution.py:12
  24.3 0.6 gather_fusion.10
  24.9 0.6 collective-permute-start.3
  25.5 1.3 %gather_fusion.7 = bf16[12,128,128]{2,1,0:T(8,128)(2,1)} fusion(bf16[4,128,128]{2,1,0:T(8,128)(2,1)S(1)} %copy.75, s32[1024]{0:T(1024)S(1)} %pad_clamp_fusion.3), kind=kCustom, calls=%fused_computation.7 | custom fusion | bytes 786480 | tf_op jit(solution)/shard_map/gather | solution.py:40
  26.9 0.8 collective-permute-start
  27.7 1.4 %gather_fusion.4 = bf16[12,128,128]{2,1,0:T(8,128)(2,1)} fusion(bf16[4,128,128]{2,1,0:T(8,128)(2,1)S(1)} %copy.67, s32[1024]{0:T(1024)S(1)} %pad_clamp_fusion.5), kind=kCustom, calls=%fused_computation.4 | custom fusion | bytes 786480 | tf_op jit(solution)/shard_map/gather | solution.py:40
  29.1 1.4 %gather_fusion.1 = bf16[12,128,128]{2,1,0:T(8,128)(2,1)} fusion(bf16[4,128,128]{2,1,0:T(8,128)(2,1)S(1)} %copy.59, s32[1024]{0:T(1024)S(1)} %pad_clamp_fusion.7), kind=kCustom, calls=%fused_computation.1 | custom fusion | bytes 786480 | tf_op jit(solution)/shard_map/gather | solution.py:40
  30.4 0.4 convolution_bitcast_fusion
  30.9 0.7 gather_fusion.9
  31.5 0.5 fusion.7
  32.2 0.5 copy-done.8
  32.8 1.7 %convolution_convert_fusion.8 = bf16[4,128,128]{2,0,1:T(4,128)(2,1)} fusion(f32[128,128,12]{1,0,2:T(8,128)S(1)} %slice_bitcast_fusion, s32[12]{0:T(128)S(1)} %copy-done.16, f32[12]{0:T(128)S(1)} %copy-done.8), kind=kOutput, calls=%fused_computation.33 | convolution fusion | flops 9502816 | bytes 917600 | tf_op jit(solution)/shard_map/dot_general | solution.py:63
  34.5 2.2 %collective-permute-start.11 = (bf16[4,128,128]{2,0,1:T(4,128)(2,1)}, bf16[4,128,128]{2,0,1:T(4,128)(2,1)}, u32[]{:S(2)}, u32[]{:S(2)}) collective-permute-start(bf16[4,128,128]{2,0,1:T(4,128)(2,1)} %convolution_convert_fusion.8), channel_id=1, source_target_pairs={{2,0},{3,1},{4,2},{5,3},{6,4},{7,5},{0,6},{1,7},{10,8},{11,9},{12,... | collective-permute-start | bytes 393224 | tf_op jit(solution)/shard_map/ppermute | solution.py:12
  36.8 0.4 fusion.6
  37.2 2.7 %collective-permute-done.6 = bf16[4,512,128]{1,2,0:T(8,128)(2,1)S(1)} collective-permute-done((bf16[4,512,128]{1,2,0:T(8,128)(2,1)}, bf16[4,512,128]{1,2,0:T(8,128)(2,1)S(1)}, u32[]{:S(2)}, u32[]{:S(2)}) %collective-permute-start.6) | collective-permute-done | bytes 524320 | tf_op jit(solution)/shard_map/ppermute | solution.py:12
  40.0 0.4 convolution_bitcast_fusion.1
  40.4 0.7 gather_fusion.6
  41.1 1.5 %fusion.5 = f32[12,128,128]{2,1,0:T(8,128)S(1)} fusion(bf16[12,128,128]{2,1,0:T(8,128)(2,1)} %gather_fusion.8, bf16[12,128,128]{1,2,0:T(8,128)(2,1)S(1)} %gather_fusion.6), kind=kOutput, calls=%fused_computation.29 | convolution fusion | flops 100859904 | bytes 1572864 | tf_op jit(solution)/shard_map/cqr,crs->cqs/dot_general | solution.py:48
  42.7 0.6 copy-done.7
  43.3 1.1 %convolution_convert_fusion.9 = bf16[4,128,128]{2,0,1:T(4,128)(2,1)S(1)} fusion(f32[128,128,12]{1,0,2:T(8,128)S(1)} %slice_bitcast_fusion.2, s32[12]{0:T(128)S(1)} %copy-done.15, f32[12]{0:T(128)S(1)} %copy-done.7), kind=kOutput, calls=%fused_computation.34 | convolution fusion | flops 9502816 | bytes 917600 | tf_op jit(solution)/shard_map/dot_general | solution.py:63
  44.4 0.4 collective-permute-start.8
  44.9 1.4 %fusion.4 = f32[12,128,128]{2,1,0:T(8,128)S(1)} fusion(bf16[12,128,128]{2,1,0:T(8,128)(2,1)} %gather_fusion.7, bf16[12,128,128]{1,2,0:T(8,128)(2,1)S(1)} %gather_fusion.6), kind=kOutput, calls=%fused_computation.28 | convolution fusion | flops 100859904 | bytes 1572864 | tf_op jit(solution)/shard_map/cpr,csr->cps/dot_general | solution.py:42
  46.3 1.5 %convolution_bitcast_fusion.2 = bf16[4,4,128,128]{2,3,0,1:T(8,128)(2,1)S(1)} fusion(bf16[4,512,128]{1,2,0:T(8,128)(2,1)} %collective-permute-done.3, bf16[1,1,4,512,128]{4,3,2,1,0:T(8,128)(2,1)S(1)} %copy-done), kind=kOutput, calls=%fused_computation.14 | convolution fusion | flops 268435456 | bytes 1572864 | tf_op jit(solution)/shard_map/amp,bmq->abpq/dot_general | solution.py:34
  47.8 0.7 gather_fusion.3
  48.5 2.4 %fusion.3 = f32[12,128,128]{2,1,0:T(8,128)} fusion(bf16[12,128,128]{2,1,0:T(8,128)(2,1)} %gather_fusion.5, bf16[12,128,128]{1,2,0:T(8,128)(2,1)S(1)} %gather_fusion.3), kind=kOutput, calls=%fused_computation.27 | convolution fusion | flops 100859904 | bytes 1572864 | tf_op jit(solution)/shard_map/cqr,crs->cqs/dot_general | solution.py:48
  50.9 1.2 %slice_bitcast_fusion.4 = f32[128,128,12]{1,0,2:T(8,128)S(1)} fusion(f32[12,128,128]{2,1,0:T(8,128)} %fusion.3), kind=kLoop, calls=%fused_computation.52 | loop fusion | bytes 1572864 | tf_op jit(solution)/shard_map/dot_general | solution.py:63
  52.1 0.7 copy-done.14
  52.8 1.7 %convolution_convert_fusion.10 = bf16[4,128,128]{2,0,1:T(4,128)(2,1)} fusion(f32[128,128,12]{1,0,2:T(8,128)S(1)} %slice_bitcast_fusion.4, s32[12]{0:T(128)S(1)} %copy-done.14, f32[12]{0:T(128)S(1)} %compare_select_fusion.10), kind=kOutput, calls=%fused_computation.35 | convolution fusion | flops 9502816 | bytes 917600 | tf_op jit(solution)/shard_map/dot_general | solution.py:63
  54.5 0.8 %collective-permute-start.5 = (bf16[4,128,128]{2,0,1:T(4,128)(2,1)}, bf16[4,128,128]{2,0,1:T(4,128)(2,1)}, u32[]{:S(2)}, u32[]{:S(2)}) collective-permute-start(bf16[4,128,128]{2,0,1:T(4,128)(2,1)} %convolution_convert_fusion.10), channel_id=1, source_target_pairs={{16,0},{24,8},{0,16},{8,24},{17,1},{25,9},{1,17},{9,25},{18,2},{26... | collective-permute-start | bytes 393224 | tf_op jit(solution)/shard_map/ppermute | solution.py:12
  55.3 2.3 %fusion.2 = f32[12,128,128]{2,1,0:T(8,128)} fusion(bf16[12,128,128]{2,1,0:T(8,128)(2,1)} %gather_fusion.4, bf16[12,128,128]{1,2,0:T(8,128)(2,1)S(1)} %gather_fusion.3), kind=kOutput, calls=%fused_computation.26 | convolution fusion | flops 100859904 | bytes 1572864 | tf_op jit(solution)/shard_map/cpr,csr->cps/dot_general | solution.py:42
  57.7 1.2 %slice_bitcast_fusion.5 = f32[128,128,12]{1,0,2:T(8,128)S(1)} fusion(f32[12,128,128]{2,1,0:T(8,128)} %fusion.2), kind=kLoop, calls=%fused_computation.53 | loop fusion | bytes 1572864 | tf_op jit(solution)/shard_map/dot_general | solution.py:60
  58.9 1.5 %convolution_bitcast_fusion.3 = bf16[4,4,128,128]{2,3,0,1:T(8,128)(2,1)S(1)} fusion(bf16[1,1,4,512,128]{4,3,2,1,0:T(8,128)(2,1)S(1)} %copy-done, bf16[4,512,128]{1,2,0:T(8,128)(2,1)} %collective-permute-done), kind=kOutput, calls=%fused_computation.15 | convolution fusion | flops 268435456 | bytes 1572864 | tf_op jit(solution)/shard_map/amp,bmq->abpq/dot_general | solution.py:34
  60.4 0.7 gather_fusion
  61.0 2.4 %fusion.1 = f32[12,128,128]{2,1,0:T(8,128)} fusion(bf16[12,128,128]{2,1,0:T(8,128)(2,1)} %gather_fusion.2, bf16[12,128,128]{1,2,0:T(8,128)(2,1)S(1)} %gather_fusion), kind=kOutput, calls=%fused_computation.25 | convolution fusion | flops 100859904 | bytes 1572864 | tf_op jit(solution)/shard_map/cqr,crs->cqs/dot_general | solution.py:48
  63.4 1.2 %slice_bitcast_fusion.6 = f32[128,128,12]{1,0,2:T(8,128)S(1)} fusion(f32[12,128,128]{2,1,0:T(8,128)} %fusion.1), kind=kLoop, calls=%fused_computation.54 | loop fusion | bytes 1572864 | tf_op jit(solution)/shard_map/dot_general | solution.py:63
  64.7 0.6 copy-done.13
  65.3 1.1 %convolution_convert_fusion.11 = bf16[4,128,128]{2,0,1:T(4,128)(2,1)S(1)} fusion(f32[128,128,12]{1,0,2:T(8,128)S(1)} %slice_bitcast_fusion.6, s32[12]{0:T(128)S(1)} %copy-done.13, f32[12]{0:T(128)S(1)} %copy-done.20), kind=kOutput, calls=%fused_computation.36 | convolution fusion | flops 9502816 | bytes 917600 | tf_op jit(solution)/shard_map/dot_general | solution.py:63
  66.6 1.3 %fusion = f32[12,128,128]{2,1,0:T(8,128)} fusion(bf16[12,128,128]{2,1,0:T(8,128)(2,1)S(1)} %copy-done.2, bf16[12,128,128]{1,2,0:T(8,128)(2,1)S(1)} %gather_fusion), kind=kOutput, calls=%fused_computation.24 | convolution fusion | flops 100859904 | bytes 1572864 | tf_op jit(solution)/shard_map/cpr,csr->cps/dot_general | solution.py:42
  68.0 0.6 copy-done.9
  68.6 1.1 %fusion.9 = f32[4,128,128]{2,0,1:T(4,128)S(1)} fusion(f32[128,128,12]{1,0,2:T(8,128)S(1)} %slice_bitcast_fusion.1, f32[12]{0:T(128)S(1)} %copy-done.9, s32[12]{0:T(128)S(1)} %copy-done.12), kind=kOutput, calls=%fused_computation.38 | convolution fusion | flops 9437280 | bytes 1048672 | tf_op jit(solution)/shard_map/dot_general | solution.py:60
  69.7 0.7 copy-done.11
  70.4 1.1 %fusion.12 = f32[4,128,128]{2,0,1:T(4,128)S(1)} fusion(f32[128,128,12]{1,0,2:T(8,128)S(1)} %slice_bitcast_fusion.3, f32[12]{0:T(128)S(1)} %copy-done.7, s32[12]{0:T(128)S(1)} %copy-done.11), kind=kOutput, calls=%fused_computation.41 | convolution fusion | flops 9437280 | bytes 1048672 | tf_op jit(solution)/shard_map/dot_general | solution.py:60
  71.5 1.1 %fusion.15 = f32[4,128,128]{2,0,1:T(4,128)S(1)} fusion(f32[128,128,12]{1,0,2:T(8,128)S(1)} %slice_bitcast_fusion.5, f32[12]{0:T(128)S(1)} %compare_select_fusion.10, s32[12]{0:T(128)S(1)} %copy-done.10), kind=kOutput, calls=%fused_computation.44 | convolution fusion | flops 9437280 | bytes 1048672 | tf_op jit(solution)/shard_map/dot_general | solution.py:60
  72.7 0.8 %copy-done.3 = bf16[1,1,4,128,128]{4,3,2,1,0:T(8,128)(2,1)S(1)} copy-done((bf16[1,1,4,128,128]{4,3,2,1,0:T(8,128)(2,1)S(1)}, bf16[1,1,4,128,128]{4,3,2,1,0:T(8,128)(2,1)}, u32[]{:S(2)}) %copy-start.3) | copy-done | bytes 131096
  73.5 2.5 %add_bitcast_fusion = f32[1,1,4,128,128]{4,2,3,1,0:T(4,128)S(1)} fusion(bf16[4,128,128]{2,0,1:T(4,128)(2,1)} %collective-permute-done.11, f32[4,128,128]{2,0,1:T(4,128)S(1)} %fusion.9, bf16[4,128,128]{2,0,1:T(4,128)(2,1)} %collective-permute-done.8, f32[4,128,128]{2,0,1:T(4,128)S(1)} %fusion.12, bf16[4,128,128]{2,0,1:T(4,128)(2,1)} %collective-permute-done.5, ...), kind=kOutput, calls=%fused_computation.64 | convolution fusion | flops 10420320 | bytes 2494560 | tf_op jit(solution)/shard_map/dot_general | solution.py:60
  76.0 0.7 copy.90
  (69 shorter events, 1.2 us)
Async XLA Ops:
  1.0 9.8 %copy-start.5 = (s32[1,1,4,3,12]{4,2,3,1,0:T(4,128)S(1)}, s32[1,1,4,3,12]{4,2,3,1,0:T(4,128)}, u32[]{:S(2)}) copy-start(s32[1,1,4,3,12]{4,2,3,1,0:T(4,128)} %param.10) | copy-start | bytes 1732
  1.0 21.6 %collective-permute-start.10 = (bf16[4,128,128]{2,0,1:T(4,128)(2,1)S(1)}, bf16[4,128,128]{2,0,1:T(4,128)(2,1)S(1)}, u32[]{:S(2)}, u32[]{:S(2)}) collective-permute-start(bf16[4,128,128]{2,0,1:T(4,128)(2,1)S(1)} %bitcast.298), channel_id=1, source_target_pairs={{6,0},{7,1},{0,2},{1,3},{2,4},{3,5},{4,6},{5,7},{14,8},{15,9},{8,1... | collective-permute-start | bytes 393224 | tf_op jit(solution)/shard_map/ppermute | solution.py:12
  4.1 20.8 %collective-permute-start.7 = (bf16[4,128,128]{2,0,1:T(4,128)(2,1)S(1)}, bf16[4,128,128]{2,0,1:T(4,128)(2,1)S(1)}, u32[]{:S(2)}, u32[]{:S(2)}) collective-permute-start(bf16[4,128,128]{2,0,1:T(4,128)(2,1)S(1)} %bitcast.299), channel_id=1, source_target_pairs={{7,0},{0,1},{1,2},{2,3},{3,4},{4,5},{5,6},{6,7},{15,8},{8,9},{9,10... | collective-permute-start | bytes 393224 | tf_op jit(solution)/shard_map/ppermute | solution.py:12
  5.6 21.2 %collective-permute-start.4 = (bf16[4,128,128]{2,0,1:T(4,128)(2,1)S(1)}, bf16[4,128,128]{2,0,1:T(4,128)(2,1)S(1)}, u32[]{:S(2)}, u32[]{:S(2)}) collective-permute-start(bf16[4,128,128]{2,0,1:T(4,128)(2,1)S(1)} %bitcast.300), channel_id=1, source_target_pairs={{16,0},{24,8},{0,16},{8,24},{17,1},{25,9},{1,17},{9,25},{18,2},{26... | collective-permute-start | bytes 393224 | tf_op jit(solution)/shard_map/ppermute | solution.py:12
  7.1 21.9 %collective-permute-start.1 = (bf16[4,128,128]{2,0,1:T(4,128)(2,1)S(1)}, bf16[4,128,128]{2,0,1:T(4,128)(2,1)S(1)}, u32[]{:S(2)}, u32[]{:S(2)}) collective-permute-start(bf16[4,128,128]{2,0,1:T(4,128)(2,1)S(1)} %bitcast.301), channel_id=1, source_target_pairs={{24,0},{0,8},{8,16},{16,24},{25,1},{1,9},{9,17},{17,25},{26,2},{2,... | collective-permute-start | bytes 393224 | tf_op jit(solution)/shard_map/ppermute | solution.py:12
  9.2 21.2 %collective-permute-start.9 = (bf16[4,512,128]{1,2,0:T(8,128)(2,1)}, bf16[4,512,128]{1,2,0:T(8,128)(2,1)S(1)}, u32[]{:S(2)}, u32[]{:S(2)}) collective-permute-start(bf16[4,512,128]{1,2,0:T(8,128)(2,1)} %bitcast.6), channel_id=1, source_target_pairs={{6,0},{7,1},{0,2},{1,3},{2,4},{3,5},{4,6},{5,7},{14,8},{15,9},{8,1... | collective-permute-start | bytes 1572872 | tf_op jit(solution)/shard_map/ppermute | solution.py:12
  10.8 0.7 copy-start.6
  12.2 0.7 copy-start.19
  20.6 1.4 %copy-start.17 = (f32[1,1,4,128]{3,2,1,0:T(4,128)S(1)}, f32[1,1,4,128]{3,2,1,0:T(4,128)}, u32[]{:S(2)}) copy-start(f32[1,1,4,128]{3,2,1,0:T(4,128)} %param.8) | copy-start | bytes 6148
  22.7 17.3 %collective-permute-start.6 = (bf16[4,512,128]{1,2,0:T(8,128)(2,1)}, bf16[4,512,128]{1,2,0:T(8,128)(2,1)S(1)}, u32[]{:S(2)}, u32[]{:S(2)}) collective-permute-start(bf16[4,512,128]{1,2,0:T(8,128)(2,1)} %bitcast.6), channel_id=1, source_target_pairs={{7,0},{0,1},{1,2},{2,3},{3,4},{4,5},{5,6},{6,7},{15,8},{8,9},{9,10... | collective-permute-start | bytes 1572872 | tf_op jit(solution)/shard_map/ppermute | solution.py:12
  24.9 21.4 %collective-permute-start.3 = (bf16[4,512,128]{1,2,0:T(8,128)(2,1)}, bf16[4,512,128]{1,2,0:T(8,128)(2,1)}, u32[]{:S(2)}, u32[]{:S(2)}) collective-permute-start(bf16[4,512,128]{1,2,0:T(8,128)(2,1)} %bitcast.6), channel_id=1, source_target_pairs={{16,0},{24,8},{0,16},{8,24},{17,1},{25,9},{1,17},{9,25},{18,2},{26... | collective-permute-start | bytes 1572872 | tf_op jit(solution)/shard_map/ppermute | solution.py:12
  26.9 32.0 %collective-permute-start = (bf16[4,512,128]{1,2,0:T(8,128)(2,1)}, bf16[4,512,128]{1,2,0:T(8,128)(2,1)}, u32[]{:S(2)}, u32[]{:S(2)}) collective-permute-start(bf16[4,512,128]{1,2,0:T(8,128)(2,1)} %bitcast.6), channel_id=1, source_target_pairs={{24,0},{0,8},{8,16},{16,24},{25,1},{1,9},{9,17},{17,25},{26,2},{2,... | collective-permute-start | bytes 1572872 | tf_op jit(solution)/shard_map/ppermute | solution.py:12
  29.0 1.4 %copy-start = (bf16[1,1,4,512,128]{4,3,2,1,0:T(8,128)(2,1)S(1)}, bf16[1,1,4,512,128]{4,3,2,1,0:T(8,128)(2,1)}, u32[]{:S(2)}) copy-start(bf16[1,1,4,512,128]{4,3,2,1,0:T(8,128)(2,1)} %param.6) | copy-start | bytes 1572868
  32.1 0.6 copy-start.8
  32.2 0.7 copy-start.16
  34.5 38.1 %collective-permute-start.11 = (bf16[4,128,128]{2,0,1:T(4,128)(2,1)}, bf16[4,128,128]{2,0,1:T(4,128)(2,1)}, u32[]{:S(2)}, u32[]{:S(2)}) collective-permute-start(bf16[4,128,128]{2,0,1:T(4,128)(2,1)} %convolution_convert_fusion.8), channel_id=1, source_target_pairs={{2,0},{3,1},{4,2},{5,3},{6,4},{7,5},{0,6},{1,7},{10,8},{11,9},{12,... | collective-permute-start | bytes 393224 | tf_op jit(solution)/shard_map/ppermute | solution.py:12
  42.7 0.7 copy-start.7
  42.7 0.7 copy-start.15
  44.4 28.3 %collective-permute-start.8 = (bf16[4,128,128]{2,0,1:T(4,128)(2,1)S(1)}, bf16[4,128,128]{2,0,1:T(4,128)(2,1)}, u32[]{:S(2)}, u32[]{:S(2)}) collective-permute-start(bf16[4,128,128]{2,0,1:T(4,128)(2,1)S(1)} %convolution_convert_fusion.9), channel_id=1, source_target_pairs={{1,0},{2,1},{3,2},{4,3},{5,4},{6,5},{7,6},{0,7},{9,8},{10,9},{11,1... | collective-permute-start | bytes 393224 | tf_op jit(solution)/shard_map/ppermute | solution.py:12
  52.1 0.7 copy-start.14
  54.5 18.2 %collective-permute-start.5 = (bf16[4,128,128]{2,0,1:T(4,128)(2,1)}, bf16[4,128,128]{2,0,1:T(4,128)(2,1)}, u32[]{:S(2)}, u32[]{:S(2)}) collective-permute-start(bf16[4,128,128]{2,0,1:T(4,128)(2,1)} %convolution_convert_fusion.10), channel_id=1, source_target_pairs={{16,0},{24,8},{0,16},{8,24},{17,1},{25,9},{1,17},{9,25},{18,2},{26... | collective-permute-start | bytes 393224 | tf_op jit(solution)/shard_map/ppermute | solution.py:12
  64.6 0.7 copy-start.13
  64.6 0.7 copy-start.20
  65.3 1.3 %copy-start.2 = (bf16[12,128,128]{2,1,0:T(8,128)(2,1)S(1)}, bf16[12,128,128]{2,1,0:T(8,128)(2,1)}, u32[]{:S(2)}) copy-start(bf16[12,128,128]{2,1,0:T(8,128)(2,1)} %gather_fusion.1) | copy-start | bytes 1179652
  66.4 6.3 %collective-permute-start.2 = (bf16[4,128,128]{2,0,1:T(4,128)(2,1)S(1)}, bf16[4,128,128]{2,0,1:T(4,128)(2,1)}, u32[]{:S(2)}, u32[]{:S(2)}) collective-permute-start(bf16[4,128,128]{2,0,1:T(4,128)(2,1)S(1)} %convolution_convert_fusion.11), channel_id=1, source_target_pairs={{8,0},{16,8},{24,16},{0,24},{9,1},{17,9},{25,17},{1,25},{10,2},{18... | collective-permute-start | bytes 393224 | tf_op jit(solution)/shard_map/ppermute | solution.py:12
  68.0 0.6 copy-start.9
  68.0 0.7 copy-start.12
  69.7 0.7 copy-start.11
  70.4 1.1 %copy-start.10 = (s32[12]{0:T(128)S(1)}, s32[12]{0:T(128)}, u32[]{:S(2)}) copy-start(s32[12]{0:T(128)} %get-tuple-element.18) | copy-start | bytes 148
  71.5 1.1 %copy-start.1 = (f32[12,128,128]{2,1,0:T(8,128)S(1)}, f32[12,128,128]{2,1,0:T(8,128)}, u32[]{:S(2)}) copy-start(f32[12,128,128]{2,1,0:T(8,128)} %fusion) | copy-start | bytes 2359300
  72.6 0.9 %copy-start.3 = (bf16[1,1,4,128,128]{4,3,2,1,0:T(8,128)(2,1)S(1)}, bf16[1,1,4,128,128]{4,3,2,1,0:T(8,128)(2,1)}, u32[]{:S(2)}) copy-start(bf16[1,1,4,128,128]{4,3,2,1,0:T(8,128)(2,1)} %param.7) | copy-start | bytes 393220
  72.6 0.9 %copy-start.4 = (f32[4,128]{0,1:T(8,128)S(1)}, f32[4,128]{0,1:T(8,128)}, u32[]{:S(2)}) copy-start(f32[4,128]{0,1:T(8,128)} %copy.55) | copy-start | bytes 6148
  72.6 0.9 %copy-start.18 = (f32[1,1,4,128]{3,2,1,0:T(4,128)S(1)}, f32[1,1,4,128]{3,2,1,0:T(4,128)}, u32[]{:S(2)}) copy-start(f32[1,1,4,128]{3,2,1,0:T(4,128)} %param.8) | copy-start | bytes 6148
  72.7 0.8 %copy-start.21 = (s32[12]{0:T(128)S(1)}, s32[12]{0:T(128)}, u32[]{:S(2)}) copy-start(s32[12]{0:T(128)} %get-tuple-element.9) | copy-start | bytes 148
where the time goes:
time: 77.5 us; the launch traced here: 76.7 us
  matrix products  27.5 us (35%)
  local copies, waits for them, and re-layouts  27.3 us (35%)
  starting transfers between devices  14.3 us (18%)
  other arithmetic  4.34 us (6%)
  waiting for transfers between devices  2.75 us (4%)
    ppermute x12, starting transfers between devices, passed_along(): return lax.ppermute(block, axis, route)  14.3 us
    unnamed x46, local copies, waits for them, and re-layouts  8.6 us
    dot_general x4, matrix products, coupling_terms(): jnp.einsum('cqr,crs->cqs', right_half, intersection, preferred_element_ty...  6.9 us
    dot_general x4, matrix products, coupling_terms(): jnp.dot(to_local, local_terms.reshape(slot_total, -1), precision=highest)  5.67 us
    dot_general x4, matrix products, coupling_terms(): jnp.dot(to_visit, visit_terms.reshape(slot_total, -1), precision=highest)  5.59 us
    dot_general x4, matrix products, coupling_terms(): jnp.einsum('cpr,csr->cps', left_half, intersection, preferred_element_typ...  5.53 us
    gather x4, local copies, waits for them, and re-layouts, coupling_terms(): visit_amps[visit_index]  4.7 us
    gather x4, local copies, waits for them, and re-layouts, coupling_terms(): own_amps[local_index]  4.7 us
  transfers between devices with their start and end apart: 12, of which 1 were waited for; matrix products, arithmetic and copies ran while one was open for 65% of the time, Pallas kernels for 0%

commit v1 on v0

v1 whole, which is shorter than its diff:
```python
import functools

import jax
import jax.numpy as jnp
from jax import lax
from jax.experimental import pallas as pl
from jax.experimental.pallas import tpu as pltpu
from jax.sharding import PartitionSpec as P

F32, BF16, I32 = jnp.float32, jnp.bfloat16, jnp.int32
AXES = ("iblk", "jblk")
PARTS = 3
ROLES = 4
OWN, PARTNER, HEAVY, LIGHT = range(ROLES)
OP, OH, PH, OL = range(4)
META = 16
LANES = 128


def routes(ni, nj):
    def flow(i, j):
        return (1 if j % 2 == 0 else -1), (1 if i % 2 == 1 else -1)

    def along_i(i, j):
        return (i - 2 * flow(i, j)[0]) % ni, j

    def along_j(i, j):
        return i, (j - 2 * flow(i, j)[1]) % nj

    def odd(i, j):
        return (i + j) % 2 == 1

    picks = (
        lambda i, j: (i ^ 1, j) if odd(i, j) else (i, j ^ 1),
        lambda i, j: along_i(i, j) if odd(i, j) else along_j(i, j),
        lambda i, j: along_j(i, j) if odd(i, j) else along_i(i, j),
    )
    made = []
    for pick in picks:
        pairs = []
        for i in range(ni):
            for j in range(nj):
                si, sj = pick(i, j)
                pairs.append((si * nj + sj, i * nj + j))
        made.append(pairs)
    return made


def moved(block, route):
    return lax.ppermute(block, AXES, route)


def back(route):
    return [(b, a) for a, b in route]


def dot(a, b):
    return lax.dot_general(a, b, (((1,), (0,)), ((), ())), preferred_element_type=F32)


def dot_nt(a, b):
    return lax.dot_general(a, b, (((1,), (1,)), ((), ())), preferred_element_type=F32)


def two_blocks(a, b):
    zero = jnp.zeros_like(a)
    return jnp.concatenate(
        [jnp.concatenate([a, zero], 1), jnp.concatenate([zero, b], 1)], 0
    )


def prep_kernel(reach, plan, counts, fock, basis, amps, sent, turned):
    pairs, _, width = amps.shape
    steps, _, slots = plan.shape
    i, j = lax.axis_index(AXES[0]) % 2, lax.axis_index(AXES[1]) % 2
    forward = (1 - j, i)
    i_heavy = (i + j) % 2
    lane = lax.broadcasted_iota(I32, (META, LANES), 1)
    row = lax.broadcasted_iota(I32, (META, LANES), 0)
    table = jnp.zeros((META, LANES), F32)
    for t in range(steps):
        axis, far = t // reach, t % reach
        heavy = i_heavy if axis == 0 else 1 - i_heavy
        ahead = forward[axis]
        if far:
            role_h, slot_h = jnp.where(ahead == 1, OWN, HEAVY), OH
            role_l, slot_l = jnp.where(ahead == 1, OWN, LIGHT), OL
        else:
            role_h, slot_h = jnp.where(ahead == 1, OWN, HEAVY), jnp.where(ahead == 1, OP, PH)
            role_l, slot_l = PARTNER, jnp.where(ahead == 1, PH, OP)
        role = jnp.where(heavy == 1, role_h, role_l)
        slot = jnp.where(heavy == 1, slot_h, slot_l)
        base = slot * (pairs * pairs)
        live = counts[t]

        def place(c, weight):
            p, q = plan[t, 0, c], plan[t, 1, c]
            at = base + jnp.where(ahead == 1, p * pairs + q, q * pairs + p)
            value = jnp.where(c < live, fock[plan[t, 2, c]], jnp.float32(0.0))
            return jnp.where(lane == at, value, weight)

        weight = lax.fori_loop(0, slots, place, jnp.zeros((META, LANES), F32), unroll=True)
        high = weight.astype(BF16).astype(F32)
        rest = weight - high
        middle = rest.astype(BF16).astype(F32)
        for part, piece in enumerate((high, middle, rest - middle)):
            table = jnp.where(row == part * ROLES + role, piece + table, table)
    sent[pl.ds(0, pairs * width), :] = amps[...].reshape(pairs * width, width)
    sent[pl.ds(pairs * width, META), :] = table.astype(BF16)
    for p in range(pairs):
        turned[pl.ds(p * width, width), :] = basis[p].T


def weight_rows(blocks, slot, pairs):
    row = jnp.zeros((1, LANES), F32)
    tables = [(table.astype(F32), role) for table, role in blocks]
    for part in range(PARTS):
        for table, role in tables:
            at = part * ROLES + role
            row = row + table[at : at + 1]
    shape = (pairs * pairs, LANES)
    mine = lax.broadcasted_iota(I32, shape, 1) == (
        slot * pairs * pairs + lax.broadcasted_iota(I32, shape, 0)
    )
    picked = jnp.sum(jnp.where(mine, row, jnp.float32(0.0)), axis=1, keepdims=True)
    wide = jnp.broadcast_to(picked, shape)
    return [[wide[p * pairs + q : p * pairs + q + 1] for q in range(pairs)] for p in range(pairs)]


def couple(turned, amps, other_basis, other_amps, weight, width):
    rows, columns = len(amps), len(other_amps)
    cut = lambda a, r, c: a[r * width : (r + 1) * width, c * width : (c + 1) * width]
    near = jnp.concatenate(
        [
            dot(turned, jnp.concatenate(other_basis[k : k + 2], 1)).astype(BF16)
            for k in range(0, columns, 2)
        ],
        1,
    )
    near_t = near.T
    left = jnp.concatenate(
        [
            dot(
                near[:, k * width : (k + 2) * width], two_blocks(other_amps[k], other_amps[k + 1])
            ).astype(BF16)
            for k in range(0, columns, 2)
        ],
        1,
    )
    right = jnp.concatenate(
        [
            dot(near_t[:, k * width : (k + 2) * width], two_blocks(amps[k], amps[k + 1])).astype(
                BF16
            )
            for k in range(0, rows, 2)
        ],
        1,
    )
    own, other = [], []
    for p in range(rows):
        own.append(
            sum(
                dot_nt(cut(left, p, q), cut(near, p, q)) * weight[p][q] for q in range(columns)
            )
        )
    for q in range(columns):
        other.append(
            sum(dot(cut(right, q, p), cut(near, p, q)) * weight[p][q] for p in range(rows))
        )
    return own, other


def amps_of(ref, pairs, width):
    return [ref[pl.ds(p * width, width), :] for p in range(pairs)]


def heavy_kernel(
    turned, own_sent, p_basis, p_sent, h_basis, h_sent, energy, total, p_back, h_back
):
    pairs, depth, width = p_basis.shape
    own_a, p_a, h_a = (amps_of(r, pairs, width) for r in (own_sent, p_sent, h_sent))
    meta = pl.ds(pairs * width, META)
    tables = ((own_sent[meta, :], OWN), (p_sent[meta, :], PARTNER), (h_sent[meta, :], HEAVY))
    p_b = [p_basis[p] for p in range(pairs)]
    h_b = [h_basis[p] for p in range(pairs)]
    own_t = turned[...]
    x1, y1 = couple(own_t, own_a, p_b, p_a, weight_rows(tables, OP, pairs), width)
    x2, y2 = couple(own_t, own_a, h_b, h_a, weight_rows(tables, OH, pairs), width)
    p_t = jnp.concatenate([b.T for b in p_b], 0)
    x3, y3 = couple(p_t, p_a, h_b, h_a, weight_rows(tables, PH, pairs), width)
    for p in range(pairs):
        across = jnp.broadcast_to(energy[pl.ds(p, 1), :], (width, width))
        diagonal = (across.T + across) * own_a[p].astype(F32)
        total[p] = diagonal + (x1[p] + x2[p])
        p_back[p] = (y1[p] + x3[p]).astype(BF16)
        h_back[p] = (y2[p] + y3[p]).astype(BF16)


def light_kernel(turned, own_sent, l_basis, l_sent, total_in, total, l_back):
    pairs, depth, width = l_basis.shape
    own_a, l_a = (amps_of(r, pairs, width) for r in (own_sent, l_sent))
    meta = pl.ds(pairs * width, META)
    tables = ((own_sent[meta, :], OWN), (l_sent[meta, :], LIGHT))
    l_b = [l_basis[p] for p in range(pairs)]
    x, y = couple(turned[...], own_a, l_b, l_a, weight_rows(tables, OL, pairs), width)
    for p in range(pairs):
        total[p] = total_in[p] + x[p]
        l_back[p] = y[p].astype(BF16)


def on_device(all_routes, reach, pno_basis, amplitudes, pno_energy, fock_values, couplings, counts):
    to_p, to_h, to_l = all_routes
    basis, amps, energy = pno_basis[0, 0], amplitudes[0, 0], pno_energy[0, 0]
    pairs, depth, width = basis.shape
    vmem, smem = pl.BlockSpec(memory_space=pltpu.VMEM), pl.BlockSpec(memory_space=pltpu.SMEM)
    params = pltpu.CompilerParams(vmem_limit_bytes=48 * 1024 * 1024)
    square = (pairs, width, width)
    sent, turned = pl.pallas_call(
        functools.partial(prep_kernel, reach),
        out_shape=(
            jax.ShapeDtypeStruct((pairs * width + META, width), BF16),
            jax.ShapeDtypeStruct((pairs * width, depth), BF16),
        ),
        in_specs=[smem, smem, smem, vmem, vmem],
        out_specs=(vmem, vmem),
        compiler_params=params,
        name="prep",
    )(couplings[0, 0], counts[0, 0], fock_values, basis, amps)
    h_basis, p_basis = moved(basis, to_h), moved(basis, to_p)
    h_sent, p_sent = moved(sent, to_h), moved(sent, to_p)
    l_basis, l_sent = moved(basis, to_l), moved(sent, to_l)
    flops = 2 * pairs * pairs * (width * width * depth + 4 * width**3)
    total, p_back, h_back = pl.pallas_call(
        heavy_kernel,
        out_shape=(
            jax.ShapeDtypeStruct(square, F32),
            jax.ShapeDtypeStruct(square, BF16),
            jax.ShapeDtypeStruct(square, BF16),
        ),
        in_specs=[vmem] * 7,
        out_specs=(vmem,) * 3,
        compiler_params=params,
        cost_estimate=pl.CostEstimate(
            flops=3 * flops, bytes_accessed=3 * basis.size * 2, transcendentals=0
        ),
        name="heavy",
    )(turned, sent, p_basis, p_sent, h_basis, h_sent, energy)
    total, l_back = pl.pallas_call(
        light_kernel,
        out_shape=(jax.ShapeDtypeStruct(square, F32), jax.ShapeDtypeStruct(square, BF16)),
        in_specs=[vmem] * 5,
        out_specs=(vmem,) * 2,
        compiler_params=params,
        cost_estimate=pl.CostEstimate(
            flops=flops, bytes_accessed=basis.size * 2, transcendentals=0
        ),
        name="light",
    )(turned, sent, l_basis, l_sent, total)
    for piece, route in ((p_back, to_p), (h_back, to_h), (l_back, to_l)):
        total = total + moved(piece, back(route)).astype(F32)
    return total[None, None]


def solution(mesh):
    ni, nj = (mesh.shape[a] for a in AXES)
    assert ni % 2 == 0 and nj % 2 == 0 and min(ni, nj) > 2
    placed = (
        P("iblk", "jblk", None, None, None),
        P("iblk", "jblk", None, None, None),
        P("iblk", "jblk", None, None),
        P(),
        P("iblk", "jblk", None, None, None),
        P("iblk", "jblk", None),
    )
    return jax.shard_map(
        functools.partial(on_device, routes(ni, nj), 2),
        mesh=mesh,
        in_specs=placed,
        out_specs=P("iblk", "jblk", None, None, None),
        check_vma=False,
    )
```

time: 77.5 us -> 34.8 us (0.45)
  matrix products: 27.5 us -> 0 us
  local copies, waits for them, and re-layouts: 27.3 us -> 3.33 us
  waiting for transfers between devices: 2.75 us -> 12.8 us
  Pallas kernels: 0 us -> 5.23 us
  other arithmetic: 4.34 us -> 0.76 us
  starting transfers between devices: 14.3 us -> 12.4 us
    dot_general x20 -> x0, matrix products: 27.5 us -> none  [the longest x4 6.9 us: coupling_terms(): jnp.einsum('cqr,crs->cqs', right_half, intersection, preferred_element_ty...]
    gather x12 -> x0, local copies, waits for them, and re-layouts: 12.1 us -> none  [the longest x4 4.7 us: coupling_terms(): visit_amps[visit_index]]
    ppermute x12 -> x9, waiting for transfers between devices: 2.75 us -> 12.8 us  [moved(): return lax.ppermute(block, AXES, route)]
    unnamed x46 -> x11, local copies, waits for them, and re-layouts: 8.6 us -> 3.33 us
    pallas_call x0 -> x3, Pallas kernels: none -> 5.23 us  [the longest x1 3.12 us: on_device(): pl.pallas_call(heavy_kernel, out_shape=(jax.ShapeDtypeStruct(square, F32)...]
    select_n x5 -> x0, other arithmetic: 4.08 us -> none  [the longest x4 4.06 us: lookup_weights(): return jnp.where(slot_ids < live_count, picked, jnp.float32(0.0))]
    dot_general x8 -> x0, local copies, waits for them, and re-layouts: 3.82 us -> none  [the longest x4 2.48 us: coupling_terms(): jnp.dot(to_visit, visit_terms.reshape(slot_total, -1), precision=highest)]
    ppermute x12 -> x9, starting transfers between devices: 14.3 us -> 12.4 us  [moved(): return lax.ppermute(block, AXES, route)]
  transfers between devices with their start and end apart: 12 -> 9, of which waited for: 1 -> 5; matrix products, arithmetic and copies ran while one was open for 65% -> 2% of each run, Pallas kernels for 0% -> 12%
where the time goes in v1:
time: 34.8 us; the launch traced here: 34.5 us
  waiting for transfers between devices  12.8 us (37%)
  starting transfers between devices  12.4 us (36%)
  Pallas kernels  5.23 us (15%)
  local copies, waits for them, and re-layouts  3.33 us (10%)
  other arithmetic  0.76 us (2%)
    ppermute x9, waiting for transfers between devices, moved(): return lax.ppermute(block, AXES, route)  12.8 us
    ppermute x9, starting transfers between devices, moved(): return lax.ppermute(block, AXES, route)  12.4 us
    unnamed x11, local copies, waits for them, and re-layouts  3.33 us
    pallas_call x1, Pallas kernels, on_device(): pl.pallas_call(heavy_kernel, out_shape=(jax.ShapeDtypeStruct(square, F32)...  3.12 us
    pallas_call x1, Pallas kernels, on_device(): pl.pallas_call(light_kernel, out_shape=(jax.ShapeDtypeStruct(square, F32)...  1.14 us
    pallas_call x1, Pallas kernels, on_device(): pl.pallas_call(functools.partial(prep_kernel, reach), out_shape=(jax.Shap...  0.97 us
    broadcast_in_dim x1, other arithmetic, on_device(): return total[None, None]  0.76 us
  transfers between devices with their start and end apart: 9, of which 5 were waited for; matrix products, arithmetic and copies ran while one was open for 2% of the time, Pallas kernels for 12%

profile of v1, /device:TPU:0, one launch (start us, length us, event | category | flops | bytes accessed | tf_op | source)
XLA Modules:
  0.0 34.5 jit_solution(10377458620456648554)
XLA Ops:
  0.0 0.5 %collective-permute-start.2 = (bf16[4,512,128]{2,1,0:T(8,128)(2,1)}, bf16[4,512,128]{2,1,0:T(8,128)(2,1)S(1)}, u32[]{:S(2)}, u32[]{:S(2)}) collective-permute-start(bf16[4,512,128]{2,1,0:T(8,128)(2,1)} %bitcast.9), channel_id=1, source_target_pairs={{1,0},{9,1},{3,2},{11,3},{5,4},{13,5},{7,6},{15,7},{0,8},{8,9},{2,... | collective-permute-start | bytes 1572872 | tf_op jit(solution)/shard_map/ppermute | solution.py:50
  0.5 4.6 %collective-permute-start.4 = (bf16[4,512,128]{2,1,0:T(8,128)(2,1)}, bf16[4,512,128]{2,1,0:T(8,128)(2,1)S(1)}, u32[]{:S(2)}, u32[]{:S(2)}) collective-permute-start(bf16[4,512,128]{2,1,0:T(8,128)(2,1)} %bitcast.10), channel_id=1, source_target_pairs={{2,0},{17,1},{4,2},{19,3},{6,4},{21,5},{0,6},{23,7},{24,8},{15,9},... | collective-permute-start | bytes 1572872 | tf_op jit(solution)/shard_map/ppermute | solution.py:50
  5.1 1.5 %collective-permute-start = (bf16[4,512,128]{2,1,0:T(8,128)(2,1)}, bf16[4,512,128]{2,1,0:T(8,128)(2,1)S(1)}, u32[]{:S(2)}, u32[]{:S(2)}) collective-permute-start(bf16[4,512,128]{2,1,0:T(8,128)(2,1)} %bitcast.11), channel_id=1, source_target_pairs={{16,0},{3,1},{18,2},{5,3},{20,4},{7,5},{22,6},{1,7},{14,8},{25,9},... | collective-permute-start | bytes 1572872 | tf_op jit(solution)/shard_map/ppermute | solution.py:50
  6.6 0.7 %copy.9 = s32[1,1,4,3,12]{4,3,2,1,0:T(4,128)S(1)} copy(s32[1,1,4,3,12]{4,2,3,1,0:T(4,128)} %param.10) | data formatting | bytes 1152 | tf_op args[4]
  7.3 0.0 copy-start.2
  7.3 0.0 copy-start.3
  7.3 0.7 %copy-done.2 = f32[256]{0:T(256)S(1)} copy-done((f32[256]{0:T(256)S(1)}, f32[256]{0:T(256)}, u32[]{:S(2)}) %copy-start.2) | copy-done | bytes 1048
  7.9 0.0 copy-done.3
  7.9 0.0 copy-start
  8.0 1.0 %copy-done = bf16[1,1,4,512,128]{4,3,2,1,0:T(8,128)(2,1)S(1)} copy-done((bf16[1,1,4,512,128]{4,3,2,1,0:T(8,128)(2,1)S(1)}, bf16[1,1,4,512,128]{4,3,2,1,0:T(8,128)(2,1)}, u32[]{:S(2)}) %copy-start) | copy-done | bytes 524312
  9.0 0.0 copy-start.1
  9.0 0.9 %copy-done.1 = bf16[1,1,4,128,128]{4,3,2,1,0:T(8,128)(2,1)S(1)} copy-done((bf16[1,1,4,128,128]{4,3,2,1,0:T(8,128)(2,1)S(1)}, bf16[1,1,4,128,128]{4,3,2,1,0:T(8,128)(2,1)}, u32[]{:S(2)}) %copy-start.1) | copy-done | bytes 131096
  9.9 1.0 %prep.1 = (bf16[528,128]{1,0:T(8,128)(2,1)S(1)}, bf16[512,512]{1,0:T(8,128)(2,1)S(1)}) custom-call(s32[4,3,12]{2,1,0:T(4,128)S(1)} %bitcast.14, s32[4]{0:T(128)S(1)} %bitcast.15, f32[256]{0:T(256)S(1)} %copy-done.2, bf16[4,512,128]{2,1,0:T(8,128)(2,1)S(1)} %bitcast.12, bf16[4,128,128]{2,1,0:T(8,128)(2,1)S(1)} %bitcast.13), custom_call_target="tpu_custom_call" | custom-call | tf_op jit(solution)/shard_map/prep/pallas_call | solution.py:218
  10.9 0.0 copy-start.4
  10.9 0.0 collective-permute-start.3
  10.9 0.8 %collective-permute-start.5 = (bf16[528,128]{1,0:T(8,128)(2,1)S(1)}, bf16[528,128]{1,0:T(8,128)(2,1)S(1)}, u32[]{:S(2)}, u32[]{:S(2)}) collective-permute-start(bf16[528,128]{1,0:T(8,128)(2,1)S(1)} %get-tuple-element.13.own_sent), channel_id=1, source_target_pairs={{2,0},{17,1},{4,2},{19,3},{6,4},{21,5},{0,6},{23,7},{24,8},{15,9},... | collective-permute-start | bytes 405512 | tf_op jit(solution)/shard_map/ppermute | solution.py:50
  11.7 4.2 %collective-permute-done.3.p_sent = bf16[528,128]{1,0:T(8,128)(2,1)S(1)} collective-permute-done((bf16[528,128]{1,0:T(8,128)(2,1)S(1)}, bf16[528,128]{1,0:T(8,128)(2,1)S(1)}, u32[]{:S(2)}, u32[]{:S(2)}) %collective-permute-start.3) | collective-permute-done | bytes 135200 | tf_op jit(solution)/shard_map/ppermute | solution.py:50
  15.9 0.5 %collective-permute-start.1 = (bf16[528,128]{1,0:T(8,128)(2,1)S(1)}, bf16[528,128]{1,0:T(8,128)(2,1)S(1)}, u32[]{:S(2)}, u32[]{:S(2)}) collective-permute-start(bf16[528,128]{1,0:T(8,128)(2,1)S(1)} %get-tuple-element.13.own_sent), channel_id=1, source_target_pairs={{16,0},{3,1},{18,2},{5,3},{20,4},{7,5},{22,6},{1,7},{14,8},{25,9},... | collective-permute-start | bytes 405512 | tf_op jit(solution)/shard_map/ppermute | solution.py:50
  16.5 3.3 %collective-permute-done.5.h_sent = bf16[528,128]{1,0:T(8,128)(2,1)S(1)} collective-permute-done((bf16[528,128]{1,0:T(8,128)(2,1)S(1)}, bf16[528,128]{1,0:T(8,128)(2,1)S(1)}, u32[]{:S(2)}, u32[]{:S(2)}) %collective-permute-start.5) | collective-permute-done | bytes 135200 | tf_op jit(solution)/shard_map/ppermute | solution.py:50
  19.8 0.0 collective-permute-done.2.p_basis
  19.8 0.0 collective-permute-done.4.h_basis
  19.8 0.0 copy-done.4
  19.8 3.1 %heavy.1 = (f32[4,128,128]{2,1,0:T(8,128)S(1)}, bf16[4,128,128]{2,1,0:T(8,128)(2,1)S(1)}, bf16[4,128,128]{2,1,0:T(8,128)(2,1)S(1)}) custom-call(bf16[512,512]{1,0:T(8,128)(2,1)S(1)} %get-tuple-element.12.turned, bf16[528,128]{1,0:T(8,128)(2,1)S(1)} %get-tuple-element.13.own_sent, bf16[4,512,128]{2,1,0:T(8,128)(2,1)S(1)} %collective-permute-done.2.p_basis, ...), custom_call_target="tpu_custom_call" | custom-call | flops 1610612736 | bytes 1572864 | tf_op jit(solution)/shard_map/heavy/pallas_call | solution.py:233
  22.9 0.0 collective-permute-done.1.l_sent
  22.9 0.0 collective-permute-done.l_basis
  22.9 1.1 %light.1 = (f32[4,128,128]{2,1,0:T(8,128)S(1)}, bf16[4,128,128]{2,1,0:T(8,128)(2,1)S(1)}) custom-call(bf16[512,512]{1,0:T(8,128)(2,1)S(1)} %get-tuple-element.12.turned, bf16[528,128]{1,0:T(8,128)(2,1)S(1)} %get-tuple-element.13.own_sent, bf16[4,512,128]{2,1,0:T(8,128)(2,1)S(1)} %collective-permute-done.l_basis, ...), custom_call_target="tpu_custom_call" | custom-call | flops 536870912 | bytes 524288 | tf_op jit(solution)/shard_map/light/pallas_call | solution.py:248
  24.1 0.6 %collective-permute-start.8 = (bf16[4,128,128]{2,1,0:T(8,128)(2,1)S(1)}, bf16[4,128,128]{2,1,0:T(8,128)(2,1)S(1)}, u32[]{:S(2)}, u32[]{:S(2)}) collective-permute-start(bf16[4,128,128]{2,1,0:T(8,128)(2,1)S(1)} %get-tuple-element.18), channel_id=1, source_target_pairs={{0,16},{1,3},{2,18},{3,5},{4,20},{5,7},{6,22},{7,1},{8,14},{9,25},... | collective-permute-start | bytes 393224 | tf_op jit(solution)/shard_map/ppermute | solution.py:50
  24.7 2.3 %collective-permute-start.6 = (bf16[4,128,128]{2,1,0:T(8,128)(2,1)S(1)}, bf16[4,128,128]{2,1,0:T(8,128)(2,1)S(1)}, u32[]{:S(2)}, u32[]{:S(2)}) collective-permute-start(bf16[4,128,128]{2,1,0:T(8,128)(2,1)S(1)} %get-tuple-element.16), channel_id=1, source_target_pairs={{0,1},{1,9},{2,3},{3,11},{4,5},{5,13},{6,7},{7,15},{8,0},{9,8},{10... | collective-permute-start | bytes 393224 | tf_op jit(solution)/shard_map/ppermute | solution.py:50
  27.0 1.6 %collective-permute-start.7 = (bf16[4,128,128]{2,1,0:T(8,128)(2,1)S(1)}, bf16[4,128,128]{2,1,0:T(8,128)(2,1)S(1)}, u32[]{:S(2)}, u32[]{:S(2)}) collective-permute-start(bf16[4,128,128]{2,1,0:T(8,128)(2,1)S(1)} %get-tuple-element.17), channel_id=1, source_target_pairs={{0,2},{1,17},{2,4},{3,19},{4,6},{5,21},{6,0},{7,23},{8,24},{9,15},... | collective-permute-start | bytes 393224 | tf_op jit(solution)/shard_map/ppermute | solution.py:50
  28.6 0.5 %collective-permute-done.8 = bf16[4,128,128]{2,1,0:T(8,128)(2,1)S(1)} collective-permute-done((bf16[4,128,128]{2,1,0:T(8,128)(2,1)S(1)}, bf16[4,128,128]{2,1,0:T(8,128)(2,1)S(1)}, u32[]{:S(2)}, u32[]{:S(2)}) %collective-permute-start.8) | collective-permute-done | bytes 131104 | tf_op jit(solution)/shard_map/ppermute | solution.py:50
  29.1 0.4 %collective-permute-done.6 = bf16[4,128,128]{2,1,0:T(8,128)(2,1)S(1)} collective-permute-done((bf16[4,128,128]{2,1,0:T(8,128)(2,1)S(1)}, bf16[4,128,128]{2,1,0:T(8,128)(2,1)S(1)}, u32[]{:S(2)}, u32[]{:S(2)}) %collective-permute-start.6) | collective-permute-done | bytes 131104 | tf_op jit(solution)/shard_map/ppermute | solution.py:50
  29.5 4.2 %collective-permute-done.7 = bf16[4,128,128]{2,1,0:T(8,128)(2,1)S(1)} collective-permute-done((bf16[4,128,128]{2,1,0:T(8,128)(2,1)S(1)}, bf16[4,128,128]{2,1,0:T(8,128)(2,1)S(1)}, u32[]{:S(2)}, u32[]{:S(2)}) %collective-permute-start.7) | collective-permute-done | bytes 131104 | tf_op jit(solution)/shard_map/ppermute | solution.py:50
  33.8 0.8 %add_bitcast_fusion = f32[1,1,4,128,128]{4,3,2,1,0:T(8,128)} fusion(bf16[4,128,128]{2,1,0:T(8,128)(2,1)S(1)} %collective-permute-done.8, bf16[4,128,128]{2,1,0:T(8,128)(2,1)S(1)} %collective-permute-done.7, f32[4,128,128]{2,1,0:T(8,128)S(1)} %get-tuple-element.15, bf16[4,128,128]{2,1,0:T(8,128)(2,1)S(1)} %collective-permute-done.6), kind=kLoop, calls=%fused_computation | loop fusion | flops 393216 | bytes 917504 | tf_op jit(solution)/shard_map/broadcast_in_dim | solution.py:261
Async XLA Ops:
  0.0 19.8 %collective-permute-start.2 = (bf16[4,512,128]{2,1,0:T(8,128)(2,1)}, bf16[4,512,128]{2,1,0:T(8,128)(2,1)S(1)}, u32[]{:S(2)}, u32[]{:S(2)}) collective-permute-start(bf16[4,512,128]{2,1,0:T(8,128)(2,1)} %bitcast.9), channel_id=1, source_target_pairs={{1,0},{9,1},{3,2},{11,3},{5,4},{13,5},{7,6},{15,7},{0,8},{8,9},{2,... | collective-permute-start | bytes 1572872 | tf_op jit(solution)/shard_map/ppermute | solution.py:50
  0.5 19.3 %collective-permute-start.4 = (bf16[4,512,128]{2,1,0:T(8,128)(2,1)}, bf16[4,512,128]{2,1,0:T(8,128)(2,1)S(1)}, u32[]{:S(2)}, u32[]{:S(2)}) collective-permute-start(bf16[4,512,128]{2,1,0:T(8,128)(2,1)} %bitcast.10), channel_id=1, source_target_pairs={{2,0},{17,1},{4,2},{19,3},{6,4},{21,5},{0,6},{23,7},{24,8},{15,9},... | collective-permute-start | bytes 1572872 | tf_op jit(solution)/shard_map/ppermute | solution.py:50
  5.1 17.9 %collective-permute-start = (bf16[4,512,128]{2,1,0:T(8,128)(2,1)}, bf16[4,512,128]{2,1,0:T(8,128)(2,1)S(1)}, u32[]{:S(2)}, u32[]{:S(2)}) collective-permute-start(bf16[4,512,128]{2,1,0:T(8,128)(2,1)} %bitcast.11), channel_id=1, source_target_pairs={{16,0},{3,1},{18,2},{5,3},{20,4},{7,5},{22,6},{1,7},{14,8},{25,9},... | collective-permute-start | bytes 1572872 | tf_op jit(solution)/shard_map/ppermute | solution.py:50
  7.3 0.7 %copy-start.2 = (f32[256]{0:T(256)S(1)}, f32[256]{0:T(256)}, u32[]{:S(2)}) copy-start(f32[256]{0:T(256)} %fock.1) | copy-start | bytes 3076
  7.3 0.7 %copy-start.3 = (s32[1,1,4]{2,1,0:T(1,128)S(1)}, s32[1,1,4]{2,1,0:T(1,128)}, u32[]{:S(2)}) copy-start(s32[1,1,4]{2,1,0:T(1,128)} %param.11) | copy-start | bytes 52
  7.9 1.0 %copy-start = (bf16[1,1,4,512,128]{4,3,2,1,0:T(8,128)(2,1)S(1)}, bf16[1,1,4,512,128]{4,3,2,1,0:T(8,128)(2,1)}, u32[]{:S(2)}) copy-start(bf16[1,1,4,512,128]{4,3,2,1,0:T(8,128)(2,1)} %param.6) | copy-start | bytes 1572868
  9.0 0.9 %copy-start.1 = (bf16[1,1,4,128,128]{4,3,2,1,0:T(8,128)(2,1)S(1)}, bf16[1,1,4,128,128]{4,3,2,1,0:T(8,128)(2,1)}, u32[]{:S(2)}) copy-start(bf16[1,1,4,128,128]{4,3,2,1,0:T(8,128)(2,1)} %param.7) | copy-start | bytes 393220
  10.9 8.9 %copy-start.4 = (f32[1,1,4,128]{3,2,1,0:T(4,128)S(1)}, f32[1,1,4,128]{3,2,1,0:T(4,128)}, u32[]{:S(2)}) copy-start(f32[1,1,4,128]{3,2,1,0:T(4,128)} %param.8) | copy-start | bytes 6148
  10.9 5.0 %collective-permute-start.3 = (bf16[528,128]{1,0:T(8,128)(2,1)S(1)}, bf16[528,128]{1,0:T(8,128)(2,1)S(1)}, u32[]{:S(2)}, u32[]{:S(2)}) collective-permute-start(bf16[528,128]{1,0:T(8,128)(2,1)S(1)} %get-tuple-element.13.own_sent), channel_id=1, source_target_pairs={{1,0},{9,1},{3,2},{11,3},{5,4},{13,5},{7,6},{15,7},{0,8},{8,9},{2,... | collective-permute-start | bytes 405512 | tf_op jit(solution)/shard_map/ppermute | solution.py:50
  10.9 8.9 %collective-permute-start.5 = (bf16[528,128]{1,0:T(8,128)(2,1)S(1)}, bf16[528,128]{1,0:T(8,128)(2,1)S(1)}, u32[]{:S(2)}, u32[]{:S(2)}) collective-permute-start(bf16[528,128]{1,0:T(8,128)(2,1)S(1)} %get-tuple-element.13.own_sent), channel_id=1, source_target_pairs={{2,0},{17,1},{4,2},{19,3},{6,4},{21,5},{0,6},{23,7},{24,8},{15,9},... | collective-permute-start | bytes 405512 | tf_op jit(solution)/shard_map/ppermute | solution.py:50
  15.9 7.0 %collective-permute-start.1 = (bf16[528,128]{1,0:T(8,128)(2,1)S(1)}, bf16[528,128]{1,0:T(8,128)(2,1)S(1)}, u32[]{:S(2)}, u32[]{:S(2)}) collective-permute-start(bf16[528,128]{1,0:T(8,128)(2,1)S(1)} %get-tuple-element.13.own_sent), channel_id=1, source_target_pairs={{16,0},{3,1},{18,2},{5,3},{20,4},{7,5},{22,6},{1,7},{14,8},{25,9},... | collective-permute-start | bytes 405512 | tf_op jit(solution)/shard_map/ppermute | solution.py:50
  24.1 5.0 %collective-permute-start.8 = (bf16[4,128,128]{2,1,0:T(8,128)(2,1)S(1)}, bf16[4,128,128]{2,1,0:T(8,128)(2,1)S(1)}, u32[]{:S(2)}, u32[]{:S(2)}) collective-permute-start(bf16[4,128,128]{2,1,0:T(8,128)(2,1)S(1)} %get-tuple-element.18), channel_id=1, source_target_pairs={{0,16},{1,3},{2,18},{3,5},{4,20},{5,7},{6,22},{7,1},{8,14},{9,25},... | collective-permute-start | bytes 393224 | tf_op jit(solution)/shard_map/ppermute | solution.py:50
  24.7 4.8 %collective-permute-start.6 = (bf16[4,128,128]{2,1,0:T(8,128)(2,1)S(1)}, bf16[4,128,128]{2,1,0:T(8,128)(2,1)S(1)}, u32[]{:S(2)}, u32[]{:S(2)}) collective-permute-start(bf16[4,128,128]{2,1,0:T(8,128)(2,1)S(1)} %get-tuple-element.16), channel_id=1, source_target_pairs={{0,1},{1,9},{2,3},{3,11},{4,5},{5,13},{6,7},{7,15},{8,0},{9,8},{10... | collective-permute-start | bytes 393224 | tf_op jit(solution)/shard_map/ppermute | solution.py:50
  27.0 6.8 %collective-permute-start.7 = (bf16[4,128,128]{2,1,0:T(8,128)(2,1)S(1)}, bf16[4,128,128]{2,1,0:T(8,128)(2,1)S(1)}, u32[]{:S(2)}, u32[]{:S(2)}) collective-permute-start(bf16[4,128,128]{2,1,0:T(8,128)(2,1)S(1)} %get-tuple-element.17), channel_id=1, source_target_pairs={{0,2},{1,17},{2,4},{3,19},{4,6},{5,21},{6,0},{7,23},{8,24},{9,15},... | collective-permute-start | bytes 393224 | tf_op jit(solution)/shard_map/ppermute | solution.py:50

commit v2 on v1

--- a/solution.py
+++ b/solution.py
@@ -6,6 +6,7 @@
 from jax.experimental import pallas as pl
 from jax.experimental.pallas import tpu as pltpu
 from jax.sharding import PartitionSpec as P
+
 
 F32, BF16, I32 = jnp.float32, jnp.bfloat16, jnp.int32
 AXES = ("iblk", "jblk")
@@ -46,10 +47,6 @@
     return made
 
 
-def moved(block, route):
-    return lax.ppermute(block, AXES, route)
-
-
 def back(route):
     return [(b, a) for a, b in route]
 
@@ -69,15 +66,26 @@
     )
 
 
-def prep_kernel(reach, plan, counts, fock, basis, amps, sent, turned):
-    pairs, _, width = amps.shape
-    steps, _, slots = plan.shape
+def prep_kernel(reach, plan_hbm, counts_hbm, fock_hbm, amps_hbm, sent, plan, counts, fock, sems):
+    pairs, width, _ = amps_hbm.shape
+    copies = [
+        pltpu.make_async_copy(src, dst, sems.at[k])
+        for k, (src, dst) in enumerate(
+            [(plan_hbm, plan), (counts_hbm, counts), (fock_hbm, fock)]
+            + [(amps_hbm.at[p], sent.at[pl.ds(p * width, width)]) for p in range(pairs)]
+        )
+    ]
+    for copy in copies:
+        copy.start()
+    _, steps, slots = plan.shape
     i, j = lax.axis_index(AXES[0]) % 2, lax.axis_index(AXES[1]) % 2
     forward = (1 - j, i)
     i_heavy = (i + j) % 2
     lane = lax.broadcasted_iota(I32, (META, LANES), 1)
     row = lax.broadcasted_iota(I32, (META, LANES), 0)
     table = jnp.zeros((META, LANES), F32)
+    for copy in copies[:3]:
+        copy.wait()
     for t in range(steps):
         axis, far = t // reach, t % reach
         heavy = i_heavy if axis == 0 else 1 - i_heavy
@@ -94,9 +102,9 @@
         live = counts[t]
 
         def place(c, weight):
-            p, q = plan[t, 0, c], plan[t, 1, c]
+            p, q = plan[0, t, c], plan[1, t, c]
             at = base + jnp.where(ahead == 1, p * pairs + q, q * pairs + p)
-            value = jnp.where(c < live, fock[plan[t, 2, c]], jnp.float32(0.0))
+            value = jnp.where(c < live, fock[plan[2, t, c]], jnp.float32(0.0))
             return jnp.where(lane == at, value, weight)
 
         weight = lax.fori_loop(0, slots, place, jnp.zeros((META, LANES), F32), unroll=True)
@@ -105,10 +113,9 @@
         middle = rest.astype(BF16).astype(F32)
         for part, piece in enumerate((high, middle, rest - middle)):
             table = jnp.where(row == part * ROLES + role, piece + table, table)
-    sent[pl.ds(0, pairs * width), :] = amps[...].reshape(pairs * width, width)
     sent[pl.ds(pairs * width, META), :] = table.astype(BF16)
-    for p in range(pairs):
-        turned[pl.ds(p * width, width), :] = basis[p].T
+    for copy in copies[3:]:
+        copy.wait()
 
 
 def weight_rows(blocks, slot, pairs):
@@ -170,39 +177,56 @@
     return own, other
 
 
-def amps_of(ref, pairs, width):
-    return [ref[pl.ds(p * width, width), :] for p in range(pairs)]
+def amps_of(ref, pairs, width, first=0):
+    return [ref[pl.ds(first + p * width, width), :] for p in range(pairs)]
+
+
+def turn_kernel(basis, turned):
+    pairs, _, width = basis.shape
+    for p in range(pairs):
+        turned[pl.ds(p * width, width), :] = basis[p].T
+
+
+def near_kernel(own_turned, own_sent, p_basis, p_sent, energy, p_turned, total, p_sum):
+    pairs, _, width = p_basis.shape
+    own_a, p_a = (amps_of(r, pairs, width) for r in (own_sent, p_sent))
+    meta = pl.ds(pairs * width, META)
+    tables = ((own_sent[meta, :], OWN), (p_sent[meta, :], PARTNER))
+    p_b = [p_basis[p] for p in range(pairs)]
+    for p in range(pairs):
+        p_turned[pl.ds(p * width, width), :] = p_b[p].T
+    x, y = couple(own_turned[...], own_a, p_b, p_a, weight_rows(tables, OP, pairs), width)
+    for p in range(pairs):
+        across = jnp.broadcast_to(energy[pl.ds(p, 1), :], (width, width))
+        total[p] = (across.T + across) * own_a[p].astype(F32) + x[p]
+        p_sum[p] = y[p]
 
 
 def heavy_kernel(
-    turned, own_sent, p_basis, p_sent, h_basis, h_sent, energy, total, p_back, h_back
+    own_turned, p_turned, own_sent, p_sent, h_basis, h_sent, total_in, p_sum,
+    total, p_back, h_back,
 ):
-    pairs, depth, width = p_basis.shape
+    pairs, _, width = h_basis.shape
     own_a, p_a, h_a = (amps_of(r, pairs, width) for r in (own_sent, p_sent, h_sent))
     meta = pl.ds(pairs * width, META)
     tables = ((own_sent[meta, :], OWN), (p_sent[meta, :], PARTNER), (h_sent[meta, :], HEAVY))
-    p_b = [p_basis[p] for p in range(pairs)]
     h_b = [h_basis[p] for p in range(pairs)]
-    own_t = turned[...]
-    x1, y1 = couple(own_t, own_a, p_b, p_a, weight_rows(tables, OP, pairs), width)
-    x2, y2 = couple(own_t, own_a, h_b, h_a, weight_rows(tables, OH, pairs), width)
-    p_t = jnp.concatenate([b.T for b in p_b], 0)
-    x3, y3 = couple(p_t, p_a, h_b, h_a, weight_rows(tables, PH, pairs), width)
-    for p in range(pairs):
-        across = jnp.broadcast_to(energy[pl.ds(p, 1), :], (width, width))
-        diagonal = (across.T + across) * own_a[p].astype(F32)
-        total[p] = diagonal + (x1[p] + x2[p])
-        p_back[p] = (y1[p] + x3[p]).astype(BF16)
-        h_back[p] = (y2[p] + y3[p]).astype(BF16)
-
-
-def light_kernel(turned, own_sent, l_basis, l_sent, total_in, total, l_back):
-    pairs, depth, width = l_basis.shape
+    weight = weight_rows(tables, OH, pairs) + weight_rows(tables, PH, pairs)
+    turned = jnp.concatenate([own_turned[...], p_turned[...]], 0)
+    x, y = couple(turned, own_a + p_a, h_b, h_a, weight, width)
+    for p in range(pairs):
+        total[p] = total_in[p] + x[p]
+        p_back[p] = (p_sum[p] + x[pairs + p]).astype(BF16)
+        h_back[p] = y[p].astype(BF16)
+
+
+def light_kernel(own_turned, own_sent, l_basis, l_sent, total_in, total, l_back):
+    pairs, _, width = l_basis.shape
     own_a, l_a = (amps_of(r, pairs, width) for r in (own_sent, l_sent))
     meta = pl.ds(pairs * width, META)
     tables = ((own_sent[meta, :], OWN), (l_sent[meta, :], LIGHT))
     l_b = [l_basis[p] for p in range(pairs)]
-    x, y = couple(turned[...], own_a, l_b, l_a, weight_rows(tables, OL, pairs), width)
+    x, y = couple(own_turned[...], own_a, l_b, l_a, weight_rows(tables, OL, pairs), width)
     for p in range(pairs):
         total[p] = total_in[p] + x[p]
         l_back[p] = y[p].astype(BF16)
@@ -211,52 +235,63 @@
 def on_device(all_routes, reach, pno_basis, amplitudes, pno_energy, fock_values, couplings, counts):
     to_p, to_h, to_l = all_routes
     basis, amps, energy = pno_basis[0, 0], amplitudes[0, 0], pno_energy[0, 0]
+    plan, live = couplings[0, 0].transpose(1, 0, 2), counts[0, 0]
     pairs, depth, width = basis.shape
-    vmem, smem = pl.BlockSpec(memory_space=pltpu.VMEM), pl.BlockSpec(memory_space=pltpu.SMEM)
+    vmem, hbm = pl.BlockSpec(memory_space=pltpu.VMEM), pl.BlockSpec(memory_space=pl.ANY)
     params = pltpu.CompilerParams(vmem_limit_bytes=48 * 1024 * 1024)
     square = (pairs, width, width)
-    sent, turned = pl.pallas_call(
+    wide = jax.ShapeDtypeStruct(square, F32)
+    narrow = jax.ShapeDtypeStruct(square, BF16)
+
+    def moved(block, route):
+        return lax.ppermute(block, AXES, route)
+
+    def kernel(body, terms, shapes, *operands):
+        flops = 2 * pairs * pairs * (width * width * depth + 4 * width**3)
+        return pl.pallas_call(
+            body,
+            out_shape=shapes,
+            in_specs=[vmem] * len(operands),
+            out_specs=(vmem,) * len(shapes),
+            compiler_params=params,
+            cost_estimate=pl.CostEstimate(
+                flops=terms * flops, bytes_accessed=2 * basis.size, transcendentals=0
+            ),
+        )(*operands)
+
+    h_basis = moved(basis, to_h)
+    p_basis = moved(basis, to_p)
+    sent = pl.pallas_call(
         functools.partial(prep_kernel, reach),
-        out_shape=(
-            jax.ShapeDtypeStruct((pairs * width + META, width), BF16),
-            jax.ShapeDtypeStruct((pairs * width, depth), BF16),
-        ),
-        in_specs=[smem, smem, smem, vmem, vmem],
-        out_specs=(vmem, vmem),
+        out_shape=jax.ShapeDtypeStruct((pairs * width + META, width), BF16),
+        in_specs=[hbm] * 4,
+        out_specs=vmem,
+        scratch_shapes=[
+            pltpu.SMEM(plan.shape, I32),
+            pltpu.SMEM(live.shape, I32),
+            pltpu.SMEM(fock_values.shape, F32),
+            pltpu.SemaphoreType.DMA((3 + pairs,)),
+        ],
         compiler_params=params,
         name="prep",
-    )(couplings[0, 0], counts[0, 0], fock_values, basis, amps)
-    h_basis, p_basis = moved(basis, to_h), moved(basis, to_p)
-    h_sent, p_sent = moved(sent, to_h), moved(sent, to_p)
-    l_basis, l_sent = moved(basis, to_l), moved(sent, to_l)
-    flops = 2 * pairs * pairs * (width * width * depth + 4 * width**3)
-    total, p_back, h_back = pl.pallas_call(
+    )(*(pltpu.with_memory_space_constraint(x, pltpu.HBM) for x in (plan, live, fock_values, amps)))
+    h_sent = moved(sent, to_h)
+    p_sent = moved(sent, to_p)
+    l_basis = moved(basis, to_l)
+    l_sent = moved(sent, to_l)
+    flat = jax.ShapeDtypeStruct((pairs * width, depth), BF16)
+    (turned,) = kernel(turn_kernel, 0, (flat,), basis)
+    p_turned, total, p_sum = kernel(
+        near_kernel, 1, (flat, wide, wide), *(turned, sent, p_basis, p_sent, energy)
+    )
+    total, p_back, h_back = kernel(
         heavy_kernel,
-        out_shape=(
-            jax.ShapeDtypeStruct(square, F32),
-            jax.ShapeDtypeStruct(square, BF16),
-            jax.ShapeDtypeStruct(square, BF16),
-        ),
-        in_specs=[vmem] * 7,
-        out_specs=(vmem,) * 3,
-        compiler_params=params,
-        cost_estimate=pl.CostEstimate(
-            flops=3 * flops, bytes_accessed=3 * basis.size * 2, transcendentals=0
-        ),
-        name="heavy",
-    )(turned, sent, p_basis, p_sent, h_basis, h_sent, energy)
-    total, l_back = pl.pallas_call(
-        light_kernel,
-        out_shape=(jax.ShapeDtypeStruct(square, F32), jax.ShapeDtypeStruct(square, BF16)),
-        in_specs=[vmem] * 5,
-        out_specs=(vmem,) * 2,
-        compiler_params=params,
-        cost_estimate=pl.CostEstimate(
-            flops=flops, bytes_accessed=basis.size * 2, transcendentals=0
-        ),
-        name="light",
-    )(turned, sent, l_basis, l_sent, total)
-    for piece, route in ((p_back, to_p), (h_back, to_h), (l_back, to_l)):
+        2,
+        (wide, narrow, narrow),
+        *(turned, p_turned, sent, p_sent, h_basis, h_sent, total, p_sum),
+    )
+    total, l_back = kernel(light_kernel, 1, (wide, narrow), turned, sent, l_basis, l_sent, total)
+    for piece, route in ((h_back, to_h), (p_back, to_p), (l_back, to_l)):
         total = total + moved(piece, back(route)).astype(F32)
     return total[None, None]
 
@@ -272,8 +307,12 @@
         P("iblk", "jblk", None, None, None),
         P("iblk", "jblk", None),
     )
+
+    def body(*arguments):
+        return on_device(routes(ni, nj), 2, *arguments)
+
     return jax.shard_map(
-        functools.partial(on_device, routes(ni, nj), 2),
+        body,
         mesh=mesh,
         in_specs=placed,
         out_specs=P("iblk", "jblk", None, None, None),

time: 34.8 us -> 32.2 us (0.925)
  local copies, waits for them, and re-layouts: 3.33 us -> 1.04 us
  waiting for transfers between devices: 12.8 us -> 11.4 us
  Pallas kernels: 5.23 us -> 6.02 us
    unnamed x11 -> x4, local copies, waits for them, and re-layouts: 3.33 us -> 1.04 us
    ppermute x9, waiting for transfers between devices: 12.8 us -> 11.4 us  [moved(): return lax.ppermute(block, AXES, route)]
    pallas_call x3 -> x5, Pallas kernels: 5.23 us -> 6.02 us  [the longest x4 4.75 us: kernel(): pl.pallas_call(body, out_shape=shapes, in_specs=[vmem] * len(operands), o...]
  transfers between devices with their start and end apart: 9 -> 9, of which waited for: 5 -> 4; matrix products, arithmetic and copies ran while one was open for 2% -> 0% of each run, Pallas kernels for 12% -> 15%
where the time goes in v2:
time: 32.2 us; the launch traced here: 31.9 us
  starting transfers between devices  12.7 us (39%)
  waiting for transfers between devices  11.4 us (35%)
  Pallas kernels  6.02 us (19%)
  local copies, waits for them, and re-layouts  1.04 us (3%)
  other arithmetic  0.76 us (2%)
    ppermute x9, starting transfers between devices, moved(): return lax.ppermute(block, AXES, route)  12.7 us
    ppermute x9, waiting for transfers between devices, moved(): return lax.ppermute(block, AXES, route)  11.4 us
    pallas_call x4, Pallas kernels, kernel(): pl.pallas_call(body, out_shape=shapes, in_specs=[vmem] * len(operands), o...  4.75 us
    pallas_call x1, Pallas kernels, on_device(): pl.pallas_call(functools.partial(prep_kernel, reach), out_shape=jax.Shape...  1.28 us
    unnamed x4, local copies, waits for them, and re-layouts  1.04 us
    broadcast_in_dim x1, other arithmetic, on_device(): return total[None, None]  0.76 us
  transfers between devices with their start and end apart: 9, of which 4 were waited for; matrix products, arithmetic and copies ran while one was open for 0% of the time, Pallas kernels for 15%

profile of v2, /device:TPU:0, one launch (start us, length us, event | category | flops | bytes accessed | tf_op | source)
XLA Modules:
  0.0 31.9 jit_solution(11828888295492787675)
XLA Ops:
  0.0 0.5 %collective-permute-start.2 = (bf16[4,512,128]{2,1,0:T(8,128)(2,1)}, bf16[4,512,128]{2,1,0:T(8,128)(2,1)S(1)}, u32[]{:S(2)}, u32[]{:S(2)}) collective-permute-start(bf16[4,512,128]{2,1,0:T(8,128)(2,1)} %bitcast.9), channel_id=1, source_target_pairs={{1,0},{9,1},{3,2},{11,3},{5,4},{13,5},{7,6},{15,7},{0,8},{8,9},{2,... | collective-permute-start | bytes 1572872 | tf_op jit(solution)/shard_map/ppermute | solution.py:247
  0.5 4.6 %collective-permute-start.4 = (bf16[4,512,128]{2,1,0:T(8,128)(2,1)}, bf16[4,512,128]{2,1,0:T(8,128)(2,1)S(1)}, u32[]{:S(2)}, u32[]{:S(2)}) collective-permute-start(bf16[4,512,128]{2,1,0:T(8,128)(2,1)} %bitcast.10), channel_id=1, source_target_pairs={{2,0},{17,1},{4,2},{19,3},{6,4},{21,5},{0,6},{23,7},{24,8},{15,9},... | collective-permute-start | bytes 1572872 | tf_op jit(solution)/shard_map/ppermute | solution.py:247
  5.1 1.5 %collective-permute-start = (bf16[4,512,128]{2,1,0:T(8,128)(2,1)}, bf16[4,512,128]{2,1,0:T(8,128)(2,1)S(1)}, u32[]{:S(2)}, u32[]{:S(2)}) collective-permute-start(bf16[4,512,128]{2,1,0:T(8,128)(2,1)} %bitcast.11), channel_id=1, source_target_pairs={{16,0},{3,1},{18,2},{5,3},{20,4},{7,5},{22,6},{1,7},{14,8},{25,9},... | collective-permute-start | bytes 1572872 | tf_op jit(solution)/shard_map/ppermute | solution.py:247
  6.6 0.0 copy-start.1
  6.6 1.3 %prep.1.own_sent = bf16[528,128]{1,0:T(8,128)(2,1)S(1)} custom-call(s32[3,4,12]{2,1,0:T(4,128)} %bitcast.15, s32[4]{0:T(128)} %bitcast.16, f32[256]{0:T(256)} %fock_hbm.1, bf16[4,128,128]{2,1,0:T(8,128)(2,1)} %bitcast.14), custom_call_target="tpu_custom_call" | custom-call | tf_op jit(solution)/shard_map/prep/pallas_call | solution.py:264
  7.9 0.0 collective-permute-start.3
  7.9 0.8 %collective-permute-start.5 = (bf16[528,128]{1,0:T(8,128)(2,1)S(1)}, bf16[528,128]{1,0:T(8,128)(2,1)S(1)}, u32[]{:S(2)}, u32[]{:S(2)}) collective-permute-start(bf16[528,128]{1,0:T(8,128)(2,1)S(1)} %prep.1.own_sent), channel_id=1, source_target_pairs={{2,0},{17,1},{4,2},{19,3},{6,4},{21,5},{0,6},{23,7},{24,8},{15,9},... | collective-permute-start | bytes 405512 | tf_op jit(solution)/shard_map/ppermute | solution.py:247
  8.7 0.0 copy-start
  8.7 1.0 %copy-done = bf16[1,1,4,512,128]{4,3,2,1,0:T(8,128)(2,1)S(1)} copy-done((bf16[1,1,4,512,128]{4,3,2,1,0:T(8,128)(2,1)S(1)}, bf16[1,1,4,512,128]{4,3,2,1,0:T(8,128)(2,1)}, u32[]{:S(2)}) %copy-start) | copy-done | bytes 524312
  9.7 0.2 shard_map.64.own_turned
  9.9 3.0 %collective-permute-done.3.p_sent = bf16[528,128]{1,0:T(8,128)(2,1)S(1)} collective-permute-done((bf16[528,128]{1,0:T(8,128)(2,1)S(1)}, bf16[528,128]{1,0:T(8,128)(2,1)S(1)}, u32[]{:S(2)}, u32[]{:S(2)}) %collective-permute-start.3) | collective-permute-done | bytes 135200 | tf_op jit(solution)/shard_map/ppermute | solution.py:247
  12.9 0.9 %collective-permute-start.1 = (bf16[528,128]{1,0:T(8,128)(2,1)S(1)}, bf16[528,128]{1,0:T(8,128)(2,1)S(1)}, u32[]{:S(2)}, u32[]{:S(2)}) collective-permute-start(bf16[528,128]{1,0:T(8,128)(2,1)S(1)} %prep.1.own_sent), channel_id=1, source_target_pairs={{16,0},{3,1},{18,2},{5,3},{20,4},{7,5},{22,6},{1,7},{14,8},{25,9},... | collective-permute-start | bytes 405512 | tf_op jit(solution)/shard_map/ppermute | solution.py:247
  13.8 0.0 collective-permute-done.2.p_basis
  13.8 0.0 copy-done.1
  13.8 1.1 %shard_map.65 = (bf16[512,512]{1,0:T(8,128)(2,1)S(1)}, f32[4,128,128]{2,1,0:T(8,128)S(1)}, f32[4,128,128]{2,1,0:T(8,128)S(1)}) custom-call(bf16[512,512]{1,0:T(8,128)(2,1)S(1)} %shard_map.64.own_turned, bf16[528,128]{1,0:T(8,128)(2,1)S(1)} %prep.1.own_sent, bf16[4,512,128]{2,1,0:T(8,128)(2,1)S(1)} %collective-permute-done.2.p_basis, ...), custom_call_target="tpu_custom_call" | custom-call | flops 536870912 | bytes 524288 | tf_op jit(solution)/shard_map/pallas_call | solution.py:251
  15.0 4.8 %collective-permute-done.5.h_sent = bf16[528,128]{1,0:T(8,128)(2,1)S(1)} collective-permute-done((bf16[528,128]{1,0:T(8,128)(2,1)S(1)}, bf16[528,128]{1,0:T(8,128)(2,1)S(1)}, u32[]{:S(2)}, u32[]{:S(2)}) %collective-permute-start.5) | collective-permute-done | bytes 135200 | tf_op jit(solution)/shard_map/ppermute | solution.py:247
  19.8 0.0 collective-permute-done.4.h_basis
  19.8 2.3 %shard_map.66 = (f32[4,128,128]{2,1,0:T(8,128)S(1)}, bf16[4,128,128]{2,1,0:T(8,128)(2,1)S(1)}, bf16[4,128,128]{2,1,0:T(8,128)(2,1)S(1)}) custom-call(bf16[512,512]{1,0:T(8,128)(2,1)S(1)} %shard_map.64.own_turned, bf16[512,512]{1,0:T(8,128)(2,1)S(1)} %get-tuple-element.13.p_turned, bf16[528,128]{1,0:T(8,128)(2,1)S(1)} %prep.1.own_sent, ...), custom_call_target="tpu_custom_call" | custom-call | flops 1073741824 | bytes 524288 | tf_op jit(solution)/shard_map/pallas_call | solution.py:251
  22.1 0.0 collective-permute-done.1.l_sent
  22.1 0.0 collective-permute-done.l_basis
  22.1 1.1 %shard_map.67 = (f32[4,128,128]{2,1,0:T(8,128)S(1)}, bf16[4,128,128]{2,1,0:T(8,128)(2,1)S(1)}) custom-call(bf16[512,512]{1,0:T(8,128)(2,1)S(1)} %shard_map.64.own_turned, bf16[528,128]{1,0:T(8,128)(2,1)S(1)} %prep.1.own_sent, bf16[4,512,128]{2,1,0:T(8,128)(2,1)S(1)} %collective-permute-done.l_basis, bf16[528,128]{1,0:T(8,128)(2,1)S(1)} %collective-permute-done.1.l_sent, ...), custom_call_target="tpu_custom_call" | custom-call | flops 536870912 | bytes 524288 | tf_op jit(solution)/shard_map/pallas_call | solution.py:251
  23.3 0.6 %collective-permute-start.8 = (bf16[4,128,128]{2,1,0:T(8,128)(2,1)S(1)}, bf16[4,128,128]{2,1,0:T(8,128)(2,1)S(1)}, u32[]{:S(2)}, u32[]{:S(2)}) collective-permute-start(bf16[4,128,128]{2,1,0:T(8,128)(2,1)S(1)} %get-tuple-element.20), channel_id=1, source_target_pairs={{0,16},{1,3},{2,18},{3,5},{4,20},{5,7},{6,22},{7,1},{8,14},{9,25},... | collective-permute-start | bytes 393224 | tf_op jit(solution)/shard_map/ppermute | solution.py:247
  23.9 0.8 %collective-permute-start.6 = (bf16[4,128,128]{2,1,0:T(8,128)(2,1)S(1)}, bf16[4,128,128]{2,1,0:T(8,128)(2,1)S(1)}, u32[]{:S(2)}, u32[]{:S(2)}) collective-permute-start(bf16[4,128,128]{2,1,0:T(8,128)(2,1)S(1)} %get-tuple-element.18), channel_id=1, source_target_pairs={{0,2},{1,17},{2,4},{3,19},{4,6},{5,21},{6,0},{7,23},{8,24},{9,15},... | collective-permute-start | bytes 393224 | tf_op jit(solution)/shard_map/ppermute | solution.py:247
  24.7 2.9 %collective-permute-start.7 = (bf16[4,128,128]{2,1,0:T(8,128)(2,1)S(1)}, bf16[4,128,128]{2,1,0:T(8,128)(2,1)S(1)}, u32[]{:S(2)}, u32[]{:S(2)}) collective-permute-start(bf16[4,128,128]{2,1,0:T(8,128)(2,1)S(1)} %get-tuple-element.19), channel_id=1, source_target_pairs={{0,1},{1,9},{2,3},{3,11},{4,5},{5,13},{6,7},{7,15},{8,0},{9,8},{10... | collective-permute-start | bytes 393224 | tf_op jit(solution)/shard_map/ppermute | solution.py:247
  27.7 0.6 %collective-permute-done.8 = bf16[4,128,128]{2,1,0:T(8,128)(2,1)S(1)} collective-permute-done((bf16[4,128,128]{2,1,0:T(8,128)(2,1)S(1)}, bf16[4,128,128]{2,1,0:T(8,128)(2,1)S(1)}, u32[]{:S(2)}, u32[]{:S(2)}) %collective-permute-start.8) | collective-permute-done | bytes 131104 | tf_op jit(solution)/shard_map/ppermute | solution.py:247
  28.3 2.9 %collective-permute-done.6 = bf16[4,128,128]{2,1,0:T(8,128)(2,1)S(1)} collective-permute-done((bf16[4,128,128]{2,1,0:T(8,128)(2,1)S(1)}, bf16[4,128,128]{2,1,0:T(8,128)(2,1)S(1)}, u32[]{:S(2)}, u32[]{:S(2)}) %collective-permute-start.6) | collective-permute-done | bytes 131104 | tf_op jit(solution)/shard_map/ppermute | solution.py:247
  31.2 0.0 collective-permute-done.7
  31.2 0.8 %add_bitcast_fusion = f32[1,1,4,128,128]{4,3,2,1,0:T(8,128)} fusion(bf16[4,128,128]{2,1,0:T(8,128)(2,1)S(1)} %collective-permute-done.8, bf16[4,128,128]{2,1,0:T(8,128)(2,1)S(1)} %collective-permute-done.7, f32[4,128,128]{2,1,0:T(8,128)S(1)} %get-tuple-element.17, bf16[4,128,128]{2,1,0:T(8,128)(2,1)S(1)} %collective-permute-done.6), kind=kLoop, calls=%fused_computation | loop fusion | flops 393216 | bytes 917504 | tf_op jit(solution)/shard_map/broadcast_in_dim | solution.py:296
Async XLA Ops:
  0.0 13.8 %collective-permute-start.2 = (bf16[4,512,128]{2,1,0:T(8,128)(2,1)}, bf16[4,512,128]{2,1,0:T(8,128)(2,1)S(1)}, u32[]{:S(2)}, u32[]{:S(2)}) collective-permute-start(bf16[4,512,128]{2,1,0:T(8,128)(2,1)} %bitcast.9), channel_id=1, source_target_pairs={{1,0},{9,1},{3,2},{11,3},{5,4},{13,5},{7,6},{15,7},{0,8},{8,9},{2,... | collective-permute-start | bytes 1572872 | tf_op jit(solution)/shard_map/ppermute | solution.py:247
  0.5 19.3 %collective-permute-start.4 = (bf16[4,512,128]{2,1,0:T(8,128)(2,1)}, bf16[4,512,128]{2,1,0:T(8,128)(2,1)S(1)}, u32[]{:S(2)}, u32[]{:S(2)}) collective-permute-start(bf16[4,512,128]{2,1,0:T(8,128)(2,1)} %bitcast.10), channel_id=1, source_target_pairs={{2,0},{17,1},{4,2},{19,3},{6,4},{21,5},{0,6},{23,7},{24,8},{15,9},... | collective-permute-start | bytes 1572872 | tf_op jit(solution)/shard_map/ppermute | solution.py:247
  5.1 17.0 %collective-permute-start = (bf16[4,512,128]{2,1,0:T(8,128)(2,1)}, bf16[4,512,128]{2,1,0:T(8,128)(2,1)S(1)}, u32[]{:S(2)}, u32[]{:S(2)}) collective-permute-start(bf16[4,512,128]{2,1,0:T(8,128)(2,1)} %bitcast.11), channel_id=1, source_target_pairs={{16,0},{3,1},{18,2},{5,3},{20,4},{7,5},{22,6},{1,7},{14,8},{25,9},... | collective-permute-start | bytes 1572872 | tf_op jit(solution)/shard_map/ppermute | solution.py:247
  6.6 7.2 %copy-start.1 = (f32[1,1,4,128]{3,2,1,0:T(4,128)S(1)}, f32[1,1,4,128]{3,2,1,0:T(4,128)}, u32[]{:S(2)}) copy-start(f32[1,1,4,128]{3,2,1,0:T(4,128)} %param.8) | copy-start | bytes 6148
  7.9 5.0 %collective-permute-start.3 = (bf16[528,128]{1,0:T(8,128)(2,1)S(1)}, bf16[528,128]{1,0:T(8,128)(2,1)S(1)}, u32[]{:S(2)}, u32[]{:S(2)}) collective-permute-start(bf16[528,128]{1,0:T(8,128)(2,1)S(1)} %prep.1.own_sent), channel_id=1, source_target_pairs={{1,0},{9,1},{3,2},{11,3},{5,4},{13,5},{7,6},{15,7},{0,8},{8,9},{2,... | collective-permute-start | bytes 405512 | tf_op jit(solution)/shard_map/ppermute | solution.py:247
  7.9 11.9 %collective-permute-start.5 = (bf16[528,128]{1,0:T(8,128)(2,1)S(1)}, bf16[528,128]{1,0:T(8,128)(2,1)S(1)}, u32[]{:S(2)}, u32[]{:S(2)}) collective-permute-start(bf16[528,128]{1,0:T(8,128)(2,1)S(1)} %prep.1.own_sent), channel_id=1, source_target_pairs={{2,0},{17,1},{4,2},{19,3},{6,4},{21,5},{0,6},{23,7},{24,8},{15,9},... | collective-permute-start | bytes 405512 | tf_op jit(solution)/shard_map/ppermute | solution.py:247
  8.7 1.0 %copy-start = (bf16[1,1,4,512,128]{4,3,2,1,0:T(8,128)(2,1)S(1)}, bf16[1,1,4,512,128]{4,3,2,1,0:T(8,128)(2,1)}, u32[]{:S(2)}) copy-start(bf16[1,1,4,512,128]{4,3,2,1,0:T(8,128)(2,1)} %param.6) | copy-start | bytes 1572868
  12.9 9.2 %collective-permute-start.1 = (bf16[528,128]{1,0:T(8,128)(2,1)S(1)}, bf16[528,128]{1,0:T(8,128)(2,1)S(1)}, u32[]{:S(2)}, u32[]{:S(2)}) collective-permute-start(bf16[528,128]{1,0:T(8,128)(2,1)S(1)} %prep.1.own_sent), channel_id=1, source_target_pairs={{16,0},{3,1},{18,2},{5,3},{20,4},{7,5},{22,6},{1,7},{14,8},{25,9},... | collective-permute-start | bytes 405512 | tf_op jit(solution)/shard_map/ppermute | solution.py:247
  23.3 5.0 %collective-permute-start.8 = (bf16[4,128,128]{2,1,0:T(8,128)(2,1)S(1)}, bf16[4,128,128]{2,1,0:T(8,128)(2,1)S(1)}, u32[]{:S(2)}, u32[]{:S(2)}) collective-permute-start(bf16[4,128,128]{2,1,0:T(8,128)(2,1)S(1)} %get-tuple-element.20), channel_id=1, source_target_pairs={{0,16},{1,3},{2,18},{3,5},{4,20},{5,7},{6,22},{7,1},{8,14},{9,25},... | collective-permute-start | bytes 393224 | tf_op jit(solution)/shard_map/ppermute | solution.py:247
  23.9 7.3 %collective-permute-start.6 = (bf16[4,128,128]{2,1,0:T(8,128)(2,1)S(1)}, bf16[4,128,128]{2,1,0:T(8,128)(2,1)S(1)}, u32[]{:S(2)}, u32[]{:S(2)}) collective-permute-start(bf16[4,128,128]{2,1,0:T(8,128)(2,1)S(1)} %get-tuple-element.18), channel_id=1, source_target_pairs={{0,2},{1,17},{2,4},{3,19},{4,6},{5,21},{6,0},{7,23},{8,24},{9,15},... | collective-permute-start | bytes 393224 | tf_op jit(solution)/shard_map/ppermute | solution.py:247
  24.7 6.4 %collective-permute-start.7 = (bf16[4,128,128]{2,1,0:T(8,128)(2,1)S(1)}, bf16[4,128,128]{2,1,0:T(8,128)(2,1)S(1)}, u32[]{:S(2)}, u32[]{:S(2)}) collective-permute-start(bf16[4,128,128]{2,1,0:T(8,128)(2,1)S(1)} %get-tuple-element.19), channel_id=1, source_target_pairs={{0,1},{1,9},{2,3},{3,11},{4,5},{5,13},{6,7},{7,15},{8,0},{9,8},{10... | collective-permute-start | bytes 393224 | tf_op jit(solution)/shard_map/ppermute | solution.py:247

commit v3 on v2

--- a/solution.py
+++ b/solution.py
@@ -134,51 +134,65 @@
     return [[wide[p * pairs + q : p * pairs + q + 1] for q in range(pairs)] for p in range(pairs)]
 
 
-def couple(turned, amps, other_basis, other_amps, weight, width):
-    rows, columns = len(amps), len(other_amps)
-    cut = lambda a, r, c: a[r * width : (r + 1) * width, c * width : (c + 1) * width]
-    near = jnp.concatenate(
+def cut(a, r, c, width):
+    return a[r * width : (r + 1) * width, c * width : (c + 1) * width]
+
+
+def intersections(turned, basis):
+    return jnp.concatenate(
         [
-            dot(turned, jnp.concatenate(other_basis[k : k + 2], 1)).astype(BF16)
-            for k in range(0, columns, 2)
+            dot(turned, jnp.concatenate(basis[k : k + 2], 1)).astype(BF16)
+            for k in range(0, len(basis), 2)
         ],
         1,
     )
-    near_t = near.T
-    left = jnp.concatenate(
+
+
+def half(near, amps, width):
+    return jnp.concatenate(
         [
-            dot(
-                near[:, k * width : (k + 2) * width], two_blocks(other_amps[k], other_amps[k + 1])
-            ).astype(BF16)
-            for k in range(0, columns, 2)
+            dot(near[:, k * width : (k + 2) * width], two_blocks(amps[k], amps[k + 1])).astype(BF16)
+            for k in range(0, len(amps), 2)
         ],
         1,
     )
-    right = jnp.concatenate(
-        [
-            dot(near_t[:, k * width : (k + 2) * width], two_blocks(amps[k], amps[k + 1])).astype(
-                BF16
-            )
-            for k in range(0, rows, 2)
-        ],
-        1,
-    )
-    own, other = [], []
-    for p in range(rows):
-        own.append(
-            sum(
-                dot_nt(cut(left, p, q), cut(near, p, q)) * weight[p][q] for q in range(columns)
-            )
+
+
+def row_terms(near, column_amps, weight, width):
+    left = half(near, column_amps, width)
+    return [
+        sum(
+            dot_nt(cut(left, p, q, width), cut(near, p, q, width)) * weight[p][q]
+            for q in range(len(column_amps))
         )
-    for q in range(columns):
-        other.append(
-            sum(dot(cut(right, q, p), cut(near, p, q)) * weight[p][q] for p in range(rows))
+        for p in range(len(weight))
+    ]
+
+
+def column_sums(near, right, weight, width):
+    return [
+        sum(
+            dot(cut(right, q, p, width), cut(near, p, q, width)) * weight[p][q]
+            for p in range(len(weight))
         )
-    return own, other
-
-
-def amps_of(ref, pairs, width, first=0):
-    return [ref[pl.ds(first + p * width, width), :] for p in range(pairs)]
+        for q in range(len(weight[0]))
+    ]
+
+
+def column_terms(near, row_amps, weight, width):
+    return column_sums(near, half(near.T, row_amps, width), weight, width)
+
+
+def bases_of(ref):
+    return [ref[p] for p in range(ref.shape[0])]
+
+
+def amps_of(ref, width):
+    return [ref[pl.ds(p * width, width), :] for p in range((ref.shape[0] - META) // width)]
+
+
+def table_of(ref, role):
+    return ref[pl.ds(ref.shape[0] - META, META), :], role
 
 
 def turn_kernel(basis, turned):
@@ -189,16 +203,16 @@
 
 def near_kernel(own_turned, own_sent, p_basis, p_sent, energy, p_turned, total, p_sum):
     pairs, _, width = p_basis.shape
-    own_a, p_a = (amps_of(r, pairs, width) for r in (own_sent, p_sent))
-    meta = pl.ds(pairs * width, META)
-    tables = ((own_sent[meta, :], OWN), (p_sent[meta, :], PARTNER))
-    p_b = [p_basis[p] for p in range(pairs)]
+    bases, amps = bases_of(p_basis), amps_of(own_sent, width)
     for p in range(pairs):
-        p_turned[pl.ds(p * width, width), :] = p_b[p].T
-    x, y = couple(own_turned[...], own_a, p_b, p_a, weight_rows(tables, OP, pairs), width)
+        p_turned[pl.ds(p * width, width), :] = bases[p].T
+    weight = weight_rows((table_of(own_sent, OWN), table_of(p_sent, PARTNER)), OP, pairs)
+    near = intersections(own_turned[...], bases)
+    x = row_terms(near, amps_of(p_sent, width), weight, width)
+    y = column_terms(near, amps, weight, width)
     for p in range(pairs):
         across = jnp.broadcast_to(energy[pl.ds(p, 1), :], (width, width))
-        total[p] = (across.T + across) * own_a[p].astype(F32) + x[p]
+        total[p] = (across.T + across) * amps[p].astype(F32) + x[p]
         p_sum[p] = y[p]
 
 
@@ -207,29 +221,37 @@
     total, p_back, h_back,
 ):
     pairs, _, width = h_basis.shape
-    own_a, p_a, h_a = (amps_of(r, pairs, width) for r in (own_sent, p_sent, h_sent))
-    meta = pl.ds(pairs * width, META)
-    tables = ((own_sent[meta, :], OWN), (p_sent[meta, :], PARTNER), (h_sent[meta, :], HEAVY))
-    h_b = [h_basis[p] for p in range(pairs)]
+    tables = (table_of(own_sent, OWN), table_of(p_sent, PARTNER), table_of(h_sent, HEAVY))
     weight = weight_rows(tables, OH, pairs) + weight_rows(tables, PH, pairs)
     turned = jnp.concatenate([own_turned[...], p_turned[...]], 0)
-    x, y = couple(turned, own_a + p_a, h_b, h_a, weight, width)
+    near = intersections(turned, bases_of(h_basis))
+    y = column_terms(near, amps_of(own_sent, width) + amps_of(p_sent, width), weight, width)
+    x = row_terms(near, amps_of(h_sent, width), weight, width)
     for p in range(pairs):
         total[p] = total_in[p] + x[p]
         p_back[p] = (p_sum[p] + x[pairs + p]).astype(BF16)
         h_back[p] = y[p].astype(BF16)
 
 
-def light_kernel(own_turned, own_sent, l_basis, l_sent, total_in, total, l_back):
-    pairs, _, width = l_basis.shape
-    own_a, l_a = (amps_of(r, pairs, width) for r in (own_sent, l_sent))
-    meta = pl.ds(pairs * width, META)
-    tables = ((own_sent[meta, :], OWN), (l_sent[meta, :], LIGHT))
-    l_b = [l_basis[p] for p in range(pairs)]
-    x, y = couple(own_turned[...], own_a, l_b, l_a, weight_rows(tables, OL, pairs), width)
-    for p in range(pairs):
-        total[p] = total_in[p] + x[p]
-        l_back[p] = y[p].astype(BF16)
+def cross_kernel(own_turned, own_sent, l_basis, near, right):
+    width = l_basis.shape[2]
+    found = intersections(own_turned[...], bases_of(l_basis))
+    near[...] = found
+    right[...] = half(found.T, amps_of(own_sent, width), width)
+
+
+def light_kernel(near, right, own_sent, l_sent, l_back):
+    pairs, width, _ = l_back.shape
+    weight = weight_rows((table_of(own_sent, OWN), table_of(l_sent, LIGHT)), OL, pairs)
+    for p, y in enumerate(column_sums(near[...], right[...], weight, width)):
+        l_back[p] = y.astype(BF16)
+
+
+def rest_kernel(near, own_sent, l_sent, total_in, total):
+    pairs, width, _ = total.shape
+    weight = weight_rows((table_of(own_sent, OWN), table_of(l_sent, LIGHT)), OL, pairs)
+    for p, x in enumerate(row_terms(near[...], amps_of(l_sent, width), weight, width)):
+        total[p] = total_in[p] + x
 
 
 def on_device(all_routes, reach, pno_basis, amplitudes, pno_energy, fock_values, couplings, counts):
@@ -242,6 +264,8 @@
     square = (pairs, width, width)
     wide = jax.ShapeDtypeStruct(square, F32)
     narrow = jax.ShapeDtypeStruct(square, BF16)
+    flat = jax.ShapeDtypeStruct((pairs * width, depth), BF16)
+    table = jax.ShapeDtypeStruct((pairs * width, pairs * width), BF16)
 
     def moved(block, route):
         return lax.ppermute(block, AXES, route)
@@ -255,16 +279,17 @@
             out_specs=(vmem,) * len(shapes),
             compiler_params=params,
             cost_estimate=pl.CostEstimate(
-                flops=terms * flops, bytes_accessed=2 * basis.size, transcendentals=0
+                flops=int(terms * flops), bytes_accessed=2 * basis.size, transcendentals=0
             ),
         )(*operands)
 
     h_basis = moved(basis, to_h)
     p_basis = moved(basis, to_p)
+    given = (plan, live, fock_values, amps)
     sent = pl.pallas_call(
         functools.partial(prep_kernel, reach),
         out_shape=jax.ShapeDtypeStruct((pairs * width + META, width), BF16),
-        in_specs=[hbm] * 4,
+        in_specs=[hbm] * len(given),
         out_specs=vmem,
         scratch_shapes=[
             pltpu.SMEM(plan.shape, I32),
@@ -274,15 +299,12 @@
         ],
         compiler_params=params,
         name="prep",
-    )(*(pltpu.with_memory_space_constraint(x, pltpu.HBM) for x in (plan, live, fock_values, amps)))
-    h_sent = moved(sent, to_h)
-    p_sent = moved(sent, to_p)
-    l_basis = moved(basis, to_l)
-    l_sent = moved(sent, to_l)
-    flat = jax.ShapeDtypeStruct((pairs * width, depth), BF16)
+    )(*(pltpu.with_memory_space_constraint(x, pltpu.HBM) for x in given))
+    h_sent, p_sent = moved(sent, to_h), moved(sent, to_p)
+    l_basis, l_sent = moved(basis, to_l), moved(sent, to_l)
     (turned,) = kernel(turn_kernel, 0, (flat,), basis)
     p_turned, total, p_sum = kernel(
-        near_kernel, 1, (flat, wide, wide), *(turned, sent, p_basis, p_sent, energy)
+        near_kernel, 1, (flat, wide, wide), turned, sent, p_basis, p_sent, energy
     )
     total, p_back, h_back = kernel(
         heavy_kernel,
@@ -290,7 +312,9 @@
         (wide, narrow, narrow),
         *(turned, p_turned, sent, p_sent, h_basis, h_sent, total, p_sum),
     )
-    total, l_back = kernel(light_kernel, 1, (wide, narrow), turned, sent, l_basis, l_sent, total)
+    near, right = kernel(cross_kernel, 0.5, (table, table), turned, sent, l_basis)
+    (l_back,) = kernel(light_kernel, 0.2, (narrow,), near, right, sent, l_sent)
+    (total,) = kernel(rest_kernel, 0.3, (wide,), near, sent, l_sent, total)
     for piece, route in ((h_back, to_h), (p_back, to_p), (l_back, to_l)):
         total = total + moved(piece, back(route)).astype(F32)
     return total[None, None]

time: 32.2 us -> 32 us (level)
  starting transfers between devices: 12.7 us -> 11.2 us
  waiting for transfers between devices: 11.4 us -> 12 us
  Pallas kernels: 6.02 us -> 6.51 us
    ppermute x9, starting transfers between devices: 12.7 us -> 11.2 us  [moved(): return lax.ppermute(block, AXES, route)]
    ppermute x9, waiting for transfers between devices: 11.4 us -> 12 us  [moved(): return lax.ppermute(block, AXES, route)]
    pallas_call x4 -> x6, Pallas kernels: 4.75 us -> 5.23 us  [kernel(): pl.pallas_call(body, out_shape=shapes, in_specs=[vmem] * len(operands), o...]
  transfers between devices with their start and end apart: 9 -> 9, of which waited for: 4 -> 4; matrix products, arithmetic and copies ran while one was open for 0% -> 0% of each run, Pallas kernels for 15% -> 21%
where the time goes in v3:
time: 32 us; the launch traced here: 31.6 us
  waiting for transfers between devices  12 us (38%)
  starting transfers between devices  11.2 us (35%)
  Pallas kernels  6.51 us (20%)
  local copies, waits for them, and re-layouts  1.04 us (3%)
  other arithmetic  0.77 us (2%)
    ppermute x9, waiting for transfers between devices, moved(): return lax.ppermute(block, AXES, route)  12 us
    ppermute x9, starting transfers between devices, moved(): return lax.ppermute(block, AXES, route)  11.2 us
    pallas_call x6, Pallas kernels, kernel(): pl.pallas_call(body, out_shape=shapes, in_specs=[vmem] * len(operands), o...  5.23 us
    pallas_call x1, Pallas kernels, on_device(): pl.pallas_call(functools.partial(prep_kernel, reach), out_shape=jax.Shape...  1.28 us
    unnamed x4, local copies, waits for them, and re-layouts  1.04 us
    broadcast_in_dim x1, other arithmetic, on_device(): return total[None, None]  0.77 us
  transfers between devices with their start and end apart: 9, of which 4 were waited for; matrix products, arithmetic and copies ran while one was open for 0% of the time, Pallas kernels for 21%

profile of v3, /device:TPU:0, one launch (start us, length us, event | category | flops | bytes accessed | tf_op | source)
XLA Modules:
  0.0 31.6 jit_solution(7230599075541152399)
XLA Ops:
  0.0 0.5 %collective-permute-start.2 = (bf16[4,512,128]{2,1,0:T(8,128)(2,1)}, bf16[4,512,128]{2,1,0:T(8,128)(2,1)S(1)}, u32[]{:S(2)}, u32[]{:S(2)}) collective-permute-start(bf16[4,512,128]{2,1,0:T(8,128)(2,1)} %bitcast.9), channel_id=1, source_target_pairs={{1,0},{9,1},{3,2},{11,3},{5,4},{13,5},{7,6},{15,7},{0,8},{8,9},{2,... | collective-permute-start | bytes 1572872 | tf_op jit(solution)/shard_map/ppermute | solution.py:271
  0.5 4.6 %collective-permute-start.4 = (bf16[4,512,128]{2,1,0:T(8,128)(2,1)}, bf16[4,512,128]{2,1,0:T(8,128)(2,1)S(1)}, u32[]{:S(2)}, u32[]{:S(2)}) collective-permute-start(bf16[4,512,128]{2,1,0:T(8,128)(2,1)} %bitcast.10), channel_id=1, source_target_pairs={{2,0},{17,1},{4,2},{19,3},{6,4},{21,5},{0,6},{23,7},{24,8},{15,9},... | collective-permute-start | bytes 1572872 | tf_op jit(solution)/shard_map/ppermute | solution.py:271
  5.1 1.5 %collective-permute-start = (bf16[4,512,128]{2,1,0:T(8,128)(2,1)}, bf16[4,512,128]{2,1,0:T(8,128)(2,1)S(1)}, u32[]{:S(2)}, u32[]{:S(2)}) collective-permute-start(bf16[4,512,128]{2,1,0:T(8,128)(2,1)} %bitcast.11), channel_id=1, source_target_pairs={{16,0},{3,1},{18,2},{5,3},{20,4},{7,5},{22,6},{1,7},{14,8},{25,9},... | collective-permute-start | bytes 1572872 | tf_op jit(solution)/shard_map/ppermute | solution.py:271
  6.6 0.0 copy-start.1
  6.6 1.3 %prep.1.own_sent = bf16[528,128]{1,0:T(8,128)(2,1)S(1)} custom-call(s32[3,4,12]{2,1,0:T(4,128)} %bitcast.15, s32[4]{0:T(128)} %bitcast.16, f32[256]{0:T(256)} %fock_hbm.1, bf16[4,128,128]{2,1,0:T(8,128)(2,1)} %bitcast.14), custom_call_target="tpu_custom_call" | custom-call | tf_op jit(solution)/shard_map/prep/pallas_call | solution.py:289
  7.9 0.0 collective-permute-start.3
  7.9 0.8 %collective-permute-start.5 = (bf16[528,128]{1,0:T(8,128)(2,1)S(1)}, bf16[528,128]{1,0:T(8,128)(2,1)S(1)}, u32[]{:S(2)}, u32[]{:S(2)}) collective-permute-start(bf16[528,128]{1,0:T(8,128)(2,1)S(1)} %prep.1.own_sent), channel_id=1, source_target_pairs={{2,0},{17,1},{4,2},{19,3},{6,4},{21,5},{0,6},{23,7},{24,8},{15,9},... | collective-permute-start | bytes 405512 | tf_op jit(solution)/shard_map/ppermute | solution.py:271
  8.7 0.0 copy-start
  8.7 1.0 %copy-done = bf16[1,1,4,512,128]{4,3,2,1,0:T(8,128)(2,1)S(1)} copy-done((bf16[1,1,4,512,128]{4,3,2,1,0:T(8,128)(2,1)S(1)}, bf16[1,1,4,512,128]{4,3,2,1,0:T(8,128)(2,1)}, u32[]{:S(2)}) %copy-start) | copy-done | bytes 524312
  9.7 0.2 shard_map.64.own_turned
  9.9 3.0 %collective-permute-done.3.p_sent = bf16[528,128]{1,0:T(8,128)(2,1)S(1)} collective-permute-done((bf16[528,128]{1,0:T(8,128)(2,1)S(1)}, bf16[528,128]{1,0:T(8,128)(2,1)S(1)}, u32[]{:S(2)}, u32[]{:S(2)}) %collective-permute-start.3) | collective-permute-done | bytes 135200 | tf_op jit(solution)/shard_map/ppermute | solution.py:271
  12.9 0.9 %collective-permute-start.1 = (bf16[528,128]{1,0:T(8,128)(2,1)S(1)}, bf16[528,128]{1,0:T(8,128)(2,1)S(1)}, u32[]{:S(2)}, u32[]{:S(2)}) collective-permute-start(bf16[528,128]{1,0:T(8,128)(2,1)S(1)} %prep.1.own_sent), channel_id=1, source_target_pairs={{16,0},{3,1},{18,2},{5,3},{20,4},{7,5},{22,6},{1,7},{14,8},{25,9},... | collective-permute-start | bytes 405512 | tf_op jit(solution)/shard_map/ppermute | solution.py:271
  13.8 0.0 collective-permute-done.2.p_basis
  13.8 0.0 copy-done.1
  13.8 1.3 %shard_map.66 = (bf16[512,512]{1,0:T(8,128)(2,1)S(1)}, f32[4,128,128]{2,1,0:T(8,128)S(1)}, f32[4,128,128]{2,1,0:T(8,128)S(1)}) custom-call(bf16[512,512]{1,0:T(8,128)(2,1)S(1)} %shard_map.64.own_turned, bf16[528,128]{1,0:T(8,128)(2,1)S(1)} %prep.1.own_sent, bf16[4,512,128]{2,1,0:T(8,128)(2,1)S(1)} %collective-permute-done.2.p_basis, ...), custom_call_target="tpu_custom_call" | custom-call | flops 536870912 | bytes 524288 | tf_op jit(solution)/shard_map/pallas_call | solution.py:275
  15.1 4.7 %collective-permute-done.5.h_sent = bf16[528,128]{1,0:T(8,128)(2,1)S(1)} collective-permute-done((bf16[528,128]{1,0:T(8,128)(2,1)S(1)}, bf16[528,128]{1,0:T(8,128)(2,1)S(1)}, u32[]{:S(2)}, u32[]{:S(2)}) %collective-permute-start.5) | collective-permute-done | bytes 135200 | tf_op jit(solution)/shard_map/ppermute | solution.py:271
  19.8 0.0 collective-permute-done.4.h_basis
  19.8 2.1 %shard_map.67 = (f32[4,128,128]{2,1,0:T(8,128)S(1)}, bf16[4,128,128]{2,1,0:T(8,128)(2,1)S(1)}, bf16[4,128,128]{2,1,0:T(8,128)(2,1)S(1)}) custom-call(bf16[512,512]{1,0:T(8,128)(2,1)S(1)} %shard_map.64.own_turned, bf16[512,512]{1,0:T(8,128)(2,1)S(1)} %get-tuple-element.14.p_turned, bf16[528,128]{1,0:T(8,128)(2,1)S(1)} %prep.1.own_sent, ...), custom_call_target="tpu_custom_call" | custom-call | flops 1073741824 | bytes 524288 | tf_op jit(solution)/shard_map/pallas_call | solution.py:275
  21.9 0.1 collective-permute-start.6
  22.0 2.8 %collective-permute-start.7 = (bf16[4,128,128]{2,1,0:T(8,128)(2,1)S(1)}, bf16[4,128,128]{2,1,0:T(8,128)(2,1)S(1)}, u32[]{:S(2)}, u32[]{:S(2)}) collective-permute-start(bf16[4,128,128]{2,1,0:T(8,128)(2,1)S(1)} %get-tuple-element.19), channel_id=1, source_target_pairs={{0,1},{1,9},{2,3},{3,11},{4,5},{5,13},{6,7},{7,15},{8,0},{9,8},{10... | collective-permute-start | bytes 393224 | tf_op jit(solution)/shard_map/ppermute | solution.py:271
  24.7 0.0 collective-permute-done.l_basis
  24.7 0.7 %shard_map.65 = (bf16[512,512]{1,0:T(8,128)(2,1)S(1)}, bf16[512,512]{1,0:T(8,128)(2,1)S(1)}) custom-call(bf16[512,512]{1,0:T(8,128)(2,1)S(1)} %shard_map.64.own_turned, bf16[528,128]{1,0:T(8,128)(2,1)S(1)} %prep.1.own_sent, bf16[4,512,128]{2,1,0:T(8,128)(2,1)S(1)} %collective-permute-done.l_basis), custom_call_target="tpu_custom_call" | custom-call | flops 268435456 | bytes 524288 | tf_op jit(solution)/shard_map/pallas_call | solution.py:275
  25.5 0.0 collective-permute-done.1.l_sent
  25.5 0.3 shard_map.69
  25.8 0.1 collective-permute-start.8
  25.9 0.6 %shard_map.68 = f32[4,128,128]{2,1,0:T(8,128)S(1)} custom-call(bf16[512,512]{1,0:T(8,128)(2,1)S(1)} %get-tuple-element.13.near, bf16[528,128]{1,0:T(8,128)(2,1)S(1)} %prep.1.own_sent, bf16[528,128]{1,0:T(8,128)(2,1)S(1)} %collective-permute-done.1.l_sent, f32[4,128,128]{2,1,0:T(8,128)S(1)} %get-tuple-element.17.total_in), custom_call_target="tpu_custom_call" | custom-call | flops 161061280 | bytes 524288 | tf_op jit(solution)/shard_map/pallas_call | solution.py:275
  26.5 2.8 %collective-permute-done.6 = bf16[4,128,128]{2,1,0:T(8,128)(2,1)S(1)} collective-permute-done((bf16[4,128,128]{2,1,0:T(8,128)(2,1)S(1)}, bf16[4,128,128]{2,1,0:T(8,128)(2,1)S(1)}, u32[]{:S(2)}, u32[]{:S(2)}) %collective-permute-start.6) | collective-permute-done | bytes 131104 | tf_op jit(solution)/shard_map/ppermute | solution.py:271
  29.3 0.0 collective-permute-done.7
  29.3 1.5 %collective-permute-done.8 = bf16[4,128,128]{2,1,0:T(8,128)(2,1)S(1)} collective-permute-done((bf16[4,128,128]{2,1,0:T(8,128)(2,1)S(1)}, bf16[4,128,128]{2,1,0:T(8,128)(2,1)S(1)}, u32[]{:S(2)}, u32[]{:S(2)}) %collective-permute-start.8) | collective-permute-done | bytes 131104 | tf_op jit(solution)/shard_map/ppermute | solution.py:271
  30.8 0.8 %add_bitcast_fusion = f32[1,1,4,128,128]{4,3,2,1,0:T(8,128)} fusion(bf16[4,128,128]{2,1,0:T(8,128)(2,1)S(1)} %collective-permute-done.8, bf16[4,128,128]{2,1,0:T(8,128)(2,1)S(1)} %collective-permute-done.7, f32[4,128,128]{2,1,0:T(8,128)S(1)} %shard_map.68, bf16[4,128,128]{2,1,0:T(8,128)(2,1)S(1)} %collective-permute-done.6), kind=kLoop, calls=%fused_computation | loop fusion | flops 393216 | bytes 917504 | tf_op jit(solution)/shard_map/broadcast_in_dim | solution.py:320
Async XLA Ops:
  0.0 13.8 %collective-permute-start.2 = (bf16[4,512,128]{2,1,0:T(8,128)(2,1)}, bf16[4,512,128]{2,1,0:T(8,128)(2,1)S(1)}, u32[]{:S(2)}, u32[]{:S(2)}) collective-permute-start(bf16[4,512,128]{2,1,0:T(8,128)(2,1)} %bitcast.9), channel_id=1, source_target_pairs={{1,0},{9,1},{3,2},{11,3},{5,4},{13,5},{7,6},{15,7},{0,8},{8,9},{2,... | collective-permute-start | bytes 1572872 | tf_op jit(solution)/shard_map/ppermute | solution.py:271
  0.5 19.3 %collective-permute-start.4 = (bf16[4,512,128]{2,1,0:T(8,128)(2,1)}, bf16[4,512,128]{2,1,0:T(8,128)(2,1)S(1)}, u32[]{:S(2)}, u32[]{:S(2)}) collective-permute-start(bf16[4,512,128]{2,1,0:T(8,128)(2,1)} %bitcast.10), channel_id=1, source_target_pairs={{2,0},{17,1},{4,2},{19,3},{6,4},{21,5},{0,6},{23,7},{24,8},{15,9},... | collective-permute-start | bytes 1572872 | tf_op jit(solution)/shard_map/ppermute | solution.py:271
  5.1 19.7 %collective-permute-start = (bf16[4,512,128]{2,1,0:T(8,128)(2,1)}, bf16[4,512,128]{2,1,0:T(8,128)(2,1)S(1)}, u32[]{:S(2)}, u32[]{:S(2)}) collective-permute-start(bf16[4,512,128]{2,1,0:T(8,128)(2,1)} %bitcast.11), channel_id=1, source_target_pairs={{16,0},{3,1},{18,2},{5,3},{20,4},{7,5},{22,6},{1,7},{14,8},{25,9},... | collective-permute-start | bytes 1572872 | tf_op jit(solution)/shard_map/ppermute | solution.py:271
  6.6 7.2 %copy-start.1 = (f32[1,1,4,128]{3,2,1,0:T(4,128)S(1)}, f32[1,1,4,128]{3,2,1,0:T(4,128)}, u32[]{:S(2)}) copy-start(f32[1,1,4,128]{3,2,1,0:T(4,128)} %param.8) | copy-start | bytes 6148
  7.9 5.0 %collective-permute-start.3 = (bf16[528,128]{1,0:T(8,128)(2,1)S(1)}, bf16[528,128]{1,0:T(8,128)(2,1)S(1)}, u32[]{:S(2)}, u32[]{:S(2)}) collective-permute-start(bf16[528,128]{1,0:T(8,128)(2,1)S(1)} %prep.1.own_sent), channel_id=1, source_target_pairs={{1,0},{9,1},{3,2},{11,3},{5,4},{13,5},{7,6},{15,7},{0,8},{8,9},{2,... | collective-permute-start | bytes 405512 | tf_op jit(solution)/shard_map/ppermute | solution.py:271
  7.9 11.9 %collective-permute-start.5 = (bf16[528,128]{1,0:T(8,128)(2,1)S(1)}, bf16[528,128]{1,0:T(8,128)(2,1)S(1)}, u32[]{:S(2)}, u32[]{:S(2)}) collective-permute-start(bf16[528,128]{1,0:T(8,128)(2,1)S(1)} %prep.1.own_sent), channel_id=1, source_target_pairs={{2,0},{17,1},{4,2},{19,3},{6,4},{21,5},{0,6},{23,7},{24,8},{15,9},... | collective-permute-start | bytes 405512 | tf_op jit(solution)/shard_map/ppermute | solution.py:271
  8.7 1.0 %copy-start = (bf16[1,1,4,512,128]{4,3,2,1,0:T(8,128)(2,1)S(1)}, bf16[1,1,4,512,128]{4,3,2,1,0:T(8,128)(2,1)}, u32[]{:S(2)}) copy-start(bf16[1,1,4,512,128]{4,3,2,1,0:T(8,128)(2,1)} %param.6) | copy-start | bytes 1572868
  12.9 12.6 %collective-permute-start.1 = (bf16[528,128]{1,0:T(8,128)(2,1)S(1)}, bf16[528,128]{1,0:T(8,128)(2,1)S(1)}, u32[]{:S(2)}, u32[]{:S(2)}) collective-permute-start(bf16[528,128]{1,0:T(8,128)(2,1)S(1)} %prep.1.own_sent), channel_id=1, source_target_pairs={{16,0},{3,1},{18,2},{5,3},{20,4},{7,5},{22,6},{1,7},{14,8},{25,9},... | collective-permute-start | bytes 405512 | tf_op jit(solution)/shard_map/ppermute | solution.py:271
  21.9 7.4 %collective-permute-start.6 = (bf16[4,128,128]{2,1,0:T(8,128)(2,1)S(1)}, bf16[4,128,128]{2,1,0:T(8,128)(2,1)S(1)}, u32[]{:S(2)}, u32[]{:S(2)}) collective-permute-start(bf16[4,128,128]{2,1,0:T(8,128)(2,1)S(1)} %get-tuple-element.18), channel_id=1, source_target_pairs={{0,2},{1,17},{2,4},{3,19},{4,6},{5,21},{6,0},{7,23},{8,24},{9,15},... | collective-permute-start | bytes 393224 | tf_op jit(solution)/shard_map/ppermute | solution.py:271
  22.0 7.3 %collective-permute-start.7 = (bf16[4,128,128]{2,1,0:T(8,128)(2,1)S(1)}, bf16[4,128,128]{2,1,0:T(8,128)(2,1)S(1)}, u32[]{:S(2)}, u32[]{:S(2)}) collective-permute-start(bf16[4,128,128]{2,1,0:T(8,128)(2,1)S(1)} %get-tuple-element.19), channel_id=1, source_target_pairs={{0,1},{1,9},{2,3},{3,11},{4,5},{5,13},{6,7},{7,15},{8,0},{9,8},{10... | collective-permute-start | bytes 393224 | tf_op jit(solution)/shard_map/ppermute | solution.py:271
  25.8 5.0 %collective-permute-start.8 = (bf16[4,128,128]{2,1,0:T(8,128)(2,1)S(1)}, bf16[4,128,128]{2,1,0:T(8,128)(2,1)S(1)}, u32[]{:S(2)}, u32[]{:S(2)}) collective-permute-start(bf16[4,128,128]{2,1,0:T(8,128)(2,1)S(1)} %shard_map.69), channel_id=1, source_target_pairs={{0,16},{1,3},{2,18},{3,5},{4,20},{5,7},{6,22},{7,1},{8,14},{9,25},... | collective-permute-start | bytes 393224 | tf_op jit(solution)/shard_map/ppermute | solution.py:271

commit v4 on v3

--- a/solution.py
+++ b/solution.py
@@ -66,7 +66,9 @@
     )
 
 
-def prep_kernel(reach, plan_hbm, counts_hbm, fock_hbm, amps_hbm, sent, plan, counts, fock, sems):
+def prep_kernel(
+    reach, plan_hbm, counts_hbm, fock_hbm, amps_hbm, sent, table_out, plan, counts, fock, sems
+):
     pairs, width, _ = amps_hbm.shape
     copies = [
         pltpu.make_async_copy(src, dst, sems.at[k])
@@ -114,6 +116,7 @@
         for part, piece in enumerate((high, middle, rest - middle)):
             table = jnp.where(row == part * ROLES + role, piece + table, table)
     sent[pl.ds(pairs * width, META), :] = table.astype(BF16)
+    table_out[...] = table.astype(BF16)
     for copy in copies[3:]:
         copy.wait()
 
@@ -240,9 +243,9 @@
     right[...] = half(found.T, amps_of(own_sent, width), width)
 
 
-def light_kernel(near, right, own_sent, l_sent, l_back):
+def light_kernel(near, right, own_table, l_table, l_back):
     pairs, width, _ = l_back.shape
-    weight = weight_rows((table_of(own_sent, OWN), table_of(l_sent, LIGHT)), OL, pairs)
+    weight = weight_rows((table_of(own_table, OWN), table_of(l_table, LIGHT)), OL, pairs)
     for p, y in enumerate(column_sums(near[...], right[...], weight, width)):
         l_back[p] = y.astype(BF16)
 
@@ -286,11 +289,14 @@
     h_basis = moved(basis, to_h)
     p_basis = moved(basis, to_p)
     given = (plan, live, fock_values, amps)
-    sent = pl.pallas_call(
+    sent, rows = pl.pallas_call(
         functools.partial(prep_kernel, reach),
-        out_shape=jax.ShapeDtypeStruct((pairs * width + META, width), BF16),
+        out_shape=(
+            jax.ShapeDtypeStruct((pairs * width + META, width), BF16),
+            jax.ShapeDtypeStruct((META, LANES), BF16),
+        ),
         in_specs=[hbm] * len(given),
-        out_specs=vmem,
+        out_specs=(vmem, vmem),
         scratch_shapes=[
             pltpu.SMEM(plan.shape, I32),
             pltpu.SMEM(live.shape, I32),
@@ -301,7 +307,9 @@
         name="prep",
     )(*(pltpu.with_memory_space_constraint(x, pltpu.HBM) for x in given))
     h_sent, p_sent = moved(sent, to_h), moved(sent, to_p)
-    l_basis, l_sent = moved(basis, to_l), moved(sent, to_l)
+    l_rows, l_basis, l_sent = (
+        moved(what, to_l) for what in (rows, basis, sent)
+    )
     (turned,) = kernel(turn_kernel, 0, (flat,), basis)
     p_turned, total, p_sum = kernel(
         near_kernel, 1, (flat, wide, wide), turned, sent, p_basis, p_sent, energy
@@ -313,7 +321,7 @@
         *(turned, p_turned, sent, p_sent, h_basis, h_sent, total, p_sum),
     )
     near, right = kernel(cross_kernel, 0.5, (table, table), turned, sent, l_basis)
-    (l_back,) = kernel(light_kernel, 0.2, (narrow,), near, right, sent, l_sent)
+    (l_back,) = kernel(light_kernel, 0.2, (narrow,), near, right, rows, l_rows)
     (total,) = kernel(rest_kernel, 0.3, (wide,), near, sent, l_sent, total)
     for piece, route in ((h_back, to_h), (p_back, to_p), (l_back, to_l)):
         total = total + moved(piece, back(route)).astype(F32)

time: 32 us -> 32 us (level)
  starting transfers between devices: 11.2 us -> 12.3 us
  waiting for transfers between devices: 12 us -> 11.1 us
    ppermute x9 -> x10, starting transfers between devices: 11.2 us -> 12.3 us  [moved(): return lax.ppermute(block, AXES, route)]
    ppermute x9 -> x10, waiting for transfers between devices: 12 us -> 11.1 us  [moved(): return lax.ppermute(block, AXES, route)]
  transfers between devices with their start and end apart: 9 -> 10, of which waited for: 4 -> 4; matrix products, arithmetic and copies ran while one was open for 0% -> 0% of each run, Pallas kernels for 21% -> 20%
where the time goes in v4:
time: 32 us; the launch traced here: 31.6 us
  starting transfers between devices  12.3 us (38%)
  waiting for transfers between devices  11.1 us (35%)
  Pallas kernels  6.35 us (20%)
  local copies, waits for them, and re-layouts  1.05 us (3%)
  other arithmetic  0.76 us (2%)
    ppermute x10, starting transfers between devices, moved(): return lax.ppermute(block, AXES, route)  12.3 us
    ppermute x10, waiting for transfers between devices, moved(): return lax.ppermute(block, AXES, route)  11.1 us
    pallas_call x6, Pallas kernels, kernel(): pl.pallas_call(body, out_shape=shapes, in_specs=[vmem] * len(operands), o...  5.21 us
    pallas_call x1, Pallas kernels, on_device(): pl.pallas_call(functools.partial(prep_kernel, reach), out_shape=(jax.Shap...  1.15 us
    unnamed x4, local copies, waits for them, and re-layouts  1.05 us
    broadcast_in_dim x1, other arithmetic, on_device(): return total[None, None]  0.76 us
  transfers between devices with their start and end apart: 10, of which 4 were waited for; matrix products, arithmetic and copies ran while one was open for 0% of the time, Pallas kernels for 20%

profile of v4, /device:TPU:0, one launch (start us, length us, event | category | flops | bytes accessed | tf_op | source)
XLA Modules:
  0.0 31.6 jit_solution(16292548183873661852)
XLA Ops:
  0.0 0.5 %collective-permute-start.2 = (bf16[4,512,128]{2,1,0:T(8,128)(2,1)}, bf16[4,512,128]{2,1,0:T(8,128)(2,1)S(1)}, u32[]{:S(2)}, u32[]{:S(2)}) collective-permute-start(bf16[4,512,128]{2,1,0:T(8,128)(2,1)} %bitcast.9), channel_id=1, source_target_pairs={{1,0},{9,1},{3,2},{11,3},{5,4},{13,5},{7,6},{15,7},{0,8},{8,9},{2,... | collective-permute-start | bytes 1572872 | tf_op jit(solution)/shard_map/ppermute | solution.py:274
  0.5 4.6 %collective-permute-start.4 = (bf16[4,512,128]{2,1,0:T(8,128)(2,1)}, bf16[4,512,128]{2,1,0:T(8,128)(2,1)S(1)}, u32[]{:S(2)}, u32[]{:S(2)}) collective-permute-start(bf16[4,512,128]{2,1,0:T(8,128)(2,1)} %bitcast.10), channel_id=1, source_target_pairs={{2,0},{17,1},{4,2},{19,3},{6,4},{21,5},{0,6},{23,7},{24,8},{15,9},... | collective-permute-start | bytes 1572872 | tf_op jit(solution)/shard_map/ppermute | solution.py:274
  5.1 1.5 %collective-permute-start = (bf16[4,512,128]{2,1,0:T(8,128)(2,1)}, bf16[4,512,128]{2,1,0:T(8,128)(2,1)S(1)}, u32[]{:S(2)}, u32[]{:S(2)}) collective-permute-start(bf16[4,512,128]{2,1,0:T(8,128)(2,1)} %bitcast.11), channel_id=1, source_target_pairs={{16,0},{3,1},{18,2},{5,3},{20,4},{7,5},{22,6},{1,7},{14,8},{25,9},... | collective-permute-start | bytes 1572872 | tf_op jit(solution)/shard_map/ppermute | solution.py:274
  6.6 1.1 %prep.1 = (bf16[528,128]{1,0:T(8,128)(2,1)S(1)}, bf16[16,128]{1,0:T(8,128)(2,1)S(1)}) custom-call(s32[3,4,12]{2,1,0:T(4,128)} %bitcast.15, s32[4]{0:T(128)} %bitcast.16, f32[256]{0:T(256)} %fock_hbm.1, bf16[4,128,128]{2,1,0:T(8,128)(2,1)} %bitcast.14), custom_call_target="tpu_custom_call" | custom-call | tf_op jit(solution)/shard_map/prep/pallas_call | solution.py:292
  7.7 0.0 collective-permute-start.3
  7.8 0.8 %collective-permute-start.5 = (bf16[528,128]{1,0:T(8,128)(2,1)S(1)}, bf16[528,128]{1,0:T(8,128)(2,1)S(1)}, u32[]{:S(2)}, u32[]{:S(2)}) collective-permute-start(bf16[528,128]{1,0:T(8,128)(2,1)S(1)} %get-tuple-element.15.own_sent), channel_id=1, source_target_pairs={{2,0},{17,1},{4,2},{19,3},{6,4},{21,5},{0,6},{23,7},{24,8},{15,9},... | collective-permute-start | bytes 405512 | tf_op jit(solution)/shard_map/ppermute | solution.py:274
  8.5 0.0 copy-start
  8.5 1.0 %copy-done = bf16[1,1,4,512,128]{4,3,2,1,0:T(8,128)(2,1)S(1)} copy-done((bf16[1,1,4,512,128]{4,3,2,1,0:T(8,128)(2,1)S(1)}, bf16[1,1,4,512,128]{4,3,2,1,0:T(8,128)(2,1)}, u32[]{:S(2)}) %copy-start) | copy-done | bytes 524312
  9.6 0.2 shard_map.64.own_turned
  9.8 0.0 copy-start.1
  9.8 3.0 %collective-permute-done.3.p_sent = bf16[528,128]{1,0:T(8,128)(2,1)S(1)} collective-permute-done((bf16[528,128]{1,0:T(8,128)(2,1)S(1)}, bf16[528,128]{1,0:T(8,128)(2,1)S(1)}, u32[]{:S(2)}, u32[]{:S(2)}) %collective-permute-start.3) | collective-permute-done | bytes 135200 | tf_op jit(solution)/shard_map/ppermute | solution.py:274
  12.8 1.0 %collective-permute-start.1 = (bf16[528,128]{1,0:T(8,128)(2,1)S(1)}, bf16[528,128]{1,0:T(8,128)(2,1)S(1)}, u32[]{:S(2)}, u32[]{:S(2)}) collective-permute-start(bf16[528,128]{1,0:T(8,128)(2,1)S(1)} %get-tuple-element.15.own_sent), channel_id=1, source_target_pairs={{16,0},{3,1},{18,2},{5,3},{20,4},{7,5},{22,6},{1,7},{14,8},{25,9},... | collective-permute-start | bytes 405512 | tf_op jit(solution)/shard_map/ppermute | solution.py:274
  13.8 0.0 collective-permute-done.2.p_basis
  13.8 1.0 %collective-permute-start.8 = (bf16[16,128]{1,0:T(8,128)(2,1)S(1)}, bf16[16,128]{1,0:T(8,128)(2,1)S(1)}, u32[]{:S(2)}, u32[]{:S(2)}) collective-permute-start(bf16[16,128]{1,0:T(8,128)(2,1)S(1)} %get-tuple-element.24.own_table), channel_id=1, source_target_pairs={{16,0},{3,1},{18,2},{5,3},{20,4},{7,5},{22,6},{1,7},{14,8},{25,9},... | collective-permute-start | bytes 12296 | tf_op jit(solution)/shard_map/ppermute | solution.py:274
  14.8 0.0 copy-done.1
  14.8 1.2 %shard_map.66 = (bf16[512,512]{1,0:T(8,128)(2,1)S(1)}, f32[4,128,128]{2,1,0:T(8,128)S(1)}, f32[4,128,128]{2,1,0:T(8,128)S(1)}) custom-call(bf16[512,512]{1,0:T(8,128)(2,1)S(1)} %shard_map.64.own_turned, bf16[528,128]{1,0:T(8,128)(2,1)S(1)} %get-tuple-element.15.own_sent, bf16[4,512,128]{2,1,0:T(8,128)(2,1)S(1)} %collective-permute-done.2.p_basis, ...), custom_call_target="tpu_custom_call" | custom-call | flops 536870912 | bytes 524288 | tf_op jit(solution)/shard_map/pallas_call | solution.py:278
  16.0 3.8 %collective-permute-done.5.h_sent = bf16[528,128]{1,0:T(8,128)(2,1)S(1)} collective-permute-done((bf16[528,128]{1,0:T(8,128)(2,1)S(1)}, bf16[528,128]{1,0:T(8,128)(2,1)S(1)}, u32[]{:S(2)}, u32[]{:S(2)}) %collective-permute-start.5) | collective-permute-done | bytes 135200 | tf_op jit(solution)/shard_map/ppermute | solution.py:274
  19.8 0.0 collective-permute-done.4.h_basis
  19.8 2.1 %shard_map.67 = (f32[4,128,128]{2,1,0:T(8,128)S(1)}, bf16[4,128,128]{2,1,0:T(8,128)(2,1)S(1)}, bf16[4,128,128]{2,1,0:T(8,128)(2,1)S(1)}) custom-call(bf16[512,512]{1,0:T(8,128)(2,1)S(1)} %shard_map.64.own_turned, bf16[512,512]{1,0:T(8,128)(2,1)S(1)} %get-tuple-element.17.p_turned, bf16[528,128]{1,0:T(8,128)(2,1)S(1)} %get-tuple-element.15.own_sent, ...), custom_call_target="tpu_custom_call" | custom-call | flops 1073741824 | bytes 524288 | tf_op jit(solution)/shard_map/pallas_call | solution.py:278
  22.0 0.1 collective-permute-start.6
  22.0 2.7 %collective-permute-start.7 = (bf16[4,128,128]{2,1,0:T(8,128)(2,1)S(1)}, bf16[4,128,128]{2,1,0:T(8,128)(2,1)S(1)}, u32[]{:S(2)}, u32[]{:S(2)}) collective-permute-start(bf16[4,128,128]{2,1,0:T(8,128)(2,1)S(1)} %get-tuple-element.22), channel_id=1, source_target_pairs={{0,1},{1,9},{2,3},{3,11},{4,5},{5,13},{6,7},{7,15},{8,0},{9,8},{10... | collective-permute-start | bytes 393224 | tf_op jit(solution)/shard_map/ppermute | solution.py:274
  24.7 0.0 collective-permute-done.l_basis
  24.7 0.8 %shard_map.65 = (bf16[512,512]{1,0:T(8,128)(2,1)S(1)}, bf16[512,512]{1,0:T(8,128)(2,1)S(1)}) custom-call(bf16[512,512]{1,0:T(8,128)(2,1)S(1)} %shard_map.64.own_turned, bf16[528,128]{1,0:T(8,128)(2,1)S(1)} %get-tuple-element.15.own_sent, bf16[4,512,128]{2,1,0:T(8,128)(2,1)S(1)} %collective-permute-done.l_basis), custom_call_target="tpu_custom_call" | custom-call | flops 268435456 | bytes 524288 | tf_op jit(solution)/shard_map/pallas_call | solution.py:278
  25.5 0.0 collective-permute-done.8.l_table
  25.5 0.3 shard_map.69
  25.8 0.1 collective-permute-start.9
  25.9 0.0 collective-permute-done.1.l_sent
  25.9 0.6 %shard_map.68 = f32[4,128,128]{2,1,0:T(8,128)S(1)} custom-call(bf16[512,512]{1,0:T(8,128)(2,1)S(1)} %get-tuple-element.16.near, bf16[528,128]{1,0:T(8,128)(2,1)S(1)} %get-tuple-element.15.own_sent, bf16[528,128]{1,0:T(8,128)(2,1)S(1)} %collective-permute-done.1.l_sent, f32[4,128,128]{2,1,0:T(8,128)S(1)} %get-tuple-element.20.total_in), custom_call_target="tpu_custom_call" | custom-call | flops 161061280 | bytes 524288 | tf_op jit(solution)/shard_map/pallas_call | solution.py:278
  26.5 2.8 %collective-permute-done.6 = bf16[4,128,128]{2,1,0:T(8,128)(2,1)S(1)} collective-permute-done((bf16[4,128,128]{2,1,0:T(8,128)(2,1)S(1)}, bf16[4,128,128]{2,1,0:T(8,128)(2,1)S(1)}, u32[]{:S(2)}, u32[]{:S(2)}) %collective-permute-start.6) | collective-permute-done | bytes 131104 | tf_op jit(solution)/shard_map/ppermute | solution.py:274
  29.3 0.0 collective-permute-done.7
  29.3 1.5 %collective-permute-done.9 = bf16[4,128,128]{2,1,0:T(8,128)(2,1)S(1)} collective-permute-done((bf16[4,128,128]{2,1,0:T(8,128)(2,1)S(1)}, bf16[4,128,128]{2,1,0:T(8,128)(2,1)S(1)}, u32[]{:S(2)}, u32[]{:S(2)}) %collective-permute-start.9) | collective-permute-done | bytes 131104 | tf_op jit(solution)/shard_map/ppermute | solution.py:274
  30.8 0.8 %add_bitcast_fusion = f32[1,1,4,128,128]{4,3,2,1,0:T(8,128)} fusion(bf16[4,128,128]{2,1,0:T(8,128)(2,1)S(1)} %collective-permute-done.9, bf16[4,128,128]{2,1,0:T(8,128)(2,1)S(1)} %collective-permute-done.7, f32[4,128,128]{2,1,0:T(8,128)S(1)} %shard_map.68, bf16[4,128,128]{2,1,0:T(8,128)(2,1)S(1)} %collective-permute-done.6), kind=kLoop, calls=%fused_computation | loop fusion | flops 393216 | bytes 917504 | tf_op jit(solution)/shard_map/broadcast_in_dim | solution.py:328
Async XLA Ops:
  0.0 13.8 %collective-permute-start.2 = (bf16[4,512,128]{2,1,0:T(8,128)(2,1)}, bf16[4,512,128]{2,1,0:T(8,128)(2,1)S(1)}, u32[]{:S(2)}, u32[]{:S(2)}) collective-permute-start(bf16[4,512,128]{2,1,0:T(8,128)(2,1)} %bitcast.9), channel_id=1, source_target_pairs={{1,0},{9,1},{3,2},{11,3},{5,4},{13,5},{7,6},{15,7},{0,8},{8,9},{2,... | collective-permute-start | bytes 1572872 | tf_op jit(solution)/shard_map/ppermute | solution.py:274
  0.5 19.3 %collective-permute-start.4 = (bf16[4,512,128]{2,1,0:T(8,128)(2,1)}, bf16[4,512,128]{2,1,0:T(8,128)(2,1)S(1)}, u32[]{:S(2)}, u32[]{:S(2)}) collective-permute-start(bf16[4,512,128]{2,1,0:T(8,128)(2,1)} %bitcast.10), channel_id=1, source_target_pairs={{2,0},{17,1},{4,2},{19,3},{6,4},{21,5},{0,6},{23,7},{24,8},{15,9},... | collective-permute-start | bytes 1572872 | tf_op jit(solution)/shard_map/ppermute | solution.py:274
  5.1 19.7 %collective-permute-start = (bf16[4,512,128]{2,1,0:T(8,128)(2,1)}, bf16[4,512,128]{2,1,0:T(8,128)(2,1)S(1)}, u32[]{:S(2)}, u32[]{:S(2)}) collective-permute-start(bf16[4,512,128]{2,1,0:T(8,128)(2,1)} %bitcast.11), channel_id=1, source_target_pairs={{16,0},{3,1},{18,2},{5,3},{20,4},{7,5},{22,6},{1,7},{14,8},{25,9},... | collective-permute-start | bytes 1572872 | tf_op jit(solution)/shard_map/ppermute | solution.py:274
  7.7 5.0 %collective-permute-start.3 = (bf16[528,128]{1,0:T(8,128)(2,1)S(1)}, bf16[528,128]{1,0:T(8,128)(2,1)S(1)}, u32[]{:S(2)}, u32[]{:S(2)}) collective-permute-start(bf16[528,128]{1,0:T(8,128)(2,1)S(1)} %get-tuple-element.15.own_sent), channel_id=1, source_target_pairs={{1,0},{9,1},{3,2},{11,3},{5,4},{13,5},{7,6},{15,7},{0,8},{8,9},{2,... | collective-permute-start | bytes 405512 | tf_op jit(solution)/shard_map/ppermute | solution.py:274
  7.8 12.1 %collective-permute-start.5 = (bf16[528,128]{1,0:T(8,128)(2,1)S(1)}, bf16[528,128]{1,0:T(8,128)(2,1)S(1)}, u32[]{:S(2)}, u32[]{:S(2)}) collective-permute-start(bf16[528,128]{1,0:T(8,128)(2,1)S(1)} %get-tuple-element.15.own_sent), channel_id=1, source_target_pairs={{2,0},{17,1},{4,2},{19,3},{6,4},{21,5},{0,6},{23,7},{24,8},{15,9},... | collective-permute-start | bytes 405512 | tf_op jit(solution)/shard_map/ppermute | solution.py:274
  8.5 1.0 %copy-start = (bf16[1,1,4,512,128]{4,3,2,1,0:T(8,128)(2,1)S(1)}, bf16[1,1,4,512,128]{4,3,2,1,0:T(8,128)(2,1)}, u32[]{:S(2)}) copy-start(bf16[1,1,4,512,128]{4,3,2,1,0:T(8,128)(2,1)} %param.6) | copy-start | bytes 1572868
  9.8 5.0 %copy-start.1 = (f32[1,1,4,128]{3,2,1,0:T(4,128)S(1)}, f32[1,1,4,128]{3,2,1,0:T(4,128)}, u32[]{:S(2)}) copy-start(f32[1,1,4,128]{3,2,1,0:T(4,128)} %param.8) | copy-start | bytes 6148
  12.8 13.1 %collective-permute-start.1 = (bf16[528,128]{1,0:T(8,128)(2,1)S(1)}, bf16[528,128]{1,0:T(8,128)(2,1)S(1)}, u32[]{:S(2)}, u32[]{:S(2)}) collective-permute-start(bf16[528,128]{1,0:T(8,128)(2,1)S(1)} %get-tuple-element.15.own_sent), channel_id=1, source_target_pairs={{16,0},{3,1},{18,2},{5,3},{20,4},{7,5},{22,6},{1,7},{14,8},{25,9},... | collective-permute-start | bytes 405512 | tf_op jit(solution)/shard_map/ppermute | solution.py:274
  13.8 11.7 %collective-permute-start.8 = (bf16[16,128]{1,0:T(8,128)(2,1)S(1)}, bf16[16,128]{1,0:T(8,128)(2,1)S(1)}, u32[]{:S(2)}, u32[]{:S(2)}) collective-permute-start(bf16[16,128]{1,0:T(8,128)(2,1)S(1)} %get-tuple-element.24.own_table), channel_id=1, source_target_pairs={{16,0},{3,1},{18,2},{5,3},{20,4},{7,5},{22,6},{1,7},{14,8},{25,9},... | collective-permute-start | bytes 12296 | tf_op jit(solution)/shard_map/ppermute | solution.py:274
  22.0 7.4 %collective-permute-start.6 = (bf16[4,128,128]{2,1,0:T(8,128)(2,1)S(1)}, bf16[4,128,128]{2,1,0:T(8,128)(2,1)S(1)}, u32[]{:S(2)}, u32[]{:S(2)}) collective-permute-start(bf16[4,128,128]{2,1,0:T(8,128)(2,1)S(1)} %get-tuple-element.21), channel_id=1, source_target_pairs={{0,2},{1,17},{2,4},{3,19},{4,6},{5,21},{6,0},{7,23},{8,24},{9,15},... | collective-permute-start | bytes 393224 | tf_op jit(solution)/shard_map/ppermute | solution.py:274
  22.0 7.3 %collective-permute-start.7 = (bf16[4,128,128]{2,1,0:T(8,128)(2,1)S(1)}, bf16[4,128,128]{2,1,0:T(8,128)(2,1)S(1)}, u32[]{:S(2)}, u32[]{:S(2)}) collective-permute-start(bf16[4,128,128]{2,1,0:T(8,128)(2,1)S(1)} %get-tuple-element.22), channel_id=1, source_target_pairs={{0,1},{1,9},{2,3},{3,11},{4,5},{5,13},{6,7},{7,15},{8,0},{9,8},{10... | collective-permute-start | bytes 393224 | tf_op jit(solution)/shard_map/ppermute | solution.py:274
  25.8 5.0 %collective-permute-start.9 = (bf16[4,128,128]{2,1,0:T(8,128)(2,1)S(1)}, bf16[4,128,128]{2,1,0:T(8,128)(2,1)S(1)}, u32[]{:S(2)}, u32[]{:S(2)}) collective-permute-start(bf16[4,128,128]{2,1,0:T(8,128)(2,1)S(1)} %shard_map.69), channel_id=1, source_target_pairs={{0,16},{1,3},{2,18},{3,5},{4,20},{5,7},{6,22},{7,1},{8,14},{9,25},... | collective-permute-start | bytes 393224 | tf_op jit(solution)/shard_map/ppermute | solution.py:274

commit v5 on v4

--- a/solution.py
+++ b/solution.py
@@ -204,35 +204,31 @@
         turned[pl.ds(p * width, width), :] = basis[p].T
 
 
-def near_kernel(own_turned, own_sent, p_basis, p_sent, energy, p_turned, total, p_sum):
+def near_kernel(own_turned, own_sent, p_basis, p_sent, near, p_turned, p_sum):
     pairs, _, width = p_basis.shape
-    bases, amps = bases_of(p_basis), amps_of(own_sent, width)
+    bases = bases_of(p_basis)
     for p in range(pairs):
         p_turned[pl.ds(p * width, width), :] = bases[p].T
     weight = weight_rows((table_of(own_sent, OWN), table_of(p_sent, PARTNER)), OP, pairs)
-    near = intersections(own_turned[...], bases)
-    x = row_terms(near, amps_of(p_sent, width), weight, width)
-    y = column_terms(near, amps, weight, width)
-    for p in range(pairs):
-        across = jnp.broadcast_to(energy[pl.ds(p, 1), :], (width, width))
-        total[p] = (across.T + across) * amps[p].astype(F32) + x[p]
-        p_sum[p] = y[p]
+    found = intersections(own_turned[...], bases)
+    near[...] = found
+    for p, y in enumerate(column_terms(found, amps_of(own_sent, width), weight, width)):
+        p_sum[p] = y
 
 
 def heavy_kernel(
-    own_turned, p_turned, own_sent, p_sent, h_basis, h_sent, total_in, p_sum,
-    total, p_back, h_back,
+    own_turned, p_turned, own_sent, p_sent, h_basis, h_sent, p_sum, near, p_back, h_back
 ):
     pairs, _, width = h_basis.shape
     tables = (table_of(own_sent, OWN), table_of(p_sent, PARTNER), table_of(h_sent, HEAVY))
     weight = weight_rows(tables, OH, pairs) + weight_rows(tables, PH, pairs)
     turned = jnp.concatenate([own_turned[...], p_turned[...]], 0)
-    near = intersections(turned, bases_of(h_basis))
-    y = column_terms(near, amps_of(own_sent, width) + amps_of(p_sent, width), weight, width)
-    x = row_terms(near, amps_of(h_sent, width), weight, width)
+    found = intersections(turned, bases_of(h_basis))
+    near[...] = found[: pairs * width]
+    y = column_terms(found, amps_of(own_sent, width) + amps_of(p_sent, width), weight, width)
+    x = row_terms(found[pairs * width :], amps_of(h_sent, width), weight[pairs:], width)
     for p in range(pairs):
-        total[p] = total_in[p] + x[p]
-        p_back[p] = (p_sum[p] + x[pairs + p]).astype(BF16)
+        p_back[p] = (p_sum[p] + x[p]).astype(BF16)
         h_back[p] = y[p].astype(BF16)
 
 
@@ -248,6 +244,17 @@
     weight = weight_rows((table_of(own_table, OWN), table_of(l_table, LIGHT)), OL, pairs)
     for p, y in enumerate(column_sums(near[...], right[...], weight, width)):
         l_back[p] = y.astype(BF16)
+
+
+def own_kernel(near_p, near_h, own_sent, p_sent, h_sent, energy, total):
+    pairs, width, _ = total.shape
+    tables = (table_of(own_sent, OWN), table_of(p_sent, PARTNER), table_of(h_sent, HEAVY))
+    weight = weight_rows(tables, OP, pairs), weight_rows(tables, OH, pairs)
+    x1 = row_terms(near_p[...], amps_of(p_sent, width), weight[0], width)
+    x2 = row_terms(near_h[...], amps_of(h_sent, width), weight[1], width)
+    for p, amps in enumerate(amps_of(own_sent, width)):
+        across = jnp.broadcast_to(energy[pl.ds(p, 1), :], (width, width))
+        total[p] = (across.T + across) * amps.astype(F32) + (x1[p] + x2[p])
 
 
 def rest_kernel(near, own_sent, l_sent, total_in, total):
@@ -311,15 +318,16 @@
         moved(what, to_l) for what in (rows, basis, sent)
     )
     (turned,) = kernel(turn_kernel, 0, (flat,), basis)
-    p_turned, total, p_sum = kernel(
-        near_kernel, 1, (flat, wide, wide), turned, sent, p_basis, p_sent, energy
-    )
-    total, p_back, h_back = kernel(
+    near_p, p_turned, p_sum = kernel(
+        near_kernel, 0.7, (table, flat, wide), turned, sent, p_basis, p_sent
+    )
+    near_h, p_back, h_back = kernel(
         heavy_kernel,
-        2,
-        (wide, narrow, narrow),
-        *(turned, p_turned, sent, p_sent, h_basis, h_sent, total, p_sum),
-    )
+        1.7,
+        (table, narrow, narrow),
+        *(turned, p_turned, sent, p_sent, h_basis, h_sent, p_sum),
+    )
+    (total,) = kernel(own_kernel, 0.6, (wide,), near_p, near_h, sent, p_sent, h_sent, energy)
     near, right = kernel(cross_kernel, 0.5, (table, table), turned, sent, l_basis)
     (l_back,) = kernel(light_kernel, 0.2, (narrow,), near, right, rows, l_rows)
     (total,) = kernel(rest_kernel, 0.3, (wide,), near, sent, l_sent, total)

time: 32 us -> 31.6 us (0.988)
  waiting for transfers between devices: 11.1 us -> 9.59 us
  local copies, waits for them, and re-layouts: 1.05 us -> 1.72 us
  Pallas kernels: 6.35 us -> 6.75 us
    ppermute x10, waiting for transfers between devices: 11.1 us -> 9.59 us  [moved(): return lax.ppermute(block, AXES, route)]
    unnamed x4, local copies, waits for them, and re-layouts: 1.05 us -> 1.72 us
    pallas_call x6 -> x7, Pallas kernels: 5.21 us -> 5.6 us  [kernel(): pl.pallas_call(body, out_shape=shapes, in_specs=[vmem] * len(operands), o...]
  transfers between devices with their start and end apart: 10 -> 10, of which waited for: 4 -> 4; matrix products, arithmetic and copies ran while one was open for 0% -> 0% of each run, Pallas kernels for 20% -> 22%
where the time goes in v5:
time: 31.6 us; the launch traced here: 31.2 us
  starting transfers between devices  12.3 us (39%)
  waiting for transfers between devices  9.59 us (30%)
  Pallas kernels  6.75 us (21%)
  local copies, waits for them, and re-layouts  1.72 us (5%)
  other arithmetic  0.77 us (2%)
    ppermute x10, starting transfers between devices, moved(): return lax.ppermute(block, AXES, route)  12.3 us
    ppermute x10, waiting for transfers between devices, moved(): return lax.ppermute(block, AXES, route)  9.59 us
    pallas_call x7, Pallas kernels, kernel(): pl.pallas_call(body, out_shape=shapes, in_specs=[vmem] * len(operands), o...  5.6 us
    unnamed x4, local copies, waits for them, and re-layouts  1.72 us
    pallas_call x1, Pallas kernels, on_device(): pl.pallas_call(functools.partial(prep_kernel, reach), out_shape=(jax.Shap...  1.15 us
    broadcast_in_dim x1, other arithmetic, on_device(): return total[None, None]  0.77 us
  transfers between devices with their start and end apart: 10, of which 4 were waited for; matrix products, arithmetic and copies ran while one was open for 0% of the time, Pallas kernels for 22%

profile of v5, /device:TPU:0, one launch (start us, length us, event | category | flops | bytes accessed | tf_op | source)
XLA Modules:
  0.0 31.2 jit_solution(18123617286727253672)
XLA Ops:
  0.0 0.5 %collective-permute-start.2 = (bf16[4,512,128]{2,1,0:T(8,128)(2,1)}, bf16[4,512,128]{2,1,0:T(8,128)(2,1)S(1)}, u32[]{:S(2)}, u32[]{:S(2)}) collective-permute-start(bf16[4,512,128]{2,1,0:T(8,128)(2,1)} %bitcast.9), channel_id=1, source_target_pairs={{1,0},{9,1},{3,2},{11,3},{5,4},{13,5},{7,6},{15,7},{0,8},{8,9},{2,... | collective-permute-start | bytes 1572872 | tf_op jit(solution)/shard_map/ppermute | solution.py:281
  0.5 4.6 %collective-permute-start.4 = (bf16[4,512,128]{2,1,0:T(8,128)(2,1)}, bf16[4,512,128]{2,1,0:T(8,128)(2,1)S(1)}, u32[]{:S(2)}, u32[]{:S(2)}) collective-permute-start(bf16[4,512,128]{2,1,0:T(8,128)(2,1)} %bitcast.10), channel_id=1, source_target_pairs={{2,0},{17,1},{4,2},{19,3},{6,4},{21,5},{0,6},{23,7},{24,8},{15,9},... | collective-permute-start | bytes 1572872 | tf_op jit(solution)/shard_map/ppermute | solution.py:281
  5.1 1.5 %collective-permute-start = (bf16[4,512,128]{2,1,0:T(8,128)(2,1)}, bf16[4,512,128]{2,1,0:T(8,128)(2,1)S(1)}, u32[]{:S(2)}, u32[]{:S(2)}) collective-permute-start(bf16[4,512,128]{2,1,0:T(8,128)(2,1)} %bitcast.11), channel_id=1, source_target_pairs={{16,0},{3,1},{18,2},{5,3},{20,4},{7,5},{22,6},{1,7},{14,8},{25,9},... | collective-permute-start | bytes 1572872 | tf_op jit(solution)/shard_map/ppermute | solution.py:281
  6.6 1.1 %prep.1 = (bf16[528,128]{1,0:T(8,128)(2,1)S(1)}, bf16[16,128]{1,0:T(8,128)(2,1)S(1)}) custom-call(s32[3,4,12]{2,1,0:T(4,128)} %bitcast.15, s32[4]{0:T(128)} %bitcast.16, f32[256]{0:T(256)} %fock_hbm.1, bf16[4,128,128]{2,1,0:T(8,128)(2,1)} %bitcast.14), custom_call_target="tpu_custom_call" | custom-call | tf_op jit(solution)/shard_map/prep/pallas_call | solution.py:299
  7.7 0.0 collective-permute-start.3
  7.8 0.8 %collective-permute-start.5 = (bf16[528,128]{1,0:T(8,128)(2,1)S(1)}, bf16[528,128]{1,0:T(8,128)(2,1)S(1)}, u32[]{:S(2)}, u32[]{:S(2)}) collective-permute-start(bf16[528,128]{1,0:T(8,128)(2,1)S(1)} %get-tuple-element.15.own_sent), channel_id=1, source_target_pairs={{2,0},{17,1},{4,2},{19,3},{6,4},{21,5},{0,6},{23,7},{24,8},{15,9},... | collective-permute-start | bytes 405512 | tf_op jit(solution)/shard_map/ppermute | solution.py:281
  8.5 0.0 copy-start
  8.5 1.0 %copy-done = bf16[1,1,4,512,128]{4,3,2,1,0:T(8,128)(2,1)S(1)} copy-done((bf16[1,1,4,512,128]{4,3,2,1,0:T(8,128)(2,1)S(1)}, bf16[1,1,4,512,128]{4,3,2,1,0:T(8,128)(2,1)}, u32[]{:S(2)}) %copy-start) | copy-done | bytes 524312
  9.6 0.2 shard_map.64.own_turned
  9.8 3.0 %collective-permute-done.3.p_sent = bf16[528,128]{1,0:T(8,128)(2,1)S(1)} collective-permute-done((bf16[528,128]{1,0:T(8,128)(2,1)S(1)}, bf16[528,128]{1,0:T(8,128)(2,1)S(1)}, u32[]{:S(2)}, u32[]{:S(2)}) %collective-permute-start.3) | collective-permute-done | bytes 135200 | tf_op jit(solution)/shard_map/ppermute | solution.py:281
  12.8 1.0 %collective-permute-start.1 = (bf16[528,128]{1,0:T(8,128)(2,1)S(1)}, bf16[528,128]{1,0:T(8,128)(2,1)S(1)}, u32[]{:S(2)}, u32[]{:S(2)}) collective-permute-start(bf16[528,128]{1,0:T(8,128)(2,1)S(1)} %get-tuple-element.15.own_sent), channel_id=1, source_target_pairs={{16,0},{3,1},{18,2},{5,3},{20,4},{7,5},{22,6},{1,7},{14,8},{25,9},... | collective-permute-start | bytes 405512 | tf_op jit(solution)/shard_map/ppermute | solution.py:281
  13.8 0.0 collective-permute-done.2.p_basis
  13.8 1.0 %collective-permute-start.8 = (bf16[16,128]{1,0:T(8,128)(2,1)S(1)}, bf16[16,128]{1,0:T(8,128)(2,1)S(1)}, u32[]{:S(2)}, u32[]{:S(2)}) collective-permute-start(bf16[16,128]{1,0:T(8,128)(2,1)S(1)} %get-tuple-element.24.own_table), channel_id=1, source_target_pairs={{16,0},{3,1},{18,2},{5,3},{20,4},{7,5},{22,6},{1,7},{14,8},{25,9},... | collective-permute-start | bytes 12296 | tf_op jit(solution)/shard_map/ppermute | solution.py:281
  14.8 0.9 %shard_map.66 = (bf16[512,512]{1,0:T(8,128)(2,1)S(1)}, bf16[512,512]{1,0:T(8,128)(2,1)S(1)}, f32[4,128,128]{2,1,0:T(8,128)S(1)}) custom-call(bf16[512,512]{1,0:T(8,128)(2,1)S(1)} %shard_map.64.own_turned, bf16[528,128]{1,0:T(8,128)(2,1)S(1)} %get-tuple-element.15.own_sent, bf16[4,512,128]{2,1,0:T(8,128)(2,1)S(1)} %collective-permute-done.2.p_basis, ...), custom_call_target="tpu_custom_call" | custom-call | flops 375809632 | bytes 524288 | tf_op jit(solution)/shard_map/pallas_call | solution.py:285
  15.7 4.2 %collective-permute-done.5.h_sent = bf16[528,128]{1,0:T(8,128)(2,1)S(1)} collective-permute-done((bf16[528,128]{1,0:T(8,128)(2,1)S(1)}, bf16[528,128]{1,0:T(8,128)(2,1)S(1)}, u32[]{:S(2)}, u32[]{:S(2)}) %collective-permute-start.5) | collective-permute-done | bytes 135200 | tf_op jit(solution)/shard_map/ppermute | solution.py:281
  19.8 0.0 collective-permute-done.4.h_basis
  19.8 1.7 %shard_map.67 = (bf16[512,512]{1,0:T(8,128)(2,1)S(1)}, bf16[4,128,128]{2,1,0:T(8,128)(2,1)S(1)}, bf16[4,128,128]{2,1,0:T(8,128)(2,1)S(1)}) custom-call(bf16[512,512]{1,0:T(8,128)(2,1)S(1)} %shard_map.64.own_turned, bf16[512,512]{1,0:T(8,128)(2,1)S(1)} %get-tuple-element.18.p_turned, bf16[528,128]{1,0:T(8,128)(2,1)S(1)} %get-tuple-element.15.own_sent, ...), custom_call_target="tpu_custom_call" | custom-call | flops 912680576 | bytes 524288 | tf_op jit(solution)/shard_map/pallas_call | solution.py:285
  21.5 0.1 collective-permute-start.6
  21.6 2.7 %collective-permute-start.7 = (bf16[4,128,128]{2,1,0:T(8,128)(2,1)S(1)}, bf16[4,128,128]{2,1,0:T(8,128)(2,1)S(1)}, u32[]{:S(2)}, u32[]{:S(2)}) collective-permute-start(bf16[4,128,128]{2,1,0:T(8,128)(2,1)S(1)} %get-tuple-element.22), channel_id=1, source_target_pairs={{0,1},{1,9},{2,3},{3,11},{4,5},{5,13},{6,7},{7,15},{8,0},{9,8},{10... | collective-permute-start | bytes 393224 | tf_op jit(solution)/shard_map/ppermute | solution.py:281
  24.3 0.0 collective-permute-done.l_basis
  24.3 0.8 %shard_map.65 = (bf16[512,512]{1,0:T(8,128)(2,1)S(1)}, bf16[512,512]{1,0:T(8,128)(2,1)S(1)}) custom-call(bf16[512,512]{1,0:T(8,128)(2,1)S(1)} %shard_map.64.own_turned, bf16[528,128]{1,0:T(8,128)(2,1)S(1)} %get-tuple-element.15.own_sent, bf16[4,512,128]{2,1,0:T(8,128)(2,1)S(1)} %collective-permute-done.l_basis), custom_call_target="tpu_custom_call" | custom-call | flops 268435456 | bytes 524288 | tf_op jit(solution)/shard_map/pallas_call | solution.py:285
  25.1 0.0 collective-permute-done.8.l_table
  25.1 0.3 shard_map.70
  25.4 0.1 collective-permute-start.9
  25.5 0.0 copy-start.1
  25.5 0.7 %copy-done.1 = f32[1,1,4,128]{3,2,1,0:T(4,128)S(1)} copy-done((f32[1,1,4,128]{3,2,1,0:T(4,128)S(1)}, f32[1,1,4,128]{3,2,1,0:T(4,128)}, u32[]{:S(2)}) %copy-start.1) | copy-done | bytes 2072
  26.2 1.2 %shard_map.68.total_in = f32[4,128,128]{2,1,0:T(8,128)S(1)} custom-call(bf16[512,512]{1,0:T(8,128)(2,1)S(1)} %get-tuple-element.17.near_p, bf16[512,512]{1,0:T(8,128)(2,1)S(1)} %get-tuple-element.20.near_h, bf16[528,128]{1,0:T(8,128)(2,1)S(1)} %get-tuple-element.15.own_sent, bf16[528,128]{1,0:T(8,128)(2,1)S(1)} %collective-permute-done.3.p_sent, ...), custom_call_target="tpu_custom_call" | custom-call | flops 322122560 | bytes 524288 | tf_op jit(solution)/shard_map/pallas_call | solution.py:285
  27.3 0.0 collective-permute-done.1.l_sent
  27.3 0.6 %shard_map.69 = f32[4,128,128]{2,1,0:T(8,128)S(1)} custom-call(bf16[512,512]{1,0:T(8,128)(2,1)S(1)} %get-tuple-element.16.near, bf16[528,128]{1,0:T(8,128)(2,1)S(1)} %get-tuple-element.15.own_sent, bf16[528,128]{1,0:T(8,128)(2,1)S(1)} %collective-permute-done.1.l_sent, f32[4,128,128]{2,1,0:T(8,128)S(1)} %shard_map.68.total_in), custom_call_target="tpu_custom_call" | custom-call | flops 161061280 | bytes 524288 | tf_op jit(solution)/shard_map/pallas_call | solution.py:285
  28.0 0.9 %collective-permute-done.6 = bf16[4,128,128]{2,1,0:T(8,128)(2,1)S(1)} collective-permute-done((bf16[4,128,128]{2,1,0:T(8,128)(2,1)S(1)}, bf16[4,128,128]{2,1,0:T(8,128)(2,1)S(1)}, u32[]{:S(2)}, u32[]{:S(2)}) %collective-permute-start.6) | collective-permute-done | bytes 131104 | tf_op jit(solution)/shard_map/ppermute | solution.py:281
  28.9 0.0 collective-permute-done.7
  28.9 1.5 %collective-permute-done.9 = bf16[4,128,128]{2,1,0:T(8,128)(2,1)S(1)} collective-permute-done((bf16[4,128,128]{2,1,0:T(8,128)(2,1)S(1)}, bf16[4,128,128]{2,1,0:T(8,128)(2,1)S(1)}, u32[]{:S(2)}, u32[]{:S(2)}) %collective-permute-start.9) | collective-permute-done | bytes 131104 | tf_op jit(solution)/shard_map/ppermute | solution.py:281
  30.4 0.8 %add_bitcast_fusion = f32[1,1,4,128,128]{4,3,2,1,0:T(8,128)} fusion(bf16[4,128,128]{2,1,0:T(8,128)(2,1)S(1)} %collective-permute-done.9, bf16[4,128,128]{2,1,0:T(8,128)(2,1)S(1)} %collective-permute-done.7, f32[4,128,128]{2,1,0:T(8,128)S(1)} %shard_map.69, bf16[4,128,128]{2,1,0:T(8,128)(2,1)S(1)} %collective-permute-done.6), kind=kLoop, calls=%fused_computation | loop fusion | flops 393216 | bytes 917504 | tf_op jit(solution)/shard_map/broadcast_in_dim | solution.py:336
Async XLA Ops:
  0.0 13.8 %collective-permute-start.2 = (bf16[4,512,128]{2,1,0:T(8,128)(2,1)}, bf16[4,512,128]{2,1,0:T(8,128)(2,1)S(1)}, u32[]{:S(2)}, u32[]{:S(2)}) collective-permute-start(bf16[4,512,128]{2,1,0:T(8,128)(2,1)} %bitcast.9), channel_id=1, source_target_pairs={{1,0},{9,1},{3,2},{11,3},{5,4},{13,5},{7,6},{15,7},{0,8},{8,9},{2,... | collective-permute-start | bytes 1572872 | tf_op jit(solution)/shard_map/ppermute | solution.py:281
  0.5 19.3 %collective-permute-start.4 = (bf16[4,512,128]{2,1,0:T(8,128)(2,1)}, bf16[4,512,128]{2,1,0:T(8,128)(2,1)S(1)}, u32[]{:S(2)}, u32[]{:S(2)}) collective-permute-start(bf16[4,512,128]{2,1,0:T(8,128)(2,1)} %bitcast.10), channel_id=1, source_target_pairs={{2,0},{17,1},{4,2},{19,3},{6,4},{21,5},{0,6},{23,7},{24,8},{15,9},... | collective-permute-start | bytes 1572872 | tf_op jit(solution)/shard_map/ppermute | solution.py:281
  5.1 19.2 %collective-permute-start = (bf16[4,512,128]{2,1,0:T(8,128)(2,1)}, bf16[4,512,128]{2,1,0:T(8,128)(2,1)S(1)}, u32[]{:S(2)}, u32[]{:S(2)}) collective-permute-start(bf16[4,512,128]{2,1,0:T(8,128)(2,1)} %bitcast.11), channel_id=1, source_target_pairs={{16,0},{3,1},{18,2},{5,3},{20,4},{7,5},{22,6},{1,7},{14,8},{25,9},... | collective-permute-start | bytes 1572872 | tf_op jit(solution)/shard_map/ppermute | solution.py:281
  7.7 5.0 %collective-permute-start.3 = (bf16[528,128]{1,0:T(8,128)(2,1)S(1)}, bf16[528,128]{1,0:T(8,128)(2,1)S(1)}, u32[]{:S(2)}, u32[]{:S(2)}) collective-permute-start(bf16[528,128]{1,0:T(8,128)(2,1)S(1)} %get-tuple-element.15.own_sent), channel_id=1, source_target_pairs={{1,0},{9,1},{3,2},{11,3},{5,4},{13,5},{7,6},{15,7},{0,8},{8,9},{2,... | collective-permute-start | bytes 405512 | tf_op jit(solution)/shard_map/ppermute | solution.py:281
  7.8 12.1 %collective-permute-start.5 = (bf16[528,128]{1,0:T(8,128)(2,1)S(1)}, bf16[528,128]{1,0:T(8,128)(2,1)S(1)}, u32[]{:S(2)}, u32[]{:S(2)}) collective-permute-start(bf16[528,128]{1,0:T(8,128)(2,1)S(1)} %get-tuple-element.15.own_sent), channel_id=1, source_target_pairs={{2,0},{17,1},{4,2},{19,3},{6,4},{21,5},{0,6},{23,7},{24,8},{15,9},... | collective-permute-start | bytes 405512 | tf_op jit(solution)/shard_map/ppermute | solution.py:281
  8.5 1.0 %copy-start = (bf16[1,1,4,512,128]{4,3,2,1,0:T(8,128)(2,1)S(1)}, bf16[1,1,4,512,128]{4,3,2,1,0:T(8,128)(2,1)}, u32[]{:S(2)}) copy-start(bf16[1,1,4,512,128]{4,3,2,1,0:T(8,128)(2,1)} %param.6) | copy-start | bytes 1572868
  12.8 14.6 %collective-permute-start.1 = (bf16[528,128]{1,0:T(8,128)(2,1)S(1)}, bf16[528,128]{1,0:T(8,128)(2,1)S(1)}, u32[]{:S(2)}, u32[]{:S(2)}) collective-permute-start(bf16[528,128]{1,0:T(8,128)(2,1)S(1)} %get-tuple-element.15.own_sent), channel_id=1, source_target_pairs={{16,0},{3,1},{18,2},{5,3},{20,4},{7,5},{22,6},{1,7},{14,8},{25,9},... | collective-permute-start | bytes 405512 | tf_op jit(solution)/shard_map/ppermute | solution.py:281
  13.8 11.3 %collective-permute-start.8 = (bf16[16,128]{1,0:T(8,128)(2,1)S(1)}, bf16[16,128]{1,0:T(8,128)(2,1)S(1)}, u32[]{:S(2)}, u32[]{:S(2)}) collective-permute-start(bf16[16,128]{1,0:T(8,128)(2,1)S(1)} %get-tuple-element.24.own_table), channel_id=1, source_target_pairs={{16,0},{3,1},{18,2},{5,3},{20,4},{7,5},{22,6},{1,7},{14,8},{25,9},... | collective-permute-start | bytes 12296 | tf_op jit(solution)/shard_map/ppermute | solution.py:281
  21.5 7.4 %collective-permute-start.6 = (bf16[4,128,128]{2,1,0:T(8,128)(2,1)S(1)}, bf16[4,128,128]{2,1,0:T(8,128)(2,1)S(1)}, u32[]{:S(2)}, u32[]{:S(2)}) collective-permute-start(bf16[4,128,128]{2,1,0:T(8,128)(2,1)S(1)} %get-tuple-element.21), channel_id=1, source_target_pairs={{0,2},{1,17},{2,4},{3,19},{4,6},{5,21},{6,0},{7,23},{8,24},{9,15},... | collective-permute-start | bytes 393224 | tf_op jit(solution)/shard_map/ppermute | solution.py:281
  21.6 7.3 %collective-permute-start.7 = (bf16[4,128,128]{2,1,0:T(8,128)(2,1)S(1)}, bf16[4,128,128]{2,1,0:T(8,128)(2,1)S(1)}, u32[]{:S(2)}, u32[]{:S(2)}) collective-permute-start(bf16[4,128,128]{2,1,0:T(8,128)(2,1)S(1)} %get-tuple-element.22), channel_id=1, source_target_pairs={{0,1},{1,9},{2,3},{3,11},{4,5},{5,13},{6,7},{7,15},{8,0},{9,8},{10... | collective-permute-start | bytes 393224 | tf_op jit(solution)/shard_map/ppermute | solution.py:281
  25.4 5.0 %collective-permute-start.9 = (bf16[4,128,128]{2,1,0:T(8,128)(2,1)S(1)}, bf16[4,128,128]{2,1,0:T(8,128)(2,1)S(1)}, u32[]{:S(2)}, u32[]{:S(2)}) collective-permute-start(bf16[4,128,128]{2,1,0:T(8,128)(2,1)S(1)} %shard_map.70), channel_id=1, source_target_pairs={{0,16},{1,3},{2,18},{3,5},{4,20},{5,7},{6,22},{7,1},{8,14},{9,25},... | collective-permute-start | bytes 393224 | tf_op jit(solution)/shard_map/ppermute | solution.py:281
  25.5 0.7 %copy-start.1 = (f32[1,1,4,128]{3,2,1,0:T(4,128)S(1)}, f32[1,1,4,128]{3,2,1,0:T(4,128)}, u32[]{:S(2)}) copy-start(f32[1,1,4,128]{3,2,1,0:T(4,128)} %param.8) | copy-start | bytes 6148

commit v6 on v5

--- a/solution.py
+++ b/solution.py
@@ -67,13 +67,14 @@
 
 
 def prep_kernel(
-    reach, plan_hbm, counts_hbm, fock_hbm, amps_hbm, sent, table_out, plan, counts, fock, sems
+    reach, plan_hbm, counts_hbm, fock_hbm, amps_hbm, energy_hbm, sent, table_out, energy,
+    plan, counts, fock, sems,
 ):
     pairs, width, _ = amps_hbm.shape
     copies = [
         pltpu.make_async_copy(src, dst, sems.at[k])
         for k, (src, dst) in enumerate(
-            [(plan_hbm, plan), (counts_hbm, counts), (fock_hbm, fock)]
+            [(plan_hbm, plan), (counts_hbm, counts), (fock_hbm, fock), (energy_hbm, energy)]
             + [(amps_hbm.at[p], sent.at[pl.ds(p * width, width)]) for p in range(pairs)]
         )
     ]
@@ -264,6 +265,17 @@
         total[p] = total_in[p] + x
 
 
+def last_kernel(total, h_in, p_in, l_in, out, held, sems):
+    copies = []
+    for p in range(total.shape[0]):
+        back_here = h_in[p].astype(F32) + p_in[p].astype(F32)
+        held[p] = (total[p] + back_here) + l_in[p].astype(F32)
+        copies.append(pltpu.make_async_copy(held.at[p], out.at[p], sems.at[p]))
+        copies[-1].start()
+    for copy in copies:
+        copy.wait()
+
+
 def on_device(all_routes, reach, pno_basis, amplitudes, pno_energy, fock_values, couplings, counts):
     to_p, to_h, to_l = all_routes
     basis, amps, energy = pno_basis[0, 0], amplitudes[0, 0], pno_energy[0, 0]
@@ -295,20 +307,21 @@
 
     h_basis = moved(basis, to_h)
     p_basis = moved(basis, to_p)
-    given = (plan, live, fock_values, amps)
-    sent, rows = pl.pallas_call(
+    given = (plan, live, fock_values, amps, energy)
+    sent, rows, energy = pl.pallas_call(
         functools.partial(prep_kernel, reach),
         out_shape=(
             jax.ShapeDtypeStruct((pairs * width + META, width), BF16),
             jax.ShapeDtypeStruct((META, LANES), BF16),
+            jax.ShapeDtypeStruct(energy.shape, F32),
         ),
         in_specs=[hbm] * len(given),
-        out_specs=(vmem, vmem),
+        out_specs=(vmem,) * 3,
         scratch_shapes=[
             pltpu.SMEM(plan.shape, I32),
             pltpu.SMEM(live.shape, I32),
             pltpu.SMEM(fock_values.shape, F32),
-            pltpu.SemaphoreType.DMA((3 + pairs,)),
+            pltpu.SemaphoreType.DMA((4 + pairs,)),
         ],
         compiler_params=params,
         name="prep",
@@ -331,8 +344,19 @@
     near, right = kernel(cross_kernel, 0.5, (table, table), turned, sent, l_basis)
     (l_back,) = kernel(light_kernel, 0.2, (narrow,), near, right, rows, l_rows)
     (total,) = kernel(rest_kernel, 0.3, (wide,), near, sent, l_sent, total)
-    for piece, route in ((h_back, to_h), (p_back, to_p), (l_back, to_l)):
-        total = total + moved(piece, back(route)).astype(F32)
+    returned = [
+        moved(piece, back(route))
+        for piece, route in ((h_back, to_h), (p_back, to_p), (l_back, to_l))
+    ]
+    total = pl.pallas_call(
+        last_kernel,
+        out_shape=wide,
+        in_specs=[vmem] * 4,
+        out_specs=hbm,
+        scratch_shapes=[pltpu.VMEM(square, F32), pltpu.SemaphoreType.DMA((pairs,))],
+        compiler_params=params,
+        name="last",
+    )(total, *returned)
     return total[None, None]
 
 

time: 31.6 us -> 31.6 us (level)
  other arithmetic: 0.77 us -> 0 us
  Pallas kernels: 6.75 us -> 7.5 us
  waiting for transfers between devices: 9.59 us -> 10.3 us
  local copies, waits for them, and re-layouts: 1.72 us -> 1.04 us
    broadcast_in_dim x1 -> x0, other arithmetic: 0.77 us -> none  [on_device(): return total[None, None]]
    pallas_call x0 -> x1, Pallas kernels: none -> 0.75 us  [on_device(): pl.pallas_call(last_kernel, out_shape=wide, in_specs=[vmem] * 4, out_spec...]
    unnamed x4 -> x2, local copies, waits for them, and re-layouts: 1.72 us -> 1.04 us
    ppermute x10, waiting for transfers between devices: 9.59 us -> 10.3 us  [moved(): return lax.ppermute(block, AXES, route)]
where the time goes in v6:
time: 31.6 us; the launch traced here: 31.2 us
  starting transfers between devices  12.3 us (39%)
  waiting for transfers between devices  10.3 us (33%)
  Pallas kernels  7.5 us (24%)
  local copies, waits for them, and re-layouts  1.04 us (3%)
    ppermute x10, starting transfers between devices, moved(): return lax.ppermute(block, AXES, route)  12.3 us
    ppermute x10, waiting for transfers between devices, moved(): return lax.ppermute(block, AXES, route)  10.3 us
    pallas_call x7, Pallas kernels, kernel(): pl.pallas_call(body, out_shape=shapes, in_specs=[vmem] * len(operands), o...  5.6 us
    pallas_call x1, Pallas kernels, on_device(): pl.pallas_call(functools.partial(prep_kernel, reach), out_shape=(jax.Shap...  1.16 us
    unnamed x2, local copies, waits for them, and re-layouts  1.04 us
    pallas_call x1, Pallas kernels, on_device(): pl.pallas_call(last_kernel, out_shape=wide, in_specs=[vmem] * 4, out_spec...  0.75 us
  transfers between devices with their start and end apart: 10, of which 4 were waited for; matrix products, arithmetic and copies ran while one was open for 0% of the time, Pallas kernels for 22%

profile of v6, /device:TPU:0, one launch (start us, length us, event | category | flops | bytes accessed | tf_op | source)
XLA Modules:
  0.0 31.2 jit_solution(8513916902492265651)
XLA Ops:
  0.0 0.5 %collective-permute-start.2 = (bf16[4,512,128]{2,1,0:T(8,128)(2,1)}, bf16[4,512,128]{2,1,0:T(8,128)(2,1)S(1)}, u32[]{:S(2)}, u32[]{:S(2)}) collective-permute-start(bf16[4,512,128]{2,1,0:T(8,128)(2,1)} %bitcast.8), channel_id=1, source_target_pairs={{1,0},{9,1},{3,2},{11,3},{5,4},{13,5},{7,6},{15,7},{0,8},{8,9},{2,... | collective-permute-start | bytes 1572872 | tf_op jit(solution)/shard_map/ppermute | solution.py:293
  0.5 4.6 %collective-permute-start.4 = (bf16[4,512,128]{2,1,0:T(8,128)(2,1)}, bf16[4,512,128]{2,1,0:T(8,128)(2,1)S(1)}, u32[]{:S(2)}, u32[]{:S(2)}) collective-permute-start(bf16[4,512,128]{2,1,0:T(8,128)(2,1)} %bitcast.9), channel_id=1, source_target_pairs={{2,0},{17,1},{4,2},{19,3},{6,4},{21,5},{0,6},{23,7},{24,8},{15,9},... | collective-permute-start | bytes 1572872 | tf_op jit(solution)/shard_map/ppermute | solution.py:293
  5.1 1.5 %collective-permute-start = (bf16[4,512,128]{2,1,0:T(8,128)(2,1)}, bf16[4,512,128]{2,1,0:T(8,128)(2,1)S(1)}, u32[]{:S(2)}, u32[]{:S(2)}) collective-permute-start(bf16[4,512,128]{2,1,0:T(8,128)(2,1)} %bitcast.10), channel_id=1, source_target_pairs={{16,0},{3,1},{18,2},{5,3},{20,4},{7,5},{22,6},{1,7},{14,8},{25,9},... | collective-permute-start | bytes 1572872 | tf_op jit(solution)/shard_map/ppermute | solution.py:293
  6.6 1.2 %prep.1 = (bf16[528,128]{1,0:T(8,128)(2,1)S(1)}, bf16[16,128]{1,0:T(8,128)(2,1)S(1)}, f32[4,128]{1,0:T(4,128)S(1)}) custom-call(s32[3,4,12]{2,1,0:T(4,128)} %bitcast.13, s32[4]{0:T(128)} %bitcast.15, f32[256]{0:T(256)} %fock_hbm.1, bf16[4,128,128]{2,1,0:T(8,128)(2,1)} %bitcast.12, f32[4,128]{1,0:T(4,128)} %bitcast.14), custom_call_target="tpu_custom_call" | custom-call | tf_op jit(solution)/shard_map/prep/pallas_call | solution.py:311
  7.7 0.0 collective-permute-start.3
  7.8 0.8 %collective-permute-start.5 = (bf16[528,128]{1,0:T(8,128)(2,1)S(1)}, bf16[528,128]{1,0:T(8,128)(2,1)S(1)}, u32[]{:S(2)}, u32[]{:S(2)}) collective-permute-start(bf16[528,128]{1,0:T(8,128)(2,1)S(1)} %get-tuple-element.16.own_sent), channel_id=1, source_target_pairs={{2,0},{17,1},{4,2},{19,3},{6,4},{21,5},{0,6},{23,7},{24,8},{15,9},... | collective-permute-start | bytes 405512 | tf_op jit(solution)/shard_map/ppermute | solution.py:293
  8.6 0.0 copy-start
  8.6 1.0 %copy-done = bf16[1,1,4,512,128]{4,3,2,1,0:T(8,128)(2,1)S(1)} copy-done((bf16[1,1,4,512,128]{4,3,2,1,0:T(8,128)(2,1)S(1)}, bf16[1,1,4,512,128]{4,3,2,1,0:T(8,128)(2,1)}, u32[]{:S(2)}) %copy-start) | copy-done | bytes 524312
  9.6 0.2 shard_map.64.own_turned
  9.8 3.0 %collective-permute-done.3.p_sent = bf16[528,128]{1,0:T(8,128)(2,1)S(1)} collective-permute-done((bf16[528,128]{1,0:T(8,128)(2,1)S(1)}, bf16[528,128]{1,0:T(8,128)(2,1)S(1)}, u32[]{:S(2)}, u32[]{:S(2)}) %collective-permute-start.3) | collective-permute-done | bytes 135200 | tf_op jit(solution)/shard_map/ppermute | solution.py:293
  12.8 1.0 %collective-permute-start.1 = (bf16[528,128]{1,0:T(8,128)(2,1)S(1)}, bf16[528,128]{1,0:T(8,128)(2,1)S(1)}, u32[]{:S(2)}, u32[]{:S(2)}) collective-permute-start(bf16[528,128]{1,0:T(8,128)(2,1)S(1)} %get-tuple-element.16.own_sent), channel_id=1, source_target_pairs={{16,0},{3,1},{18,2},{5,3},{20,4},{7,5},{22,6},{1,7},{14,8},{25,9},... | collective-permute-start | bytes 405512 | tf_op jit(solution)/shard_map/ppermute | solution.py:293
  13.8 0.0 collective-permute-done.2.p_basis
  13.8 1.0 %collective-permute-start.8 = (bf16[16,128]{1,0:T(8,128)(2,1)S(1)}, bf16[16,128]{1,0:T(8,128)(2,1)S(1)}, u32[]{:S(2)}, u32[]{:S(2)}) collective-permute-start(bf16[16,128]{1,0:T(8,128)(2,1)S(1)} %get-tuple-element.26.own_table), channel_id=1, source_target_pairs={{16,0},{3,1},{18,2},{5,3},{20,4},{7,5},{22,6},{1,7},{14,8},{25,9},... | collective-permute-start | bytes 12296 | tf_op jit(solution)/shard_map/ppermute | solution.py:293
  14.8 0.9 %shard_map.66 = (bf16[512,512]{1,0:T(8,128)(2,1)S(1)}, bf16[512,512]{1,0:T(8,128)(2,1)S(1)}, f32[4,128,128]{2,1,0:T(8,128)S(1)}) custom-call(bf16[512,512]{1,0:T(8,128)(2,1)S(1)} %shard_map.64.own_turned, bf16[528,128]{1,0:T(8,128)(2,1)S(1)} %get-tuple-element.16.own_sent, bf16[4,512,128]{2,1,0:T(8,128)(2,1)S(1)} %collective-permute-done.2.p_basis, ...), custom_call_target="tpu_custom_call" | custom-call | flops 375809632 | bytes 524288 | tf_op jit(solution)/shard_map/pallas_call | solution.py:297
  15.7 4.1 %collective-permute-done.5.h_sent = bf16[528,128]{1,0:T(8,128)(2,1)S(1)} collective-permute-done((bf16[528,128]{1,0:T(8,128)(2,1)S(1)}, bf16[528,128]{1,0:T(8,128)(2,1)S(1)}, u32[]{:S(2)}, u32[]{:S(2)}) %collective-permute-start.5) | collective-permute-done | bytes 135200 | tf_op jit(solution)/shard_map/ppermute | solution.py:293
  19.8 0.0 collective-permute-done.4.h_basis
  19.8 1.7 %shard_map.67 = (bf16[512,512]{1,0:T(8,128)(2,1)S(1)}, bf16[4,128,128]{2,1,0:T(8,128)(2,1)S(1)}, bf16[4,128,128]{2,1,0:T(8,128)(2,1)S(1)}) custom-call(bf16[512,512]{1,0:T(8,128)(2,1)S(1)} %shard_map.64.own_turned, bf16[512,512]{1,0:T(8,128)(2,1)S(1)} %get-tuple-element.19.p_turned, bf16[528,128]{1,0:T(8,128)(2,1)S(1)} %get-tuple-element.16.own_sent, ...), custom_call_target="tpu_custom_call" | custom-call | flops 912680576 | bytes 524288 | tf_op jit(solution)/shard_map/pallas_call | solution.py:297
  21.5 0.1 collective-permute-start.6
  21.6 2.7 %collective-permute-start.7 = (bf16[4,128,128]{2,1,0:T(8,128)(2,1)S(1)}, bf16[4,128,128]{2,1,0:T(8,128)(2,1)S(1)}, u32[]{:S(2)}, u32[]{:S(2)}) collective-permute-start(bf16[4,128,128]{2,1,0:T(8,128)(2,1)S(1)} %get-tuple-element.24), channel_id=1, source_target_pairs={{0,1},{1,9},{2,3},{3,11},{4,5},{5,13},{6,7},{7,15},{8,0},{9,8},{10... | collective-permute-start | bytes 393224 | tf_op jit(solution)/shard_map/ppermute | solution.py:293
  24.3 0.0 collective-permute-done.l_basis
  24.3 0.8 %shard_map.65 = (bf16[512,512]{1,0:T(8,128)(2,1)S(1)}, bf16[512,512]{1,0:T(8,128)(2,1)S(1)}) custom-call(bf16[512,512]{1,0:T(8,128)(2,1)S(1)} %shard_map.64.own_turned, bf16[528,128]{1,0:T(8,128)(2,1)S(1)} %get-tuple-element.16.own_sent, bf16[4,512,128]{2,1,0:T(8,128)(2,1)S(1)} %collective-permute-done.l_basis), custom_call_target="tpu_custom_call" | custom-call | flops 268435456 | bytes 524288 | tf_op jit(solution)/shard_map/pallas_call | solution.py:297
  25.1 0.0 collective-permute-done.8.l_table
  25.1 0.3 shard_map.70
  25.4 0.1 collective-permute-start.9
  25.5 1.2 %shard_map.68.total_in = f32[4,128,128]{2,1,0:T(8,128)S(1)} custom-call(bf16[512,512]{1,0:T(8,128)(2,1)S(1)} %get-tuple-element.18.near_p, bf16[512,512]{1,0:T(8,128)(2,1)S(1)} %get-tuple-element.21.near_h, bf16[528,128]{1,0:T(8,128)(2,1)S(1)} %get-tuple-element.16.own_sent, bf16[528,128]{1,0:T(8,128)(2,1)S(1)} %collective-permute-done.3.p_sent, ...), custom_call_target="tpu_custom_call" | custom-call | flops 322122560 | bytes 524288 | tf_op jit(solution)/shard_map/pallas_call | solution.py:297
  26.6 0.0 collective-permute-done.1.l_sent
  26.7 0.6 %shard_map.69.total = f32[4,128,128]{2,1,0:T(8,128)S(1)} custom-call(bf16[512,512]{1,0:T(8,128)(2,1)S(1)} %get-tuple-element.17.near, bf16[528,128]{1,0:T(8,128)(2,1)S(1)} %get-tuple-element.16.own_sent, bf16[528,128]{1,0:T(8,128)(2,1)S(1)} %collective-permute-done.1.l_sent, f32[4,128,128]{2,1,0:T(8,128)S(1)} %shard_map.68.total_in), custom_call_target="tpu_custom_call" | custom-call | flops 161061280 | bytes 524288 | tf_op jit(solution)/shard_map/pallas_call | solution.py:297
  27.3 1.6 %collective-permute-done.6.h_in = bf16[4,128,128]{2,1,0:T(8,128)(2,1)S(1)} collective-permute-done((bf16[4,128,128]{2,1,0:T(8,128)(2,1)S(1)}, bf16[4,128,128]{2,1,0:T(8,128)(2,1)S(1)}, u32[]{:S(2)}, u32[]{:S(2)}) %collective-permute-start.6) | collective-permute-done | bytes 131104 | tf_op jit(solution)/shard_map/ppermute | solution.py:293
  28.9 0.0 collective-permute-done.7.p_in
  28.9 1.5 %collective-permute-done.9.l_in = bf16[4,128,128]{2,1,0:T(8,128)(2,1)S(1)} collective-permute-done((bf16[4,128,128]{2,1,0:T(8,128)(2,1)S(1)}, bf16[4,128,128]{2,1,0:T(8,128)(2,1)S(1)}, u32[]{:S(2)}, u32[]{:S(2)}) %collective-permute-start.9) | collective-permute-done | bytes 131104 | tf_op jit(solution)/shard_map/ppermute | solution.py:293
  30.4 0.7 %last.1 = f32[4,128,128]{2,1,0:T(8,128)} custom-call(f32[4,128,128]{2,1,0:T(8,128)S(1)} %shard_map.69.total, bf16[4,128,128]{2,1,0:T(8,128)(2,1)S(1)} %collective-permute-done.6.h_in, bf16[4,128,128]{2,1,0:T(8,128)(2,1)S(1)} %collective-permute-done.7.p_in, bf16[4,128,128]{2,1,0:T(8,128)(2,1)S(1)} %collective-permute-done.9.l_in), custom_call_target="tpu_custom_call" | custom-call | tf_op jit(solution)/shard_map/last/pallas_call | solution.py:351
Async XLA Ops:
  0.0 13.8 %collective-permute-start.2 = (bf16[4,512,128]{2,1,0:T(8,128)(2,1)}, bf16[4,512,128]{2,1,0:T(8,128)(2,1)S(1)}, u32[]{:S(2)}, u32[]{:S(2)}) collective-permute-start(bf16[4,512,128]{2,1,0:T(8,128)(2,1)} %bitcast.8), channel_id=1, source_target_pairs={{1,0},{9,1},{3,2},{11,3},{5,4},{13,5},{7,6},{15,7},{0,8},{8,9},{2,... | collective-permute-start | bytes 1572872 | tf_op jit(solution)/shard_map/ppermute | solution.py:293
  0.5 19.3 %collective-permute-start.4 = (bf16[4,512,128]{2,1,0:T(8,128)(2,1)}, bf16[4,512,128]{2,1,0:T(8,128)(2,1)S(1)}, u32[]{:S(2)}, u32[]{:S(2)}) collective-permute-start(bf16[4,512,128]{2,1,0:T(8,128)(2,1)} %bitcast.9), channel_id=1, source_target_pairs={{2,0},{17,1},{4,2},{19,3},{6,4},{21,5},{0,6},{23,7},{24,8},{15,9},... | collective-permute-start | bytes 1572872 | tf_op jit(solution)/shard_map/ppermute | solution.py:293
  5.1 19.2 %collective-permute-start = (bf16[4,512,128]{2,1,0:T(8,128)(2,1)}, bf16[4,512,128]{2,1,0:T(8,128)(2,1)S(1)}, u32[]{:S(2)}, u32[]{:S(2)}) collective-permute-start(bf16[4,512,128]{2,1,0:T(8,128)(2,1)} %bitcast.10), channel_id=1, source_target_pairs={{16,0},{3,1},{18,2},{5,3},{20,4},{7,5},{22,6},{1,7},{14,8},{25,9},... | collective-permute-start | bytes 1572872 | tf_op jit(solution)/shard_map/ppermute | solution.py:293
  7.7 5.0 %collective-permute-start.3 = (bf16[528,128]{1,0:T(8,128)(2,1)S(1)}, bf16[528,128]{1,0:T(8,128)(2,1)S(1)}, u32[]{:S(2)}, u32[]{:S(2)}) collective-permute-start(bf16[528,128]{1,0:T(8,128)(2,1)S(1)} %get-tuple-element.16.own_sent), channel_id=1, source_target_pairs={{1,0},{9,1},{3,2},{11,3},{5,4},{13,5},{7,6},{15,7},{0,8},{8,9},{2,... | collective-permute-start | bytes 405512 | tf_op jit(solution)/shard_map/ppermute | solution.py:293
  7.8 12.1 %collective-permute-start.5 = (bf16[528,128]{1,0:T(8,128)(2,1)S(1)}, bf16[528,128]{1,0:T(8,128)(2,1)S(1)}, u32[]{:S(2)}, u32[]{:S(2)}) collective-permute-start(bf16[528,128]{1,0:T(8,128)(2,1)S(1)} %get-tuple-element.16.own_sent), channel_id=1, source_target_pairs={{2,0},{17,1},{4,2},{19,3},{6,4},{21,5},{0,6},{23,7},{24,8},{15,9},... | collective-permute-start | bytes 405512 | tf_op jit(solution)/shard_map/ppermute | solution.py:293
  8.6 1.0 %copy-start = (bf16[1,1,4,512,128]{4,3,2,1,0:T(8,128)(2,1)S(1)}, bf16[1,1,4,512,128]{4,3,2,1,0:T(8,128)(2,1)}, u32[]{:S(2)}) copy-start(bf16[1,1,4,512,128]{4,3,2,1,0:T(8,128)(2,1)} %param.6) | copy-start | bytes 1572868
  12.8 13.9 %collective-permute-start.1 = (bf16[528,128]{1,0:T(8,128)(2,1)S(1)}, bf16[528,128]{1,0:T(8,128)(2,1)S(1)}, u32[]{:S(2)}, u32[]{:S(2)}) collective-permute-start(bf16[528,128]{1,0:T(8,128)(2,1)S(1)} %get-tuple-element.16.own_sent), channel_id=1, source_target_pairs={{16,0},{3,1},{18,2},{5,3},{20,4},{7,5},{22,6},{1,7},{14,8},{25,9},... | collective-permute-start | bytes 405512 | tf_op jit(solution)/shard_map/ppermute | solution.py:293
  13.8 11.3 %collective-permute-start.8 = (bf16[16,128]{1,0:T(8,128)(2,1)S(1)}, bf16[16,128]{1,0:T(8,128)(2,1)S(1)}, u32[]{:S(2)}, u32[]{:S(2)}) collective-permute-start(bf16[16,128]{1,0:T(8,128)(2,1)S(1)} %get-tuple-element.26.own_table), channel_id=1, source_target_pairs={{16,0},{3,1},{18,2},{5,3},{20,4},{7,5},{22,6},{1,7},{14,8},{25,9},... | collective-permute-start | bytes 12296 | tf_op jit(solution)/shard_map/ppermute | solution.py:293
  21.5 7.4 %collective-permute-start.6 = (bf16[4,128,128]{2,1,0:T(8,128)(2,1)S(1)}, bf16[4,128,128]{2,1,0:T(8,128)(2,1)S(1)}, u32[]{:S(2)}, u32[]{:S(2)}) collective-permute-start(bf16[4,128,128]{2,1,0:T(8,128)(2,1)S(1)} %get-tuple-element.23), channel_id=1, source_target_pairs={{0,2},{1,17},{2,4},{3,19},{4,6},{5,21},{6,0},{7,23},{8,24},{9,15},... | collective-permute-start | bytes 393224 | tf_op jit(solution)/shard_map/ppermute | solution.py:293
  21.6 7.3 %collective-permute-start.7 = (bf16[4,128,128]{2,1,0:T(8,128)(2,1)S(1)}, bf16[4,128,128]{2,1,0:T(8,128)(2,1)S(1)}, u32[]{:S(2)}, u32[]{:S(2)}) collective-permute-start(bf16[4,128,128]{2,1,0:T(8,128)(2,1)S(1)} %get-tuple-element.24), channel_id=1, source_target_pairs={{0,1},{1,9},{2,3},{3,11},{4,5},{5,13},{6,7},{7,15},{8,0},{9,8},{10... | collective-permute-start | bytes 393224 | tf_op jit(solution)/shard_map/ppermute | solution.py:293
  25.4 5.0 %collective-permute-start.9 = (bf16[4,128,128]{2,1,0:T(8,128)(2,1)S(1)}, bf16[4,128,128]{2,1,0:T(8,128)(2,1)S(1)}, u32[]{:S(2)}, u32[]{:S(2)}) collective-permute-start(bf16[4,128,128]{2,1,0:T(8,128)(2,1)S(1)} %shard_map.70), channel_id=1, source_target_pairs={{0,16},{1,3},{2,18},{3,5},{4,20},{5,7},{6,22},{7,1},{8,14},{9,25},... | collective-permute-start | bytes 393224 | tf_op jit(solution)/shard_map/ppermute | solution.py:293
